TPU v7x, 32 devices: a whole 2x2x4 slice. The times are simulated.
32 devices in a mesh: grp: 2 (over y), ctx: 4 (over z), sec: 2 (over core), tp: 2 (over x).
Axes of the slice: x: 2, y: 2, z: 4, core: 2. Of those that a mesh axis runs over, the one named last changes fastest.
Arguments:
- hidden: bfloat16 [1024, 8192], P(('grp', 'ctx', 'sec')), parts along dimension 0, may hold values from -6 to 6
- w_query: bfloat16 [2, 8192, 4096], P('sec', 'ctx', 'tp'), may hold values from -0.0625 to 0.0625
- key_projection: bfloat16 [2, 8192, 1024], P('sec', 'ctx', 'tp'), may hold values from -0.0625 to 0.0625
- value_projection: bfloat16 [2, 8192, 1024], P('sec', 'ctx', 'tp'), may hold values from -0.0625 to 0.0625
- score_head: bfloat16 [2, 4096], P('sec', 'tp'), may hold values from -0.09375 to 0.09375
- lengths: int32 [8], P('grp'), parts along dimension 0, may hold values from 1 to 320, 512 in all
- prompt_len: int32 [8], P('grp'), parts along dimension 0, may hold values from 1 to 159
- reward: float32 [8], P('grp'), parts along dimension 0, may hold values from -4 to 4
Outputs:
- kl_term: float32 [1024], P(('grp', 'ctx', 'sec')), parts along dimension 0
- objective: float32 [1024], P(('grp', 'ctx', 'sec')), parts along dimension 0
There are 2 independent parts, one for each index of `grp`. A program takes and returns all parts, laid end to end along the dimension named above; an argument that names none is the same for every part. Nothing has to cross between parts.
Inputs may be any that keep to these rules, and one draw needn't show every extreme that they name: `lengths`: rollouts are packed in order and fill all 512 positions; the longest has exactly 320 tokens. `prompt_len`: A prompt may cover its whole rollout, leaving no response tokens.
All inputs are finite; a program needn't handle non-finite values.
Results may differ from a plain program's by a relative error of at most 0.012.
Values may be sent and summed in bfloat16 or wider, within the bound.
No kernel may reach another device: no remote copies, remote signals or barrier semaphores. Data moves between devices by JAX's collectives and lax.ppermute only.
A program may use at most 128 MiB of HBM per device.

v0:
```python
import jax
import jax.numpy as jnp
from jax import lax
from jax.sharding import PartitionSpec as P

QUERY_HEAD_COUNT = 32
KEY_VALUE_HEADS = 8
HEAD_SIZE = 128


BETA = 0.1
NEGATIVE = -1e30


def swapped(array, axis, distance):
    return lax.ppermute(array, axis, [(i, i ^ 1 << distance) for i in range(lax.axis_size(axis))])


def rollout_tables(lengths, prompt_len, reward, position):
    starts = jnp.cumsum(lengths) - lengths
    inside = starts[None, :] <= position[:, None]
    begin = jnp.max(jnp.where(inside, starts[None, :], 0), axis=1)
    latest = jnp.sum(inside.astype(jnp.int32), axis=1) - 1
    chosen = jnp.arange(lengths.shape[0], dtype=jnp.int32)[None, :] == latest[:, None]
    prompt = jnp.sum(jnp.where(chosen, prompt_len[None, :], 0), axis=1)
    centred = reward - jnp.mean(reward)
    advantage = jnp.sum(
        jnp.where(chosen, centred[None, :], jnp.zeros_like(centred)[None, :]), axis=1
    )
    answer = (position - begin >= prompt).astype(reward.dtype)
    return (begin, answer, advantage)


def shards(
    hidden, w_query, key_projection, value_projection, score_head, lengths, prompt_len, reward
):
    row_block = lax.all_gather(hidden, "sec", axis=0, tiled=True)
    token_rows = row_block.shape[0]
    query_w = w_query[0]
    key_w = key_projection[0]
    value_w = value_projection[0]
    head_w = score_head[0]
    query_cols = query_w.shape[1]
    pair_cols = key_w.shape[1]

    def add_rows(piece):
        return jnp.dot(row_block, piece, preferred_element_type=jnp.float32)

    query_rows = add_rows(lax.all_gather(query_w, "ctx", axis=0, tiled=True))
    key_rows = add_rows(lax.all_gather(key_w, "ctx", axis=0, tiled=True))
    value_rows = add_rows(lax.all_gather(value_w, "ctx", axis=0, tiled=True))
    query_rows = query_rows.astype(jnp.bfloat16)
    key_rows = key_rows.astype(jnp.bfloat16)
    value_rows = value_rows.astype(jnp.bfloat16)
    heads_here = pair_cols // HEAD_SIZE
    query_group = QUERY_HEAD_COUNT // KEY_VALUE_HEADS
    score_scale = HEAD_SIZE ** (-0.5)
    row_pos = lax.axis_index("ctx") * token_rows + jnp.arange(token_rows, dtype=jnp.int32)
    begin, answer, advantage = rollout_tables(lengths, prompt_len, reward, row_pos)
    first_begin = jnp.min(begin)
    last_row = row_pos[token_rows - 1]
    query_heads = query_rows.reshape(token_rows, heads_here, query_group, HEAD_SIZE)
    start_state = (
        jnp.full((heads_here, query_group, token_rows), NEGATIVE, jnp.float32),
        jnp.zeros((heads_here, query_group, token_rows), jnp.float32),
        jnp.zeros((heads_here, query_group, token_rows, HEAD_SIZE), jnp.float32),
    )
    key_piece = lax.all_gather(key_rows, "ctx", axis=0, tiled=True)
    value_piece = lax.all_gather(value_rows, "ctx", axis=0, tiled=True)
    count = key_piece.shape[0] // token_rows

    def tile_step(index, carried):
        offset = index * token_rows
        key_tile = lax.dynamic_slice_in_dim(key_piece, offset, token_rows, 0).reshape(
            token_rows, heads_here, HEAD_SIZE
        )
        value_tile = lax.dynamic_slice_in_dim(value_piece, offset, token_rows, 0).reshape(
            token_rows, heads_here, HEAD_SIZE
        )
        key_pos = offset + jnp.arange(token_rows, dtype=jnp.int32)

        def update(current):
            peak, weight_sum, mixed_values = current
            score_logits = (
                jnp.einsum(
                    "rkgd,pkd->kgrp", query_heads, key_tile, preferred_element_type=jnp.float32
                )
                * score_scale
            )
            valid = (key_pos[None, :] <= row_pos[:, None]) & (key_pos[None, :] >= begin[:, None])
            masked = jnp.where(valid[None, None], score_logits, NEGATIVE)
            new_peak = jnp.maximum(peak, jnp.max(masked, axis=3))
            weights = jnp.where(
                valid[None, None],
                jnp.exp(score_logits - new_peak[..., None]),
                jnp.zeros_like(score_logits),
            )
            factor = jnp.exp(peak - new_peak)
            new_sum = weight_sum * factor + jnp.sum(weights, axis=3)
            product = jnp.einsum(
                "kgrp,pkd->kgrd",
                weights.astype(jnp.bfloat16),
                value_tile,
                preferred_element_type=jnp.float32,
            )
            return (new_peak, new_sum, mixed_values * factor[..., None] + product)

        live = (offset <= last_row) & (offset + token_rows - 1 >= first_begin)
        return lax.cond(live, update, lambda kept: kept, carried)

    peak, weight_sum, mixed_values = lax.fori_loop(0, count, tile_step, start_state)
    attended = (
        (mixed_values / weight_sum[..., None]).transpose(2, 0, 1, 3).reshape(token_rows, query_cols)
    )
    numerator = jnp.dot(attended, head_w.astype(jnp.float32), precision=lax.Precision.HIGHEST)
    squares = jnp.sum(attended * attended, axis=1)
    section = lax.axis_index("sec")
    total_num, total_sq = lax.psum((numerator, squares), "tp")
    score = total_num / jnp.sqrt(total_sq / (QUERY_HEAD_COUNT * HEAD_SIZE) + 1e-05)
    other = swapped(score, "sec", 0)
    policy = jnp.where(section == 0, score, other)
    frozen = jnp.where(section == 0, other, score)
    gap = frozen - policy
    kl_full = answer * (jnp.exp(gap) - gap - 1.0)
    objective_full = answer * advantage - BETA * kl_full
    half = token_rows // 2
    kl_term = lax.dynamic_slice_in_dim(kl_full, section * half, half, 0)
    objective = lax.dynamic_slice_in_dim(objective_full, section * half, half, 0)
    return (kl_term, objective)


def solution(mesh):
    placed = (
        P(("grp", "ctx", "sec"), None),
        P("sec", "ctx", "tp"),
        P("sec", "ctx", "tp"),
        P("sec", "ctx", "tp"),
        P("sec", "tp"),
        P("grp"),
        P("grp"),
        P("grp"),
    )
    return jax.shard_map(
        shards,
        mesh=mesh,
        in_specs=placed,
        out_specs=(P(("grp", "ctx", "sec")), P(("grp", "ctx", "sec"))),
        check_vma=False,
    )
```

profile of v0, /device:TPU:0, one launch (start us, length us, event | category | flops | bytes accessed | tf_op | source)
XLA Modules:
  0.0 928.4 jit_solution(15389997855569136279)
XLA Ops:
  7.2 0.0 copy-start
  7.2 0.0 copy-start.2
  7.2 0.0 copy-start.3
  7.2 0.0 copy-start.4
  7.2 0.0 all-gather.8.cloned.1.call-start
  7.3 0.7 all-gather.8.cloned.1.call-update
  7.9 0.0 all-gather.14.cloned.1.call-start
  8.0 0.7 all-gather.14.cloned.1.call-update
  8.7 0.0 all-gather.10.cloned.1.call-start
  8.7 0.7 all-gather.10.cloned.1.call-update
  9.4 0.0 all-gather.12.cloned.1.call-start
  9.5 0.5 all-gather.12.cloned.1.call-update
  10.0 0.7 slice.3
  10.7 0.0 copy-done.2
  10.7 0.2 reduce-window.9
  10.9 0.6 reduce_sum.60
  12.1 0.1 fusion.28
  12.2 0.6 reduce_min.9
  12.9 0.1 select_reduce_fusion.1
  12.9 0.1 select_reduce_fusion.2
  13.0 9.9 %all-gather.8.cloned.1.call-done = bf16[128,8192]{1,0:T(8,128)(2,1)} async-done(((bf16[64,8192]{1,0:T(8,128)(2,1)}), bf16[128,8192]{1,0:T(8,128)(2,1)}) %all-gather.8.cloned.1.call-update) | async-done | bytes 2097168 | tf_op jit(solution)/shard_map/all_gather | solution.py:37
  22.9 152.4 %all-gather.14.cloned.1.call-done = bf16[1,8192,512]{2,1,0:T(8,128)(2,1)} async-done(((bf16[1,2048,512]{2,1,0:T(8,128)(2,1)}), bf16[1,8192,512]{2,1,0:T(8,128)(2,1)}) %all-gather.14.cloned.1.call-update) | async-done | bytes 8388624 | tf_op jit(solution)/shard_map/all_gather | solution.py:51
  175.3 5.3 fusion.22
  180.6 25.3 %all_gather.23 = bf16[512,512]{1,0:T(8,128)(2,1)S(1)} all-gather(bf16[128,512]{1,0:T(8,128)(2,1)S(1)} %fusion.22), channel_id=1, replica_groups=mesh['grp'=2,'ctx'=4,'sec'=2,'tp'=2] {'ctx'}, dimensions={0}, use_global_device_ids=true | all-gather | bytes 655360 | tf_op jit(solution)/shard_map/all_gather | solution.py:69
  205.9 0.2 copy.24
  206.1 123.3 %all-gather.10.cloned.1.call-done = bf16[1,8192,512]{2,1,0:T(8,128)(2,1)} async-done(((bf16[1,2048,512]{2,1,0:T(8,128)(2,1)}), bf16[1,8192,512]{2,1,0:T(8,128)(2,1)}) %all-gather.10.cloned.1.call-update) | async-done | bytes 8388624 | tf_op jit(solution)/shard_map/all_gather | solution.py:50
  329.4 4.6 fusion.19
  334.1 16.9 %all_gather.20 = bf16[512,512]{1,0:T(8,128)(2,1)} all-gather(bf16[128,512]{1,0:T(8,128)(2,1)S(1)} %fusion.19), channel_id=1, replica_groups=mesh['grp'=2,'ctx'=4,'sec'=2,'tp'=2] {'ctx'}, dimensions={0}, use_global_device_ids=true | all-gather | bytes 655360 | tf_op jit(solution)/shard_map/all_gather | solution.py:68
  351.0 1.3 copy.22
  352.3 538.8 %all-gather.12.cloned.1.call-done = bf16[1,8192,2048]{2,1,0:T(8,128)(2,1)} async-done(((bf16[1,2048,2048]{2,1,0:T(8,128)(2,1)}), bf16[1,8192,2048]{2,1,0:T(8,128)(2,1)}) %all-gather.12.cloned.1.call-update) | async-done | bytes 33554448 | tf_op jit(solution)/shard_map/all_gather | solution.py:49
  891.0 13.8 %fusion.16 = bf16[128,2048]{1,0:T(8,128)(2,1)} fusion(bf16[128,8192]{1,0:T(8,128)(2,1)S(1)} %copy-done.1, bf16[1,8192,2048]{2,1,0:T(8,128)(2,1)} %all-gather.12.cloned.1.call-done), kind=kOutput, calls=%fused_computation.25 | convolution fusion | flops 4295229440 | bytes 36175872 | tf_op jit(solution)/shard_map/dot_general | solution.py:47
  904.8 1.4 reshape.128
  906.2 0.1 copy.23
  906.4 0.1 broadcast.95
  906.5 7.0 while.22
  907.9 1.5 conditional.3
  907.9 0.1 compare_and_fusion
  908.0 0.4 select_reduce_fusion
  908.4 0.2 fusion.4
  908.7 0.7 convolution_add_fusion
  913.5 0.3 copy.25
  913.9 0.3 fusion.25
  914.2 0.5 convolution_bitcast_fusion
  914.6 4.9 all-reduce
  919.6 0.0 collective-permute-start
  919.6 1.1 collective-permute-done
  920.7 0.6 dynamic_slice.35
  921.3 0.6 dynamic_slice.34
  (25 shorter events, 0.2 us)
Async XLA Ops:
  7.2 907.0 %copy-start = (bf16[1,2048]{1,0:T(2,128)(2,1)S(1)}, bf16[1,2048]{1,0:T(2,128)(2,1)}, u32[]{:S(2)}) copy-start(bf16[1,2048]{1,0:T(2,128)(2,1)} %param.16) | copy-start | bytes 12292
  7.2 3.5 copy-start.2
  7.2 3.7 copy-start.3
  7.2 5.7 copy-start.4
  7.2 15.7 %all-gather.8.cloned.1.call-start = ((), (), s32[]{:S(2)}) async-start(), calls=%async_computation | async-start | bytes 3145728 | tf_op jit(solution)/shard_map/all_gather | solution.py:37
  7.9 167.4 %all-gather.14.cloned.1.call-start = ((), (), s32[]{:S(2)}) async-start(), calls=%async_computation.3 | async-start | bytes 10485760 | tf_op jit(solution)/shard_map/all_gather | solution.py:51
  8.7 320.7 %all-gather.10.cloned.1.call-start = ((), (), s32[]{:S(2)}) async-start(), calls=%async_computation.1 | async-start | bytes 10485760 | tf_op jit(solution)/shard_map/all_gather | solution.py:50
  9.4 881.6 %all-gather.12.cloned.1.call-start = ((), (), s32[]{:S(2)}) async-start(), calls=%async_computation.2 | async-start | bytes 41943040 | tf_op jit(solution)/shard_map/all_gather | solution.py:49
  22.9 306.5 %copy-start.1 = (bf16[128,8192]{1,0:T(8,128)(2,1)S(1)}, bf16[128,8192]{1,0:T(8,128)(2,1)}, u32[]{:S(2)}) copy-start(bf16[128,8192]{1,0:T(8,128)(2,1)} %all-gather.8.cloned.1.call-done) | copy-start | bytes 6291460
  919.6 1.1 collective-permute-start
Sparse Core Ops, SparseCore 0:
  9.6 13.2 all-gather.7
  24.5 150.7 all-gather.13
  176.9 152.4 all-gather.9
  330.8 560.1 all-gather.11
where the time goes:
time: 929 us; the launch traced here: 928 us
  waiting for transfers between devices  828 us (89%)
  blocking collectives  47.2 us (5%)
  matrix products  25.2 us (3%)
  between operations  14.6 us (2%)
    all_gather x1, waiting for transfers between devices, shards(): query_rows = add_rows(lax.all_gather(query_w, 'ctx', axis=0, tiled=True))  539 us
    all_gather x1, waiting for transfers between devices, shards(): value_rows = add_rows(lax.all_gather(value_w, 'ctx', axis=0, tiled=True))  152 us
    all_gather x1, waiting for transfers between devices, shards(): key_rows = add_rows(lax.all_gather(key_w, 'ctx', axis=0, tiled=True))  123 us
    all_gather x1, blocking collectives, shards(): value_piece = lax.all_gather(value_rows, 'ctx', axis=0, tiled=True)  25.3 us
    dot_general x3, matrix products, add_rows(): return jnp.dot(row_block, piece, preferred_element_type=jnp.float32)  23.7 us
  transfers between devices with their start and end apart: 5, of which 5 were waited for; matrix products, arithmetic and copies ran while one was open for 1% of the time, Pallas kernels for 0%

commit v1 on v0

--- a/solution.py
+++ b/solution.py
@@ -1,6 +1,8 @@
 import jax
 import jax.numpy as jnp
 from jax import lax
+from jax.experimental import pallas as pl
+from jax.experimental.pallas import tpu as pltpu
 from jax.sharding import PartitionSpec as P
 
 QUERY_HEAD_COUNT = 32
@@ -10,6 +12,8 @@
 
 BETA = 0.1
 NEGATIVE = -1e30
+LINK_SCALE = 16.0
+GROUP = QUERY_HEAD_COUNT // KEY_VALUE_HEADS
 
 
 def swapped(array, axis, distance):
@@ -31,7 +35,7 @@
     return (begin, answer, advantage)
 
 
-def shards(
+def gathered_shards(
     hidden, w_query, key_projection, value_projection, score_head, lengths, prompt_len, reward
 ):
     row_block = lax.all_gather(hidden, "sec", axis=0, tiled=True)
@@ -53,17 +57,16 @@
     key_rows = key_rows.astype(jnp.bfloat16)
     value_rows = value_rows.astype(jnp.bfloat16)
     heads_here = pair_cols // HEAD_SIZE
-    query_group = QUERY_HEAD_COUNT // KEY_VALUE_HEADS
     score_scale = HEAD_SIZE ** (-0.5)
     row_pos = lax.axis_index("ctx") * token_rows + jnp.arange(token_rows, dtype=jnp.int32)
     begin, answer, advantage = rollout_tables(lengths, prompt_len, reward, row_pos)
     first_begin = jnp.min(begin)
     last_row = row_pos[token_rows - 1]
-    query_heads = query_rows.reshape(token_rows, heads_here, query_group, HEAD_SIZE)
+    query_heads = query_rows.reshape(token_rows, heads_here, GROUP, HEAD_SIZE)
     start_state = (
-        jnp.full((heads_here, query_group, token_rows), NEGATIVE, jnp.float32),
-        jnp.zeros((heads_here, query_group, token_rows), jnp.float32),
-        jnp.zeros((heads_here, query_group, token_rows, HEAD_SIZE), jnp.float32),
+        jnp.full((heads_here, GROUP, token_rows), NEGATIVE, jnp.float32),
+        jnp.zeros((heads_here, GROUP, token_rows), jnp.float32),
+        jnp.zeros((heads_here, GROUP, token_rows, HEAD_SIZE), jnp.float32),
     )
     key_piece = lax.all_gather(key_rows, "ctx", axis=0, tiled=True)
     value_piece = lax.all_gather(value_rows, "ctx", axis=0, tiled=True)
@@ -129,6 +132,139 @@
     return (kl_term, objective)
 
 
+def attention_kernel(lengths, section, block, head, out, rows):
+    tokens = block.shape[0]
+    flip = section[0] * rows
+
+    def place(shape, axis):
+        return lax.broadcasted_iota(jnp.int32, shape, axis) ^ flip
+
+    query_pos = place((1, tokens), 1)
+    begin = jnp.zeros((1, tokens), jnp.int32)
+    start = jnp.int32(0)
+    for index in range(lengths.shape[0] - 1):
+        start = start + lengths[index]
+        begin = jnp.where(query_pos >= start, start, begin)
+    key_pos = place((tokens, 1), 0)
+    valid = (key_pos <= query_pos) & (key_pos >= begin)
+    wide = GROUP * HEAD_SIZE
+    key = block[:, wide : wide + HEAD_SIZE]
+    value = block[:, wide + HEAD_SIZE :]
+    numerator = jnp.zeros((1, tokens), jnp.float32)
+    squares = jnp.zeros((1, tokens), jnp.float32)
+    for index in range(GROUP):
+        cols = slice(index * HEAD_SIZE, (index + 1) * HEAD_SIZE)
+        logits = lax.dot_general(
+            key, block[:, cols], (((1,), (1,)), ((), ())), preferred_element_type=jnp.float32
+        ) * (HEAD_SIZE ** (-0.5))
+        masked = jnp.where(valid, logits, NEGATIVE)
+        peak = jnp.max(masked, axis=0, keepdims=True)
+        weights = jnp.exp(masked - peak)
+        total = jnp.sum(weights, axis=0, keepdims=True)
+        mixed = lax.dot_general(
+            value,
+            weights.astype(jnp.bfloat16),
+            (((0,), (0,)), ((), ())),
+            preferred_element_type=jnp.float32,
+        )
+        attended = mixed / total
+        numerator += jnp.sum(attended * head[cols, :], axis=0, keepdims=True)
+        squares += jnp.sum(attended * attended, axis=0, keepdims=True)
+    out[0:1, :] = numerator
+    out[1:2, :] = squares
+
+
+def split_shards(
+    hidden, w_query, key_projection, value_projection, score_head, lengths, prompt_len, reward
+):
+    rows = hidden.shape[0]
+    depth = w_query.shape[1]
+    ctx = lax.axis_index("ctx")
+    section = lax.axis_index("sec")
+    count = 4
+    f16, f32 = jnp.float16, jnp.float32
+
+    def columns(target):
+        return lax.dynamic_slice_in_dim(hidden, (target % count) * depth, depth, 1)
+
+    pieces = {0: columns(ctx)}
+    for step in (2, 1, 3):
+        pairs = [(i, (i + step) % count) for i in range(count)]
+        pieces[step] = lax.ppermute(columns(ctx + step), "ctx", pairs)
+    both = {
+        step: jnp.concatenate([piece, swapped(piece, "sec", 0)], axis=0)
+        for step, piece in pieces.items()
+    }
+    ring = jnp.concatenate([both[3], both[2], both[1], both[0]], axis=0)
+    doubled = jnp.concatenate([ring, ring], axis=0)
+    chip_rows = 2 * rows
+    tokens_by_ctx = lax.dynamic_slice_in_dim(
+        doubled, ((count - 1 - ctx) % count) * chip_rows, count * chip_rows, 0
+    )
+
+    def product(weight):
+        total = jnp.dot(tokens_by_ctx, weight, preferred_element_type=f32)
+        return (total * LINK_SCALE).astype(f16)
+
+    query_part = product(w_query[0])
+    key_part = product(key_projection[0])
+    value_part = product(value_projection[0])
+    wide = GROUP * HEAD_SIZE
+
+    def block(owner):
+        return jnp.concatenate(
+            [
+                lax.dynamic_slice_in_dim(query_part, owner * wide, wide, 1),
+                lax.dynamic_slice_in_dim(key_part, owner * HEAD_SIZE, HEAD_SIZE, 1),
+                lax.dynamic_slice_in_dim(value_part, owner * HEAD_SIZE, HEAD_SIZE, 1),
+            ],
+            axis=1,
+        )
+
+    left = ctx < 2
+    far = block(jnp.where(left, 3, 0))
+    fold = lax.ppermute(far, "ctx", [(0, 1), (3, 2)])
+    middle = lax.ppermute(block(3 - ctx), "ctx", [(1, 2), (2, 1)])
+    skip = lax.ppermute(block(jnp.where(left, 2, 1)), "ctx", [(0, 2), (3, 1)])
+    near = lax.ppermute(block(ctx ^ 1), "ctx", [(0, 1), (1, 0), (2, 3), (3, 2)])
+    folded = (far.astype(f32) + fold.astype(f32)).astype(f16)
+    ends = lax.ppermute(folded, "ctx", [(1, 3), (2, 0)])
+    total = block(ctx).astype(f32)
+    for part in (middle, skip, near, ends):
+        total = total + part.astype(f32)
+    mine = (total * (1.0 / LINK_SCALE)).astype(jnp.bfloat16)
+
+    head = lax.dynamic_slice_in_dim(score_head[0], ctx * wide, wide, 0).astype(f32)
+    tokens = mine.shape[0]
+    sums = pl.pallas_call(
+        lambda *refs: attention_kernel(*refs, rows),
+        out_shape=jax.ShapeDtypeStruct((2, tokens), f32),
+        in_specs=[
+            pl.BlockSpec(memory_space=pltpu.SMEM),
+            pl.BlockSpec(memory_space=pltpu.SMEM),
+            pl.BlockSpec(memory_space=pltpu.VMEM),
+            pl.BlockSpec(memory_space=pltpu.VMEM),
+        ],
+        out_specs=pl.BlockSpec(memory_space=pltpu.VMEM),
+        compiler_params=pltpu.CompilerParams(vmem_limit_bytes=32 * 1024 * 1024),
+    )(lengths, section.reshape(1), mine, head.reshape(wide, 1))
+
+    spread = sums.reshape(2, count, 2, rows)
+    spread = jnp.where(section == 0, spread, jnp.flip(spread, axis=2))
+    spread = jnp.broadcast_to(
+        spread.transpose(1, 2, 0, 3)[:, :, None], (count, 2, 2, 2, rows)
+    ).reshape(count * 4, 2, rows)
+    spread = lax.all_to_all(spread, ("ctx", "sec", "tp"), 0, 0, tiled=True)
+    spread = jnp.sum(spread.reshape(count, 2, 2, 2, rows), axis=(0, 2))
+    scores = spread[:, 0] / jnp.sqrt(spread[:, 1] / (QUERY_HEAD_COUNT * HEAD_SIZE) + 1e-05)
+    position = (ctx * 2 + section) * rows + jnp.arange(rows, dtype=jnp.int32)
+    _, answer, advantage = rollout_tables(lengths, prompt_len, reward, position)
+    gap = scores[1] - scores[0]
+    kl_term = answer * (jnp.exp(gap) - gap - 1.0)
+    objective = answer * advantage - BETA * kl_term
+    return (kl_term, objective)
+
+
 def solution(mesh):
     placed = (
         P(("grp", "ctx", "sec"), None),
@@ -140,8 +276,10 @@
         P("grp"),
         P("grp"),
     )
+    own_heads = KEY_VALUE_HEADS // mesh.shape["tp"]
+    by_heads = mesh.shape["ctx"] == 4 and own_heads == 4
     return jax.shard_map(
-        shards,
+        split_shards if by_heads else gathered_shards,
         mesh=mesh,
         in_specs=placed,
         out_specs=(P(("grp", "ctx", "sec")), P(("grp", "ctx", "sec"))),

time: 929 us -> 148 us (0.16)
  waiting for transfers between devices: 828 us -> 73.1 us
  blocking collectives: 47.2 us -> 0 us
  starting transfers between devices: 0.15 us -> 20.6 us
  local copies, waits for them, and re-layouts: 5.4 us -> 23.6 us
  between operations: 14.6 us -> 1.61 us
  matrix products: 25.2 us -> 14.4 us
    all_gather x4 -> x0, waiting for transfers between devices: 824 us -> none  [the longest x1 539 us: shards(): query_rows = add_rows(lax.all_gather(query_w, 'ctx', axis=0, tiled=True))]
    ppermute x0 -> x8, waiting for transfers between devices: none -> 64.9 us  [the longest x3 21.3 us: split_shards(): pieces[step] = lax.ppermute(columns(ctx + step), 'ctx', pairs)]
    all_gather x2 -> x0, blocking collectives: 42.2 us -> none  [the longest x1 25.3 us: shards(): value_piece = lax.all_gather(value_rows, 'ctx', axis=0, tiled=True)]
    ppermute x0 -> x8, starting transfers between devices: none -> 15.2 us  [the longest x3 6.06 us: split_shards(): pieces[step] = lax.ppermute(columns(ctx + step), 'ctx', pairs)]
    unnamed x13 -> x37, local copies, waits for them, and re-layouts: 1.68 us -> 16.3 us
    dot_general x6 -> x3, matrix products: 25.2 us -> 14.4 us  [product(): total = jnp.dot(tokens_by_ctx, weight, preferred_element_type=f32)]
  transfers between devices with their start and end apart: 5 -> 13, of which waited for: 5 -> 8; matrix products, arithmetic and copies ran while one was open for 1% -> 8% of each run, Pallas kernels for 0% -> 0%
where the time goes in v1:
time: 148 us; the launch traced here: 147 us
  waiting for transfers between devices  73.1 us (49%)
  local copies, waits for them, and re-layouts  23.6 us (16%)
  starting transfers between devices  20.6 us (14%)
  matrix products  14.4 us (10%)
  other arithmetic  10.7 us (7%)
  Pallas kernels  2.97 us (2%)
  between operations  1.61 us (1%)
    ppermute x3, waiting for transfers between devices, split_shards(): pieces[step] = lax.ppermute(columns(ctx + step), 'ctx', pairs)  21.3 us
    ppermute x1, waiting for transfers between devices, split_shards(): near = lax.ppermute(block(ctx ^ 1), 'ctx', [(0, 1), (1, 0), (2, 3), (3, 2)])  16.3 us
    unnamed x37, local copies, waits for them, and re-layouts  16.3 us
    dot_general x3, matrix products, product(): total = jnp.dot(tokens_by_ctx, weight, preferred_element_type=f32)  14.4 us
    ppermute x1, waiting for transfers between devices, split_shards(): skip = lax.ppermute(block(jnp.where(left, 2, 1)), 'ctx', [(0, 2), (3, 1)])  13.6 us
    ppermute x1, waiting for transfers between devices, split_shards(): ends = lax.ppermute(folded, 'ctx', [(1, 3), (2, 0)])  7.38 us
    ppermute x1, waiting for transfers between devices, split_shards(): fold = lax.ppermute(far, 'ctx', [(0, 1), (3, 2)])  6.35 us
    all_to_all x1, waiting for transfers between devices, split_shards(): spread = lax.all_to_all(spread, ('ctx', 'sec', 'tp'), 0, 0, tiled=True)  6.28 us
  transfers between devices with their start and end apart: 13, of which 8 were waited for; matrix products, arithmetic and copies ran while one was open for 8% of the time, Pallas kernels for 0%

profile of v1, /device:TPU:0, one launch (start us, length us, event | category | flops | bytes accessed | tf_op | source)
XLA Modules:
  0.0 147.0 jit_solution(16752273753266378537)
XLA Ops:
  0.7 2.0 %constant_dynamic-slice_fusion.17 = (bf16[64,2048]{1,0:T(8,128)(2,1)}, bf16[64,2048]{1,0:T(8,128)(2,1)S(1)}, bf16[64,2048]{1,0:T(8,128)(2,1)S(1)}) fusion(bf16[64,8192]{1,0:T(8,128)(2,1)} %param.8, s32[]{:T(128)S(6)} %select_n.108, s32[]{:T(128)S(6)} %select_n.106, s32[]{:T(128)S(6)} %select_n.104), kind=kLoop, calls=%fused_computation.57 | loop fusion | bytes 1572876 | tf_op jit(solution)/shard_map/dynamic_slice | solution.py:188
  2.7 5.0 %collective-permute-start = (bf16[64,2048]{1,0:T(8,128)(2,1)S(1)}, bf16[64,2048]{1,0:T(8,128)(2,1)S(1)}, u32[]{:S(2)}, u32[]{:S(2)}) collective-permute-start(bf16[64,2048]{1,0:T(8,128)(2,1)S(1)} %get-tuple-element.15), channel_id=1, source_target_pairs={{0,12},{4,0},{8,4},{12,8},{1,13},{5,1},{9,5},{13,9},{2,14},{6,2},{... | collective-permute-start | bytes 786440 | tf_op jit(solution)/shard_map/ppermute | solution.py:193
  7.8 1.0 collective-permute-start.4
  8.8 5.7 %collective-permute-done = bf16[64,2048]{1,0:T(8,128)(2,1)S(1)} collective-permute-done((bf16[64,2048]{1,0:T(8,128)(2,1)S(1)}, bf16[64,2048]{1,0:T(8,128)(2,1)S(1)}, u32[]{:S(2)}, u32[]{:S(2)}) %collective-permute-start) | collective-permute-done | bytes 262176 | tf_op jit(solution)/shard_map/ppermute | solution.py:193
  14.5 15.6 %collective-permute-done.2 = bf16[64,2048]{1,0:T(8,128)(2,1)S(1)} collective-permute-done((bf16[64,2048]{1,0:T(8,128)(2,1)S(1)}, bf16[64,2048]{1,0:T(8,128)(2,1)S(1)}, u32[]{:S(2)}, u32[]{:S(2)}) %collective-permute-start.2) | collective-permute-done | bytes 262176 | tf_op jit(solution)/shard_map/ppermute | solution.py:193
  30.6 0.7 constant_dynamic-update-slice_fusion.15
  31.3 0.7 constant_dynamic-update-slice_fusion.14
  32.0 0.7 constant_dynamic-update-slice_fusion.13
  32.7 0.7 constant_dynamic-update-slice_fusion.12
  33.5 0.7 constant_dynamic-update-slice_fusion.11
  34.2 0.7 copy-done.4
  34.9 0.7 constant_dynamic-update-slice_fusion.10
  35.6 1.8 %constant_dynamic-update-slice_fusion.9 = (bf16[1024,2048]{1,0:T(8,128)(2,1)}, bf16[64,2048]{1,0:T(8,128)(2,1)}) fusion(bf16[1024,2048]{1,0:T(8,128)(2,1)} %constant_dynamic-update-slice_fusion.10, bf16[64,8192]{1,0:T(8,128)(2,1)} %param.8, s32[]{:T(128)S(6)} %select_n.110), kind=kLoop, calls=%fused_computation.29 | loop fusion | bytes 786436
  37.4 1.9 %collective-permute-done.6 = bf16[64,2048]{1,0:T(8,128)(2,1)} collective-permute-done((bf16[64,2048]{1,0:T(8,128)(2,1)}, bf16[64,2048]{1,0:T(8,128)(2,1)}, u32[]{:S(2)}, u32[]{:S(2)}) %collective-permute-start.6) | collective-permute-done | bytes 262176 | tf_op jit(solution)/shard_map/ppermute | solution.py:20
  39.3 1.7 %constant_dynamic-update-slice_fusion.8 = bf16[1024,2048]{1,0:T(8,128)(2,1)} fusion(bf16[1024,2048]{1,0:T(8,128)(2,1)} %get-tuple-element.6, bf16[64,2048]{1,0:T(8,128)(2,1)} %collective-permute-done.6), kind=kLoop, calls=%fused_computation.28 | loop fusion | bytes 524288
  41.0 0.7 constant_dynamic-update-slice_fusion.7
  41.7 0.7 constant_dynamic-update-slice_fusion.6
  42.4 0.7 constant_dynamic-update-slice_fusion.5
  43.1 0.7 constant_dynamic-update-slice_fusion.4
  43.9 0.7 constant_dynamic-update-slice_fusion.3
  44.6 1.7 %constant_dynamic-update-slice_fusion.2 = bf16[1024,2048]{1,0:T(8,128)(2,1)} fusion(bf16[1024,2048]{1,0:T(8,128)(2,1)} %constant_dynamic-update-slice_fusion.3, bf16[64,2048]{1,0:T(8,128)(2,1)} %copy-done.4), kind=kLoop, calls=%fused_computation.22 | loop fusion | bytes 524288
  46.3 1.7 %constant_dynamic-update-slice_fusion.1 = bf16[1024,2048]{1,0:T(8,128)(2,1)} fusion(bf16[1024,2048]{1,0:T(8,128)(2,1)} %constant_dynamic-update-slice_fusion.2, bf16[64,2048]{1,0:T(8,128)(2,1)} %get-tuple-element.7), kind=kLoop, calls=%fused_computation.21 | loop fusion | bytes 524288
  47.9 1.7 %constant_dynamic-update-slice_fusion = bf16[1024,2048]{1,0:T(8,128)(2,1)} fusion(bf16[1024,2048]{1,0:T(8,128)(2,1)} %constant_dynamic-update-slice_fusion.1, bf16[64,2048]{1,0:T(8,128)(2,1)} %collective-permute-done.6), kind=kLoop, calls=%fused_computation.20 | loop fusion | bytes 524288 | tf_op jit(solution)/shard_map/concatenate | solution.py:199
  49.6 8.5 %multiply_convert_fusion = f16[512,2048]{1,0:T(8,128)(2,1)S(1)} fusion(bf16[1,2048,2048]{2,1,0:T(8,128)(2,1)} %param.9, bf16[1024,2048]{1,0:T(8,128)(2,1)} %constant_dynamic-update-slice_fusion, s32[]{:T(128)S(6)} %select_n.112), kind=kOutput, calls=%fused_computation.2 | convolution fusion | flops 4297064448 | bytes 12582916 | tf_op jit(solution)/shard_map/dot_general | solution.py:206
  58.1 3.0 %fusion.26 = f16[512,512]{1,0:T(8,128)(2,1)S(1)} fusion(bf16[1,2048,512]{2,1,0:T(8,128)(2,1)S(1)} %copy-done, bf16[1024,2048]{1,0:T(8,128)(2,1)} %constant_dynamic-update-slice_fusion, s32[]{:T(128)S(6)} %select_n.112), kind=kOutput, calls=%fused_computation.15 | convolution fusion | flops 1074266112 | bytes 4718596 | tf_op jit(solution)/shard_map/dot_general | solution.py:206
  61.1 2.9 %fusion.21 = f16[512,512]{1,0:T(8,128)(2,1)S(1)} fusion(bf16[1,2048,512]{2,1,0:T(8,128)(2,1)S(1)} %copy-done.7, bf16[1024,2048]{1,0:T(8,128)(2,1)} %constant_dynamic-update-slice_fusion, s32[]{:T(128)S(6)} %select_n.112), kind=kOutput, calls=%fused_computation.14 | convolution fusion | flops 1074266112 | bytes 4718596 | tf_op jit(solution)/shard_map/dot_general | solution.py:206
  64.0 1.7 %constant_dynamic-slice_fusion.15 = (f16[512,512]{1,0:T(8,128)(2,1)S(1)}, f16[512,512]{1,0:T(8,128)(2,1)S(1)}, f16[512,512]{1,0:T(8,128)(2,1)}, f16[512,512]{1,0:T(8,128)(2,1)}, f16[512,512]{1,0:T(8,128)(2,1)}) fusion(f16[512,2048]{1,0:T(8,128)(2,1)S(1)} %multiply_convert_fusion, s32[]{:T(128)S(6)} %select_n.113, s32[]{:T(128)S(6)} %select_n.123, ...), kind=kLoop, calls=%fused_computation.54 | loop fusion | bytes 5242900 | tf_op jit(solution)/shard_map/dynamic_slice | solution.py:217
  65.8 1.1 constant_dynamic-slice_fusion.13
  66.9 1.1 pad_maximum_fusion.3
  68.0 3.5 %collective-permute-start.10 = (f16[512,768]{1,0:T(8,128)(2,1)}, f16[512,768]{1,0:T(8,128)(2,1)}, u32[]{:S(2)}, u32[]{:S(2)}) collective-permute-start(f16[512,768]{1,0:T(8,128)(2,1)} %pad_maximum_fusion.3), channel_id=1, source_target_pairs={{0,4},{12,8},{1,5},{13,9},{2,6},{14,10},{3,7},{15,11},{16,20},{28,... | collective-permute-start | bytes 2359304 | tf_op jit(solution)/shard_map/ppermute | solution.py:226
  71.5 0.7 fusion.37
  73.8 1.5 %pad_maximum_fusion = f16[512,768]{1,0:T(8,128)(2,1)S(1)} fusion(f16[512,128]{1,0:T(8,128)(2,1)} %get-tuple-element.25, f16[512,128]{1,0:T(8,128)(2,1)} %get-tuple-element.26, f16[512,512]{1,0:T(8,128)(2,1)} %get-tuple-element.12), kind=kLoop, calls=%fused_computation.16 | loop fusion | flops 786432 | bytes 1572864 | tf_op jit(solution)/shard_map/concatenate | solution.py:215
  75.3 0.7 collective-permute-start.7
  76.0 1.4 pad_maximum_fusion.1
  77.4 3.4 %collective-permute-start.8 = (f16[512,768]{1,0:T(8,128)(2,1)S(1)}, f16[512,768]{1,0:T(8,128)(2,1)S(1)}, u32[]{:S(2)}, u32[]{:S(2)}) collective-permute-start(f16[512,768]{1,0:T(8,128)(2,1)S(1)} %pad_maximum_fusion.1), channel_id=1, source_target_pairs={{0,8},{12,4},{1,9},{13,5},{2,10},{14,6},{3,11},{15,7},{16,24},{28,... | collective-permute-start | bytes 2359304 | tf_op jit(solution)/shard_map/ppermute | solution.py:228
  80.9 1.4 pad_maximum_fusion.2
  82.4 6.4 %collective-permute-done.10 = f16[512,768]{1,0:T(8,128)(2,1)} collective-permute-done((f16[512,768]{1,0:T(8,128)(2,1)}, f16[512,768]{1,0:T(8,128)(2,1)}, u32[]{:S(2)}, u32[]{:S(2)}) %collective-permute-start.10) | collective-permute-done | bytes 786464 | tf_op jit(solution)/shard_map/ppermute | solution.py:226
  88.7 1.5 %add_convert_fusion = f16[512,768]{1,0:T(8,128)(2,1)S(1)} fusion(f16[512,768]{1,0:T(8,128)(2,1)} %collective-permute-done.10, f16[512,128]{1,0:T(8,128)(2,1)S(1)} %get-tuple-element.22, f16[512,128]{1,0:T(8,128)(2,1)S(1)} %copy-done.3, f16[512,512]{1,0:T(8,128)(2,1)S(1)} %get-tuple-element.9), kind=kLoop, calls=%fused_computation.11 | loop fusion | flops 2359296 | bytes 2359296 | tf_op jit(solution)/shard_map/convert_element_type | solution.py:230
  90.2 1.5 %collective-permute-start.11 = (f16[512,768]{1,0:T(8,128)(2,1)S(1)}, f16[512,768]{1,0:T(8,128)(2,1)S(1)}, u32[]{:S(2)}, u32[]{:S(2)}) collective-permute-start(f16[512,768]{1,0:T(8,128)(2,1)S(1)} %add_convert_fusion), channel_id=1, source_target_pairs={{4,12},{8,0},{5,13},{9,1},{6,14},{10,2},{7,15},{11,3},{20,28},{24,... | collective-permute-start | bytes 2359304 | tf_op jit(solution)/shard_map/ppermute | solution.py:231
  91.9 13.6 %collective-permute-done.8 = f16[512,768]{1,0:T(8,128)(2,1)S(1)} collective-permute-done((f16[512,768]{1,0:T(8,128)(2,1)S(1)}, f16[512,768]{1,0:T(8,128)(2,1)S(1)}, u32[]{:S(2)}, u32[]{:S(2)}) %collective-permute-start.8) | collective-permute-done | bytes 786464 | tf_op jit(solution)/shard_map/ppermute | solution.py:228
  105.5 16.3 %collective-permute-done.9 = f16[512,768]{1,0:T(8,128)(2,1)S(1)} collective-permute-done((f16[512,768]{1,0:T(8,128)(2,1)S(1)}, f16[512,768]{1,0:T(8,128)(2,1)S(1)}, u32[]{:S(2)}, u32[]{:S(2)}) %collective-permute-start.9) | collective-permute-done | bytes 786464 | tf_op jit(solution)/shard_map/ppermute | solution.py:229
  121.8 7.4 %collective-permute-done.11 = f16[512,768]{1,0:T(8,128)(2,1)S(1)} collective-permute-done((f16[512,768]{1,0:T(8,128)(2,1)S(1)}, f16[512,768]{1,0:T(8,128)(2,1)S(1)}, u32[]{:S(2)}, u32[]{:S(2)}) %collective-permute-start.11) | collective-permute-done | bytes 786464 | tf_op jit(solution)/shard_map/ppermute | solution.py:231
  129.2 0.7 multiply_convert_fusion.1.refs_2_
  130.0 3.0 %shard_map.95 = f32[2,512]{1,0:T(2,128)S(1)} custom-call(s32[4]{0:T(128)S(1)} %copy-done.1, s32[1]{0:T(128)} %bitcast.2.refs_1_, bf16[512,768]{1,0:T(8,128)(2,1)S(1)} %multiply_convert_fusion.1.refs_2_, f32[512,1]{1,0:T(8,128)S(1)} %copy.27.refs_3_), custom_call_target="tpu_custom_call" | custom-call | tf_op jit(solution)/shard_map/pallas_call | solution.py:239
  133.1 0.7 reshape.85
  133.8 4.9 %all-to-all-start = ((f32[16,1,128]{2,1,0:T(1,128)}), f32[16,1,128]{2,1,0:T(1,128)S(1)}, u32[]{:S(2)}, u32[]{:S(2)}) async-start(f32[16,1,128]{2,1,0:T(1,128)} %reshape.85), calls=%async_computation | async-start | bytes 16384 | tf_op jit(solution)/shard_map/all_to_all | solution.py:257
  138.8 6.3 %all-to-all-done = f32[16,1,128]{2,1,0:T(1,128)S(1)} async-done(((f32[16,1,128]{2,1,0:T(1,128)}), f32[16,1,128]{2,1,0:T(1,128)S(1)}, u32[]{:S(2)}, u32[]{:S(2)}) %all-to-all-start) | async-done | bytes 8224 | tf_op jit(solution)/shard_map/all_to_all | solution.py:257
  145.6 0.7 reduce
  (50 shorter events, 3.2 us)
Async XLA Ops:
  0.6 57.5 %copy-start = (bf16[1,2048,512]{2,1,0:T(8,128)(2,1)S(1)}, bf16[1,2048,512]{2,1,0:T(8,128)(2,1)}, u32[]{:S(2)}) copy-start(bf16[1,2048,512]{2,1,0:T(8,128)(2,1)} %param.10) | copy-start | bytes 6291460
  2.7 11.8 %collective-permute-start = (bf16[64,2048]{1,0:T(8,128)(2,1)S(1)}, bf16[64,2048]{1,0:T(8,128)(2,1)S(1)}, u32[]{:S(2)}, u32[]{:S(2)}) collective-permute-start(bf16[64,2048]{1,0:T(8,128)(2,1)S(1)} %get-tuple-element.15), channel_id=1, source_target_pairs={{0,12},{4,0},{8,4},{12,8},{1,13},{5,1},{9,5},{13,9},{2,14},{6,2},{... | collective-permute-start | bytes 786440 | tf_op jit(solution)/shard_map/ppermute | solution.py:193
  7.8 22.3 %collective-permute-start.2 = (bf16[64,2048]{1,0:T(8,128)(2,1)S(1)}, bf16[64,2048]{1,0:T(8,128)(2,1)S(1)}, u32[]{:S(2)}, u32[]{:S(2)}) collective-permute-start(bf16[64,2048]{1,0:T(8,128)(2,1)S(1)} %get-tuple-element.14), channel_id=1, source_target_pairs={{0,8},{4,12},{8,0},{12,4},{1,9},{5,13},{9,1},{13,5},{2,10},{6,14},... | collective-permute-start | bytes 786440 | tf_op jit(solution)/shard_map/ppermute | solution.py:193
  7.8 22.3 %collective-permute-start.4 = (bf16[64,2048]{1,0:T(8,128)(2,1)}, bf16[64,2048]{1,0:T(8,128)(2,1)S(1)}, u32[]{:S(2)}, u32[]{:S(2)}) collective-permute-start(bf16[64,2048]{1,0:T(8,128)(2,1)} %get-tuple-element.13), channel_id=1, source_target_pairs={{0,4},{4,8},{8,12},{12,0},{1,5},{5,9},{9,13},{13,1},{2,6},{6,10},{... | collective-permute-start | bytes 786440 | tf_op jit(solution)/shard_map/ppermute | solution.py:193
  14.5 16.8 %collective-permute-start.1 = (bf16[64,2048]{1,0:T(8,128)(2,1)S(1)}, bf16[64,2048]{1,0:T(8,128)(2,1)S(1)}, u32[]{:S(2)}, u32[]{:S(2)}) collective-permute-start(bf16[64,2048]{1,0:T(8,128)(2,1)S(1)} %collective-permute-done), channel_id=1, source_target_pairs={{0,2},{2,0},{1,3},{3,1},{4,6},{6,4},{5,7},{7,5},{8,10},{10,8},{9,1... | collective-permute-start | bytes 786440 | tf_op jit(solution)/shard_map/ppermute | solution.py:20
  30.1 2.7 %collective-permute-start.3 = (bf16[64,2048]{1,0:T(8,128)(2,1)S(1)}, bf16[64,2048]{1,0:T(8,128)(2,1)S(1)}, u32[]{:S(2)}, u32[]{:S(2)}) collective-permute-start(bf16[64,2048]{1,0:T(8,128)(2,1)S(1)} %collective-permute-done.2), channel_id=1, source_target_pairs={{0,2},{2,0},{1,3},{3,1},{4,6},{6,4},{5,7},{7,5},{8,10},{10,8},{9,1... | collective-permute-start | bytes 786440 | tf_op jit(solution)/shard_map/ppermute | solution.py:20
  30.1 4.1 %collective-permute-start.5 = (bf16[64,2048]{1,0:T(8,128)(2,1)S(1)}, bf16[64,2048]{1,0:T(8,128)(2,1)S(1)}, u32[]{:S(2)}, u32[]{:S(2)}) collective-permute-start(bf16[64,2048]{1,0:T(8,128)(2,1)S(1)} %collective-permute-done.4), channel_id=1, source_target_pairs={{0,2},{2,0},{1,3},{3,1},{4,6},{6,4},{5,7},{7,5},{8,10},{10,8},{9,1... | collective-permute-start | bytes 786440 | tf_op jit(solution)/shard_map/ppermute | solution.py:20
  34.2 0.7 copy-start.4
  37.4 1.9 %collective-permute-start.6 = (bf16[64,2048]{1,0:T(8,128)(2,1)}, bf16[64,2048]{1,0:T(8,128)(2,1)}, u32[]{:S(2)}, u32[]{:S(2)}) collective-permute-start(bf16[64,2048]{1,0:T(8,128)(2,1)} %get-tuple-element.7), channel_id=1, source_target_pairs={{0,2},{2,0},{1,3},{3,1},{4,6},{6,4},{5,7},{7,5},{8,10},{10,8},{9,1... | collective-permute-start | bytes 786440 | tf_op jit(solution)/shard_map/ppermute | solution.py:20
  58.1 3.0 %copy-start.7 = (bf16[1,2048,512]{2,1,0:T(8,128)(2,1)S(1)}, bf16[1,2048,512]{2,1,0:T(8,128)(2,1)}, u32[]{:S(2)}) copy-start(bf16[1,2048,512]{2,1,0:T(8,128)(2,1)} %param.11) | copy-start | bytes 6291460
  64.0 8.3 %copy-start.1 = (s32[4]{0:T(128)S(1)}, s32[4]{0:T(128)}, u32[]{:S(2)}) copy-start(s32[4]{0:T(128)} %refs_0_.1) | copy-start | bytes 52
  64.0 8.5 %copy-start.8 = (f32[4]{0:T(128)S(1)}, f32[4]{0:T(128)}, u32[]{:S(2)}) copy-start(f32[4]{0:T(128)} %param.15) | copy-start | bytes 52
  66.9 4.6 %copy-start.2 = (f16[512,128]{1,0:T(8,128)(2,1)}, f16[512,128]{1,0:T(8,128)(2,1)S(1)}, u32[]{:S(2)}) copy-start(f16[512,128]{1,0:T(8,128)(2,1)S(1)} %get-tuple-element.29) | copy-start | bytes 393220
  68.0 20.7 %collective-permute-start.10 = (f16[512,768]{1,0:T(8,128)(2,1)}, f16[512,768]{1,0:T(8,128)(2,1)}, u32[]{:S(2)}, u32[]{:S(2)}) collective-permute-start(f16[512,768]{1,0:T(8,128)(2,1)} %pad_maximum_fusion.3), channel_id=1, source_target_pairs={{0,4},{12,8},{1,5},{13,9},{2,6},{14,10},{3,7},{15,11},{16,20},{28,... | collective-permute-start | bytes 2359304 | tf_op jit(solution)/shard_map/ppermute | solution.py:226
  73.8 15.0 %copy-start.3 = (f16[512,128]{1,0:T(8,128)(2,1)S(1)}, f16[512,128]{1,0:T(8,128)(2,1)}, u32[]{:S(2)}) copy-start(f16[512,128]{1,0:T(8,128)(2,1)} %copy-done.2) | copy-start | bytes 393220
  73.8 55.5 %copy-start.5 = (f16[512,128]{1,0:T(8,128)(2,1)S(1)}, f16[512,128]{1,0:T(8,128)(2,1)}, u32[]{:S(2)}) copy-start(f16[512,128]{1,0:T(8,128)(2,1)} %get-tuple-element.21) | copy-start | bytes 393220
  73.8 55.4 %copy-start.6 = (f16[512,128]{1,0:T(8,128)(2,1)S(1)}, f16[512,128]{1,0:T(8,128)(2,1)}, u32[]{:S(2)}) copy-start(f16[512,128]{1,0:T(8,128)(2,1)} %get-tuple-element.30) | copy-start | bytes 393220
  75.3 16.7 %collective-permute-start.7 = (f16[512,768]{1,0:T(8,128)(2,1)S(1)}, f16[512,768]{1,0:T(8,128)(2,1)S(1)}, u32[]{:S(2)}, u32[]{:S(2)}) collective-permute-start(f16[512,768]{1,0:T(8,128)(2,1)S(1)} %pad_maximum_fusion), channel_id=1, source_target_pairs={{4,8},{8,4},{5,9},{9,5},{6,10},{10,6},{7,11},{11,7},{20,24},{24,20... | collective-permute-start | bytes 2359304 | tf_op jit(solution)/shard_map/ppermute | solution.py:227
  77.4 28.1 %collective-permute-start.8 = (f16[512,768]{1,0:T(8,128)(2,1)S(1)}, f16[512,768]{1,0:T(8,128)(2,1)S(1)}, u32[]{:S(2)}, u32[]{:S(2)}) collective-permute-start(f16[512,768]{1,0:T(8,128)(2,1)S(1)} %pad_maximum_fusion.1), channel_id=1, source_target_pairs={{0,8},{12,4},{1,9},{13,5},{2,10},{14,6},{3,11},{15,7},{16,24},{28,... | collective-permute-start | bytes 2359304 | tf_op jit(solution)/shard_map/ppermute | solution.py:228
  82.3 56.4 %copy-start.9 = (s32[4]{0:T(128)S(1)}, s32[4]{0:T(128)}, u32[]{:S(2)}) copy-start(s32[4]{0:T(128)} %param.14) | copy-start | bytes 52
  82.3 39.5 %collective-permute-start.9 = (f16[512,768]{1,0:T(8,128)(2,1)S(1)}, f16[512,768]{1,0:T(8,128)(2,1)S(1)}, u32[]{:S(2)}, u32[]{:S(2)}) collective-permute-start(f16[512,768]{1,0:T(8,128)(2,1)S(1)} %pad_maximum_fusion.2), channel_id=1, source_target_pairs={{0,4},{4,0},{8,12},{12,8},{1,5},{5,1},{9,13},{13,9},{2,6},{6,2},{1... | collective-permute-start | bytes 2359304 | tf_op jit(solution)/shard_map/ppermute | solution.py:229
  90.2 39.0 %collective-permute-start.11 = (f16[512,768]{1,0:T(8,128)(2,1)S(1)}, f16[512,768]{1,0:T(8,128)(2,1)S(1)}, u32[]{:S(2)}, u32[]{:S(2)}) collective-permute-start(f16[512,768]{1,0:T(8,128)(2,1)S(1)} %add_convert_fusion), channel_id=1, source_target_pairs={{4,12},{8,0},{5,13},{9,1},{6,14},{10,2},{7,15},{11,3},{20,28},{24,... | collective-permute-start | bytes 2359304 | tf_op jit(solution)/shard_map/ppermute | solution.py:231
  133.8 11.3 %all-to-all-start = ((f32[16,1,128]{2,1,0:T(1,128)}), f32[16,1,128]{2,1,0:T(1,128)S(1)}, u32[]{:S(2)}, u32[]{:S(2)}) async-start(f32[16,1,128]{2,1,0:T(1,128)} %reshape.85), calls=%async_computation | async-start | bytes 16384 | tf_op jit(solution)/shard_map/all_to_all | solution.py:257

commit v2 on v1

--- a/solution.py
+++ b/solution.py
@@ -174,6 +174,57 @@
     out[1:2, :] = squares
 
 
+def partial_kernel(plan, *refs):
+    pieces, (query_w, key_w, value_w, out, tokens) = refs[:8], refs[8:]
+    rows = pieces[0].shape[0]
+    wide = query_w.shape[2]
+
+    @pl.when(pl.program_id(0) == 0)
+    def _():
+        for index, piece in enumerate(pieces):
+            base = plan[index // 2] * (2 * rows) + (index % 2) * rows
+            tokens[pl.ds(pl.multiple_of(base, rows), rows), :] = piece[...]
+
+    step = 2 * rows
+    for first in range(0, tokens.shape[0], step):
+        held = tokens[first : first + step, :]
+        for weight, start in ((query_w, 0), (key_w, wide), (value_w, wide + HEAD_SIZE)):
+            total = jnp.dot(held, weight[0], preferred_element_type=jnp.float32)
+            out[0, first : first + step, start : start + weight.shape[2]] = total * LINK_SCALE
+
+
+def partials(plan, pieces, weights, skipped, count):
+    rows, depth = pieces[0].shape
+    wide = GROUP * HEAD_SIZE
+    tokens = len(pieces) * rows
+    cols = wide + 2 * HEAD_SIZE
+    sources = len(pieces) // 2
+
+    def owner_block(width):
+        return pl.BlockSpec(
+            (1, depth, width), lambda i, plan: (0, 0, plan[sources + skipped + i])
+        )
+
+    return pl.pallas_call(
+        partial_kernel,
+        out_shape=jax.ShapeDtypeStruct((count, tokens, cols), jnp.float32),
+        grid_spec=pltpu.PrefetchScalarGridSpec(
+            num_scalar_prefetch=1,
+            grid=(count,),
+            in_specs=[pl.BlockSpec((rows, depth), lambda i, plan: (0, 0)) for _ in pieces]
+            + [owner_block(wide), owner_block(HEAD_SIZE), owner_block(HEAD_SIZE)],
+            out_specs=pl.BlockSpec((1, tokens, cols), lambda i, plan: (i, 0, 0)),
+            scratch_shapes=[pltpu.VMEM((tokens, depth), jnp.bfloat16)],
+        ),
+        compiler_params=pltpu.CompilerParams(vmem_limit_bytes=40 * 1024 * 1024),
+        cost_estimate=pl.CostEstimate(
+            flops=2 * count * tokens * depth * cols,
+            bytes_accessed=2 * tokens * depth + count * cols * (2 * depth + 4 * tokens),
+            transcendentals=0,
+        ),
+    )(plan, *pieces, *weights)
+
+
 def split_shards(
     hidden, w_query, key_projection, value_projection, score_head, lengths, prompt_len, reward
 ):
@@ -187,53 +238,35 @@
     def columns(target):
         return lax.dynamic_slice_in_dim(hidden, (target % count) * depth, depth, 1)
 
-    pieces = {0: columns(ctx)}
-    for step in (2, 1, 3):
+    order = (2, 1, 3, 0)
+    pieces = []
+    for step in order:
         pairs = [(i, (i + step) % count) for i in range(count)]
-        pieces[step] = lax.ppermute(columns(ctx + step), "ctx", pairs)
-    both = {
-        step: jnp.concatenate([piece, swapped(piece, "sec", 0)], axis=0)
-        for step, piece in pieces.items()
-    }
-    ring = jnp.concatenate([both[3], both[2], both[1], both[0]], axis=0)
-    doubled = jnp.concatenate([ring, ring], axis=0)
-    chip_rows = 2 * rows
-    tokens_by_ctx = lax.dynamic_slice_in_dim(
-        doubled, ((count - 1 - ctx) % count) * chip_rows, count * chip_rows, 0
-    )
-
-    def product(weight):
-        total = jnp.dot(tokens_by_ctx, weight, preferred_element_type=f32)
-        return (total * LINK_SCALE).astype(f16)
-
-    query_part = product(w_query[0])
-    key_part = product(key_projection[0])
-    value_part = product(value_projection[0])
-    wide = GROUP * HEAD_SIZE
-
-    def block(owner):
-        return jnp.concatenate(
-            [
-                lax.dynamic_slice_in_dim(query_part, owner * wide, wide, 1),
-                lax.dynamic_slice_in_dim(key_part, owner * HEAD_SIZE, HEAD_SIZE, 1),
-                lax.dynamic_slice_in_dim(value_part, owner * HEAD_SIZE, HEAD_SIZE, 1),
-            ],
-            axis=1,
-        )
+        piece = columns(ctx + step)
+        if step:
+            piece = lax.ppermute(piece, "ctx", pairs)
+        pieces += [piece, swapped(piece, "sec", 0)]
 
     left = ctx < 2
-    far = block(jnp.where(left, 3, 0))
-    fold = lax.ppermute(far, "ctx", [(0, 1), (3, 2)])
-    middle = lax.ppermute(block(3 - ctx), "ctx", [(1, 2), (2, 1)])
-    skip = lax.ppermute(block(jnp.where(left, 2, 1)), "ctx", [(0, 2), (3, 1)])
-    near = lax.ppermute(block(ctx ^ 1), "ctx", [(0, 1), (1, 0), (2, 3), (3, 2)])
-    folded = (far.astype(f32) + fold.astype(f32)).astype(f16)
+    owners = (jnp.where(left, 3, 0), jnp.where(left, 2, 1), ctx ^ 1, ctx)
+    plan = jnp.stack([(ctx - step) % count for step in order] + list(owners)).astype(jnp.int32)
+    weights = (w_query, key_projection, value_projection)
+    first = partials(plan, pieces, weights, 0, 2)
+    second = partials(plan, pieces, weights, 2, 2)
+
+    fold = lax.ppermute(first[0].astype(f16), "ctx", [(0, 1), (3, 2)])
+    inner = first[1].astype(f16)
+    middle = lax.ppermute(inner, "ctx", [(1, 2), (2, 1)])
+    skip = lax.ppermute(inner, "ctx", [(0, 2), (3, 1)])
+    near = lax.ppermute(second[0].astype(f16), "ctx", [(0, 1), (1, 0), (2, 3), (3, 2)])
+    folded = (first[0] + fold.astype(f32)).astype(f16)
     ends = lax.ppermute(folded, "ctx", [(1, 3), (2, 0)])
-    total = block(ctx).astype(f32)
+    total = second[1]
     for part in (middle, skip, near, ends):
         total = total + part.astype(f32)
     mine = (total * (1.0 / LINK_SCALE)).astype(jnp.bfloat16)
 
+    wide = GROUP * HEAD_SIZE
     head = lax.dynamic_slice_in_dim(score_head[0], ctx * wide, wide, 0).astype(f32)
     tokens = mine.shape[0]
     sums = pl.pallas_call(

time: 148 us -> 117 us (0.79)
  local copies, waits for them, and re-layouts: 23.6 us -> 5.39 us
  Pallas kernels: 2.97 us -> 17.5 us
  matrix products: 14.4 us -> 0 us
  waiting for transfers between devices: 73.1 us -> 61.3 us
  other arithmetic: 10.7 us -> 4 us
  starting transfers between devices: 20.6 us -> 27.1 us
    pallas_call x0 -> x2, Pallas kernels: none -> 14.5 us  [partials(): pl.pallas_call(partial_kernel, out_shape=jax.ShapeDtypeStruct((count, tok...]
    dot_general x3 -> x0, matrix products: 14.4 us -> none  [product(): total = jnp.dot(tokens_by_ctx, weight, preferred_element_type=f32)]
    unnamed x37 -> x14, local copies, waits for them, and re-layouts: 16.3 us -> 2.36 us
    ppermute x7, starting transfers between devices: 13.7 us -> 20.3 us  [the longest x3 7.93 us: split_shards(): piece = lax.ppermute(piece, 'ctx', pairs)]
    ppermute x7, waiting for transfers between devices: 57.5 us -> 51.1 us  [the longest x1 15.9 us: split_shards(): lax.ppermute(second[0].astype(f16), 'ctx', [(0, 1), (1, 0), (2, 3), (3, 2)])]
    concatenate x4 -> x0, other arithmetic: 5.47 us -> none  [block(): jnp.concatenate([lax.dynamic_slice_in_dim(query_part, owner * wide, wide,...]
    ppermute x1, waiting for transfers between devices: 7.38 us -> 3.91 us  [split_shards(): ends = lax.ppermute(folded, 'ctx', [(1, 3), (2, 0)])]
    dynamic_slice x2 -> x0, local copies, waits for them, and re-layouts: 2.83 us -> none  [the longest x1 1.74 us: block(): lax.dynamic_slice_in_dim(query_part, owner * wide, wide, 1)]
  transfers between devices with their start and end apart: 13 -> 13, of which waited for: 8 -> 7; matrix products, arithmetic and copies ran while one was open for 8% -> 3% of each run, Pallas kernels for 0% -> 6%
where the time goes in v2:
time: 117 us
  waiting for transfers between devices  61.3 us (52%)
  starting transfers between devices  27.1 us (23%)
  Pallas kernels  17.5 us (15%)
  local copies, waits for them, and re-layouts  5.39 us (5%)
  other arithmetic  4 us (3%)
  between operations  1.59 us (1%)
    ppermute x1, waiting for transfers between devices, split_shards(): lax.ppermute(second[0].astype(f16), 'ctx', [(0, 1), (1, 0), (2, 3), (3, 2)])  15.9 us
    ppermute x1, waiting for transfers between devices, split_shards(): skip = lax.ppermute(inner, 'ctx', [(0, 2), (3, 1)])  15.2 us
    ppermute x3, waiting for transfers between devices, split_shards(): piece = lax.ppermute(piece, 'ctx', pairs)  14.8 us
    pallas_call x2, Pallas kernels, partials(): pl.pallas_call(partial_kernel, out_shape=jax.ShapeDtypeStruct((count, tok...  14.5 us
    ppermute x3, starting transfers between devices, split_shards(): piece = lax.ppermute(piece, 'ctx', pairs)  7.93 us
    ppermute x1, starting transfers between devices, split_shards(): fold = lax.ppermute(first[0].astype(f16), 'ctx', [(0, 1), (3, 2)])  7.19 us
    all_to_all x1, waiting for transfers between devices, split_shards(): spread = lax.all_to_all(spread, ('ctx', 'sec', 'tp'), 0, 0, tiled=True)  6.28 us
    ppermute x1, waiting for transfers between devices, split_shards(): fold = lax.ppermute(first[0].astype(f16), 'ctx', [(0, 1), (3, 2)])  5.24 us
  transfers between devices with their start and end apart: 13, of which 7 were waited for; matrix products, arithmetic and copies ran while one was open for 3% of the time, Pallas kernels for 6%

profile of v2, /device:TPU:0, one launch (start us, length us, event | category | flops | bytes accessed | tf_op | source)
XLA Modules:
  0.0 116.9 jit_solution(6058493536281411847)
XLA Ops:
  0.7 1.4 %constant_dynamic-slice_fusion = (bf16[64,2048]{1,0:T(8,128)(2,1)S(1)}, bf16[64,2048]{1,0:T(8,128)(2,1)S(1)}, bf16[64,2048]{1,0:T(8,128)(2,1)S(1)}, bf16[64,2048]{1,0:T(8,128)(2,1)S(1)}) fusion(bf16[64,8192]{1,0:T(8,128)(2,1)} %param.8, s32[]{:T(128)S(6)} %select_n.89, s32[]{:T(128)S(6)} %select_n.86, s32[]{:T(128)S(6)} %select_n.84, s32[]{:T(128)S(6)} %select_n.88), kind=kLoop, calls=%fused_computation.23 | loop fusion | bytes 2097168 | tf_op jit(solution)/shard_map/dynamic_slice | solution.py:239
  2.2 4.1 %collective-permute-start = (bf16[64,2048]{1,0:T(8,128)(2,1)S(1)}, bf16[64,2048]{1,0:T(8,128)(2,1)S(1)}, u32[]{:S(2)}, u32[]{:S(2)}) collective-permute-start(bf16[64,2048]{1,0:T(8,128)(2,1)S(1)} %get-tuple-element.10), channel_id=1, source_target_pairs={{0,8},{4,12},{8,0},{12,4},{1,9},{5,13},{9,1},{13,5},{2,10},{6,14},... | collective-permute-start | bytes 786440 | tf_op jit(solution)/shard_map/ppermute | solution.py:247
  6.3 1.6 %collective-permute-start.2 = (bf16[64,2048]{1,0:T(8,128)(2,1)S(1)}, bf16[64,2048]{1,0:T(8,128)(2,1)S(1)}, u32[]{:S(2)}, u32[]{:S(2)}) collective-permute-start(bf16[64,2048]{1,0:T(8,128)(2,1)S(1)} %get-tuple-element.9), channel_id=1, source_target_pairs={{0,4},{4,8},{8,12},{12,0},{1,5},{5,9},{9,13},{13,1},{2,6},{6,10},{... | collective-permute-start | bytes 786440 | tf_op jit(solution)/shard_map/ppermute | solution.py:247
  7.8 2.2 %collective-permute-start.4 = (bf16[64,2048]{1,0:T(8,128)(2,1)S(1)}, bf16[64,2048]{1,0:T(8,128)(2,1)S(1)}, u32[]{:S(2)}, u32[]{:S(2)}) collective-permute-start(bf16[64,2048]{1,0:T(8,128)(2,1)S(1)} %get-tuple-element.11), channel_id=1, source_target_pairs={{0,12},{4,0},{8,4},{12,8},{1,13},{5,1},{9,5},{13,9},{2,14},{6,2},{... | collective-permute-start | bytes 786440 | tf_op jit(solution)/shard_map/ppermute | solution.py:247
  10.1 0.0 collective-permute-start.6
  10.1 14.6 %collective-permute-done.refs_0_ = bf16[64,2048]{1,0:T(8,128)(2,1)S(1)} collective-permute-done((bf16[64,2048]{1,0:T(8,128)(2,1)S(1)}, bf16[64,2048]{1,0:T(8,128)(2,1)S(1)}, u32[]{:S(2)}, u32[]{:S(2)}) %collective-permute-start) | collective-permute-done | bytes 262176 | tf_op jit(solution)/shard_map/ppermute | solution.py:247
  24.7 0.0 collective-permute-start.1
  24.7 0.0 collective-permute-done.2.refs_2_
  24.7 0.5 collective-permute-start.3
  25.2 0.2 collective-permute-done.4.refs_4_
  25.4 0.0 collective-permute-start.5
  25.4 0.7 bitcast_convert_fusion
  26.1 0.9 copy.17.refs_3_
  26.9 0.2 reduce-window.9
  27.1 0.6 reduce_sum.48
  28.4 0.1 stack.35.plan
  28.5 0.0 collective-permute-done.6.refs_7_
  28.5 0.0 collective-permute-done.1.refs_1_
  28.5 0.0 collective-permute-done.5.refs_5_
  28.5 0.0 copy-start.1
  28.5 1.6 %copy-done.1 = bf16[1,2048,512]{2,1,0:T(8,128)(2,1)S(1)} copy-done((bf16[1,2048,512]{2,1,0:T(8,128)(2,1)S(1)}, bf16[1,2048,512]{2,1,0:T(8,128)(2,1)}, u32[]{:S(2)}) %copy-start.1) | copy-done | bytes 2097176
  30.1 7.3 %shard_map.96 = f32[2,512,768]{2,1,0:T(8,128)S(1)} custom-call(s32[8]{0:T(128)S(1)} %stack.35.plan, bf16[64,2048]{1,0:T(8,128)(2,1)S(1)} %collective-permute-done.refs_0_, bf16[64,2048]{1,0:T(8,128)(2,1)} %collective-permute-done.1.refs_1_, bf16[64,2048]{1,0:T(8,128)(2,1)S(1)} %collective-permute-done.2.refs_2_, ...), custom_call_target="tpu_custom_call" | custom-call | flops 3221225472 | bytes 11534336 | tf_op jit(solution)/shard_map/pallas_call | solution.py:208
  37.4 0.2 fusion.7
  37.6 7.2 %collective-permute-start.10 = (f16[512,768]{1,0:T(8,128)(2,1)S(1)}, f16[512,768]{1,0:T(8,128)(2,1)S(1)}, u32[]{:S(2)}, u32[]{:S(2)}) collective-permute-start(f16[512,768]{1,0:T(8,128)(2,1)S(1)} %get-tuple-element.7), channel_id=1, source_target_pairs={{0,4},{12,8},{1,5},{13,9},{2,6},{14,10},{3,7},{15,11},{16,20},{28,... | collective-permute-start | bytes 2359304 | tf_op jit(solution)/shard_map/ppermute | solution.py:257
  44.8 0.7 collective-permute-start.7
  45.6 4.4 %collective-permute-start.8 = (f16[512,768]{1,0:T(8,128)(2,1)S(1)}, f16[512,768]{1,0:T(8,128)(2,1)S(1)}, u32[]{:S(2)}, u32[]{:S(2)}) collective-permute-start(f16[512,768]{1,0:T(8,128)(2,1)S(1)} %get-tuple-element.6), channel_id=1, source_target_pairs={{0,8},{12,4},{1,9},{13,5},{2,10},{14,6},{3,11},{15,7},{16,24},{28,... | collective-permute-start | bytes 2359304 | tf_op jit(solution)/shard_map/ppermute | solution.py:260
  50.0 7.3 %shard_map.95 = f32[2,512,768]{2,1,0:T(8,128)S(1)} custom-call(s32[8]{0:T(128)S(1)} %stack.35.plan, bf16[64,2048]{1,0:T(8,128)(2,1)S(1)} %collective-permute-done.refs_0_, bf16[64,2048]{1,0:T(8,128)(2,1)} %collective-permute-done.1.refs_1_, bf16[64,2048]{1,0:T(8,128)(2,1)S(1)} %collective-permute-done.2.refs_2_, ...), custom_call_target="tpu_custom_call" | custom-call | flops 3221225472 | bytes 11534336 | tf_op jit(solution)/shard_map/pallas_call | solution.py:208
  57.3 0.1 fusion.8
  57.4 0.1 collective-permute-start.9
  57.4 5.2 %collective-permute-done.10 = f16[512,768]{1,0:T(8,128)(2,1)S(1)} collective-permute-done((f16[512,768]{1,0:T(8,128)(2,1)S(1)}, f16[512,768]{1,0:T(8,128)(2,1)S(1)}, u32[]{:S(2)}, u32[]{:S(2)}) %collective-permute-start.10) | collective-permute-done | bytes 786464 | tf_op jit(solution)/shard_map/ppermute | solution.py:257
  62.7 0.2 add_convert_fusion
  62.9 1.3 %collective-permute-start.11 = (f16[512,768]{1,0:T(8,128)(2,1)S(1)}, f16[512,768]{1,0:T(8,128)(2,1)S(1)}, u32[]{:S(2)}, u32[]{:S(2)}) collective-permute-start(f16[512,768]{1,0:T(8,128)(2,1)S(1)} %add_convert_fusion), channel_id=1, source_target_pairs={{4,12},{8,0},{5,13},{9,1},{6,14},{10,2},{7,15},{11,3},{20,28},{24,... | collective-permute-start | bytes 2359304 | tf_op jit(solution)/shard_map/ppermute | solution.py:263
  64.2 0.1 fusion.9
  64.3 0.1 select_reduce_fusion
  64.4 15.2 %collective-permute-done.8 = f16[512,768]{1,0:T(8,128)(2,1)S(1)} collective-permute-done((f16[512,768]{1,0:T(8,128)(2,1)S(1)}, f16[512,768]{1,0:T(8,128)(2,1)S(1)}, u32[]{:S(2)}, u32[]{:S(2)}) %collective-permute-start.8) | collective-permute-done | bytes 786464 | tf_op jit(solution)/shard_map/ppermute | solution.py:260
  79.6 15.9 %collective-permute-done.9 = f16[512,768]{1,0:T(8,128)(2,1)S(1)} collective-permute-done((f16[512,768]{1,0:T(8,128)(2,1)S(1)}, f16[512,768]{1,0:T(8,128)(2,1)S(1)}, u32[]{:S(2)}, u32[]{:S(2)}) %collective-permute-start.9) | collective-permute-done | bytes 786464 | tf_op jit(solution)/shard_map/ppermute | solution.py:261
  95.5 3.9 %collective-permute-done.11 = f16[512,768]{1,0:T(8,128)(2,1)S(1)} collective-permute-done((f16[512,768]{1,0:T(8,128)(2,1)S(1)}, f16[512,768]{1,0:T(8,128)(2,1)S(1)}, u32[]{:S(2)}, u32[]{:S(2)}) %collective-permute-start.11) | collective-permute-done | bytes 786464 | tf_op jit(solution)/shard_map/ppermute | solution.py:263
  99.4 0.5 fusion.5.refs_2_
  99.9 3.0 %shard_map.97 = f32[2,512]{1,0:T(2,128)S(1)} custom-call(s32[4]{0:T(128)S(1)} %copy-done.3, s32[1]{0:T(128)} %bitcast.2.refs_1_, bf16[512,768]{1,0:T(8,128)(2,1)S(1)} %fusion.5.refs_2_, f32[512,1]{1,0:T(8,128)S(1)} %copy-done.2), custom_call_target="tpu_custom_call" | custom-call | tf_op jit(solution)/shard_map/pallas_call | solution.py:272
  102.9 0.1 reshape.81
  103.1 0.7 reshape.87
  103.7 5.0 %all-to-all-start = ((f32[16,1,128]{2,1,0:T(1,128)}), f32[16,1,128]{2,1,0:T(1,128)S(1)}, u32[]{:S(2)}, u32[]{:S(2)}) async-start(f32[16,1,128]{2,1,0:T(1,128)} %reshape.87), calls=%async_computation | async-start | bytes 16384 | tf_op jit(solution)/shard_map/all_to_all | solution.py:290
  108.7 0.1 select_reduce_fusion.1
  108.8 6.3 %all-to-all-done = f32[16,1,128]{2,1,0:T(1,128)S(1)} async-done(((f32[16,1,128]{2,1,0:T(1,128)}), f32[16,1,128]{2,1,0:T(1,128)S(1)}, u32[]{:S(2)}, u32[]{:S(2)}) %all-to-all-start) | async-done | bytes 8224 | tf_op jit(solution)/shard_map/all_to_all | solution.py:290
  115.1 0.5 broadcast.47
  115.6 0.7 reduce
  116.3 0.1 reshape.88
  116.4 0.5 multiply_subtract_fusion
  (22 shorter events, 0.1 us)
Async XLA Ops:
  0.6 26.3 %copy-start.3 = (s32[4]{0:T(128)S(1)}, s32[4]{0:T(128)}, u32[]{:S(2)}) copy-start(s32[4]{0:T(128)} %refs_0_.1) | copy-start | bytes 52
  0.6 26.5 %copy-start.4 = (f32[4]{0:T(128)S(1)}, f32[4]{0:T(128)}, u32[]{:S(2)}) copy-start(f32[4]{0:T(128)} %param.15) | copy-start | bytes 52
  0.7 27.9 %copy-start = (bf16[1,2048,512]{2,1,0:T(8,128)(2,1)S(1)}, bf16[1,2048,512]{2,1,0:T(8,128)(2,1)}, u32[]{:S(2)}) copy-start(bf16[1,2048,512]{2,1,0:T(8,128)(2,1)} %refs_9_.3) | copy-start | bytes 6291460
  2.2 22.5 %collective-permute-start = (bf16[64,2048]{1,0:T(8,128)(2,1)S(1)}, bf16[64,2048]{1,0:T(8,128)(2,1)S(1)}, u32[]{:S(2)}, u32[]{:S(2)}) collective-permute-start(bf16[64,2048]{1,0:T(8,128)(2,1)S(1)} %get-tuple-element.10), channel_id=1, source_target_pairs={{0,8},{4,12},{8,0},{12,4},{1,9},{5,13},{9,1},{13,5},{2,10},{6,14},... | collective-permute-start | bytes 786440 | tf_op jit(solution)/shard_map/ppermute | solution.py:247
  6.3 18.4 %collective-permute-start.2 = (bf16[64,2048]{1,0:T(8,128)(2,1)S(1)}, bf16[64,2048]{1,0:T(8,128)(2,1)S(1)}, u32[]{:S(2)}, u32[]{:S(2)}) collective-permute-start(bf16[64,2048]{1,0:T(8,128)(2,1)S(1)} %get-tuple-element.9), channel_id=1, source_target_pairs={{0,4},{4,8},{8,12},{12,0},{1,5},{5,9},{9,13},{13,1},{2,6},{6,10},{... | collective-permute-start | bytes 786440 | tf_op jit(solution)/shard_map/ppermute | solution.py:247
  7.8 17.6 %collective-permute-start.4 = (bf16[64,2048]{1,0:T(8,128)(2,1)S(1)}, bf16[64,2048]{1,0:T(8,128)(2,1)S(1)}, u32[]{:S(2)}, u32[]{:S(2)}) collective-permute-start(bf16[64,2048]{1,0:T(8,128)(2,1)S(1)} %get-tuple-element.11), channel_id=1, source_target_pairs={{0,12},{4,0},{8,4},{12,8},{1,13},{5,1},{9,5},{13,9},{2,14},{6,2},{... | collective-permute-start | bytes 786440 | tf_op jit(solution)/shard_map/ppermute | solution.py:247
  10.1 18.4 %collective-permute-start.6 = (bf16[64,2048]{1,0:T(8,128)(2,1)S(1)}, bf16[64,2048]{1,0:T(8,128)(2,1)S(1)}, u32[]{:S(2)}, u32[]{:S(2)}) collective-permute-start(bf16[64,2048]{1,0:T(8,128)(2,1)S(1)} %get-tuple-element.8.refs_6_), channel_id=1, source_target_pairs={{0,2},{2,0},{1,3},{3,1},{4,6},{6,4},{5,7},{7,5},{8,10},{10,8},{9,1... | collective-permute-start | bytes 786440 | tf_op jit(solution)/shard_map/ppermute | solution.py:20
  24.7 3.8 %collective-permute-start.1 = (bf16[64,2048]{1,0:T(8,128)(2,1)S(1)}, bf16[64,2048]{1,0:T(8,128)(2,1)}, u32[]{:S(2)}, u32[]{:S(2)}) collective-permute-start(bf16[64,2048]{1,0:T(8,128)(2,1)S(1)} %collective-permute-done.refs_0_), channel_id=1, source_target_pairs={{0,2},{2,0},{1,3},{3,1},{4,6},{6,4},{5,7},{7,5},{8,10},{10,8},{9,1... | collective-permute-start | bytes 786440 | tf_op jit(solution)/shard_map/ppermute | solution.py:20
  24.7 3.8 %collective-permute-start.3 = (bf16[64,2048]{1,0:T(8,128)(2,1)S(1)}, bf16[64,2048]{1,0:T(8,128)(2,1)}, u32[]{:S(2)}, u32[]{:S(2)}) collective-permute-start(bf16[64,2048]{1,0:T(8,128)(2,1)S(1)} %collective-permute-done.2.refs_2_), channel_id=1, source_target_pairs={{0,2},{2,0},{1,3},{3,1},{4,6},{6,4},{5,7},{7,5},{8,10},{10,8},{9,1... | collective-permute-start | bytes 786440 | tf_op jit(solution)/shard_map/ppermute | solution.py:20
  25.4 3.1 %collective-permute-start.5 = (bf16[64,2048]{1,0:T(8,128)(2,1)S(1)}, bf16[64,2048]{1,0:T(8,128)(2,1)}, u32[]{:S(2)}, u32[]{:S(2)}) collective-permute-start(bf16[64,2048]{1,0:T(8,128)(2,1)S(1)} %collective-permute-done.4.refs_4_), channel_id=1, source_target_pairs={{0,2},{2,0},{1,3},{3,1},{4,6},{6,4},{5,7},{7,5},{8,10},{10,8},{9,1... | collective-permute-start | bytes 786440 | tf_op jit(solution)/shard_map/ppermute | solution.py:20
  28.5 1.6 %copy-start.1 = (bf16[1,2048,512]{2,1,0:T(8,128)(2,1)S(1)}, bf16[1,2048,512]{2,1,0:T(8,128)(2,1)}, u32[]{:S(2)}) copy-start(bf16[1,2048,512]{2,1,0:T(8,128)(2,1)} %refs_10_.3) | copy-start | bytes 6291460
  37.6 25.1 %collective-permute-start.10 = (f16[512,768]{1,0:T(8,128)(2,1)S(1)}, f16[512,768]{1,0:T(8,128)(2,1)S(1)}, u32[]{:S(2)}, u32[]{:S(2)}) collective-permute-start(f16[512,768]{1,0:T(8,128)(2,1)S(1)} %get-tuple-element.7), channel_id=1, source_target_pairs={{0,4},{12,8},{1,5},{13,9},{2,6},{14,10},{3,7},{15,11},{16,20},{28,... | collective-permute-start | bytes 2359304 | tf_op jit(solution)/shard_map/ppermute | solution.py:257
  44.8 19.6 %collective-permute-start.7 = (f16[512,768]{1,0:T(8,128)(2,1)S(1)}, f16[512,768]{1,0:T(8,128)(2,1)S(1)}, u32[]{:S(2)}, u32[]{:S(2)}) collective-permute-start(f16[512,768]{1,0:T(8,128)(2,1)S(1)} %get-tuple-element.6), channel_id=1, source_target_pairs={{4,8},{8,4},{5,9},{9,5},{6,10},{10,6},{7,11},{11,7},{20,24},{24,20... | collective-permute-start | bytes 2359304 | tf_op jit(solution)/shard_map/ppermute | solution.py:259
  45.6 34.0 %collective-permute-start.8 = (f16[512,768]{1,0:T(8,128)(2,1)S(1)}, f16[512,768]{1,0:T(8,128)(2,1)S(1)}, u32[]{:S(2)}, u32[]{:S(2)}) collective-permute-start(f16[512,768]{1,0:T(8,128)(2,1)S(1)} %get-tuple-element.6), channel_id=1, source_target_pairs={{0,8},{12,4},{1,9},{13,5},{2,10},{14,6},{3,11},{15,7},{16,24},{28,... | collective-permute-start | bytes 2359304 | tf_op jit(solution)/shard_map/ppermute | solution.py:260
  57.4 38.1 %collective-permute-start.9 = (f16[512,768]{1,0:T(8,128)(2,1)S(1)}, f16[512,768]{1,0:T(8,128)(2,1)S(1)}, u32[]{:S(2)}, u32[]{:S(2)}) collective-permute-start(f16[512,768]{1,0:T(8,128)(2,1)S(1)} %fusion.8), channel_id=1, source_target_pairs={{0,4},{4,0},{8,12},{12,8},{1,5},{5,1},{9,13},{13,9},{2,6},{6,2},{1... | collective-permute-start | bytes 2359304 | tf_op jit(solution)/shard_map/ppermute | solution.py:261
  62.9 36.5 %collective-permute-start.11 = (f16[512,768]{1,0:T(8,128)(2,1)S(1)}, f16[512,768]{1,0:T(8,128)(2,1)S(1)}, u32[]{:S(2)}, u32[]{:S(2)}) collective-permute-start(f16[512,768]{1,0:T(8,128)(2,1)S(1)} %add_convert_fusion), channel_id=1, source_target_pairs={{4,12},{8,0},{5,13},{9,1},{6,14},{10,2},{7,15},{11,3},{20,28},{24,... | collective-permute-start | bytes 2359304 | tf_op jit(solution)/shard_map/ppermute | solution.py:263
  64.4 35.5 %copy-start.2 = (f32[512,1]{1,0:T(8,128)S(1)}, f32[512,1]{1,0:T(8,128)}, u32[]{:S(2)}) copy-start(f32[512,1]{1,0:T(8,128)} %copy.17.refs_3_) | copy-start | bytes 6148
  64.4 44.3 %copy-start.5 = (s32[4]{0:T(128)S(1)}, s32[4]{0:T(128)}, u32[]{:S(2)}) copy-start(s32[4]{0:T(128)} %param.14) | copy-start | bytes 52
  103.7 11.3 %all-to-all-start = ((f32[16,1,128]{2,1,0:T(1,128)}), f32[16,1,128]{2,1,0:T(1,128)S(1)}, u32[]{:S(2)}, u32[]{:S(2)}) async-start(f32[16,1,128]{2,1,0:T(1,128)} %reshape.87), calls=%async_computation | async-start | bytes 16384 | tf_op jit(solution)/shard_map/all_to_all | solution.py:290

commit v3 on v0

--- a/solution.py
+++ b/solution.py
@@ -1,6 +1,8 @@
 import jax
 import jax.numpy as jnp
 from jax import lax
+from jax.experimental import pallas as pl
+from jax.experimental.pallas import tpu as pltpu
 from jax.sharding import PartitionSpec as P
 
 QUERY_HEAD_COUNT = 32
@@ -10,6 +12,10 @@
 
 BETA = 0.1
 NEGATIVE = -1e30
+LINK_SCALE = 16.0
+GROUP = QUERY_HEAD_COUNT // KEY_VALUE_HEADS
+GRANT = 12
+PRICE = 1.0
 
 
 def swapped(array, axis, distance):
@@ -31,7 +37,7 @@
     return (begin, answer, advantage)
 
 
-def shards(
+def gathered_shards(
     hidden, w_query, key_projection, value_projection, score_head, lengths, prompt_len, reward
 ):
     row_block = lax.all_gather(hidden, "sec", axis=0, tiled=True)
@@ -53,17 +59,16 @@
     key_rows = key_rows.astype(jnp.bfloat16)
     value_rows = value_rows.astype(jnp.bfloat16)
     heads_here = pair_cols // HEAD_SIZE
-    query_group = QUERY_HEAD_COUNT // KEY_VALUE_HEADS
     score_scale = HEAD_SIZE ** (-0.5)
     row_pos = lax.axis_index("ctx") * token_rows + jnp.arange(token_rows, dtype=jnp.int32)
     begin, answer, advantage = rollout_tables(lengths, prompt_len, reward, row_pos)
     first_begin = jnp.min(begin)
     last_row = row_pos[token_rows - 1]
-    query_heads = query_rows.reshape(token_rows, heads_here, query_group, HEAD_SIZE)
+    query_heads = query_rows.reshape(token_rows, heads_here, GROUP, HEAD_SIZE)
     start_state = (
-        jnp.full((heads_here, query_group, token_rows), NEGATIVE, jnp.float32),
-        jnp.zeros((heads_here, query_group, token_rows), jnp.float32),
-        jnp.zeros((heads_here, query_group, token_rows, HEAD_SIZE), jnp.float32),
+        jnp.full((heads_here, GROUP, token_rows), NEGATIVE, jnp.float32),
+        jnp.zeros((heads_here, GROUP, token_rows), jnp.float32),
+        jnp.zeros((heads_here, GROUP, token_rows, HEAD_SIZE), jnp.float32),
     )
     key_piece = lax.all_gather(key_rows, "ctx", axis=0, tiled=True)
     value_piece = lax.all_gather(value_rows, "ctx", axis=0, tiled=True)
@@ -129,6 +134,272 @@
     return (kl_term, objective)
 
 
+def token_places(index, section, rows):
+    chip = 2 * rows
+    row = lax.rem(index, chip)
+    return index - row + lax.rem(row + section * rows, chip)
+
+
+def attention_kernel(lengths, where, block, head, out, rows):
+    tokens = block.shape[0]
+    section = where[0]
+
+    def place(shape, axis):
+        return token_places(lax.broadcasted_iota(jnp.int32, shape, axis), section, rows)
+
+    query_pos = place((1, tokens), 1)
+    begin = jnp.zeros((1, tokens), jnp.int32)
+    start = jnp.int32(0)
+    for index in range(lengths.shape[0] - 1):
+        start = start + lengths[index]
+        begin = jnp.where(query_pos >= start, start, begin)
+    key_pos = place((tokens, 1), 0)
+    valid = (key_pos <= query_pos) & (key_pos >= begin)
+    wide = GROUP * HEAD_SIZE
+    key = block[:, wide : wide + HEAD_SIZE]
+    value = block[:, wide + HEAD_SIZE :]
+    numerator = jnp.zeros((1, tokens), jnp.float32)
+    squares = jnp.zeros((1, tokens), jnp.float32)
+    for index in range(GROUP):
+        cols = slice(index * HEAD_SIZE, (index + 1) * HEAD_SIZE)
+        logits = lax.dot_general(
+            key, block[:, cols], (((1,), (1,)), ((), ())), preferred_element_type=jnp.float32
+        ) * (HEAD_SIZE ** (-0.5))
+        masked = jnp.where(valid, logits, NEGATIVE)
+        peak = jnp.max(masked, axis=0, keepdims=True)
+        weights = jnp.exp(masked - peak)
+        total = jnp.sum(weights, axis=0, keepdims=True)
+        mixed = lax.dot_general(
+            value,
+            weights.astype(jnp.bfloat16),
+            (((0,), (0,)), ((), ())),
+            preferred_element_type=jnp.float32,
+        )
+        attended = mixed / total
+        column = jnp.broadcast_to(head[:, cols].astype(jnp.float32), (HEAD_SIZE, HEAD_SIZE)).T
+        numerator += jnp.sum(attended * column[:, :1], axis=0, keepdims=True)
+        squares += jnp.sum(attended * attended, axis=0, keepdims=True)
+    for ctx in range(tokens // (2 * rows)):
+        own = slice(2 * ctx * rows, (2 * ctx + 1) * rows)
+        other = slice((2 * ctx + 1) * rows, (2 * ctx + 2) * rows)
+        same, cross = (
+            jnp.concatenate([numerator[:, part], squares[:, part]], axis=1)
+            for part in (own, other)
+        )
+        for core in range(2):
+            row = jnp.where(section == core, same, cross)
+            for share in range(2):
+                out[ctx * 4 + core * 2 + share] = row
+
+
+def final_kernel(lengths, prompt_len, reward, where, parts, kl_term, objective):
+    rows = kl_term.shape[1]
+    shares = parts.shape[0]
+    scores = []
+    for core in range(2):
+        picked = [parts[i] for i in range(shares) if i // 2 % 2 == core]
+        while len(picked) > 1:
+            picked = [one + two for one, two in zip(picked[::2], picked[1::2])]
+        mean_square = picked[0][:, rows:] / (QUERY_HEAD_COUNT * HEAD_SIZE)
+        scores.append(picked[0][:, :rows] / jnp.sqrt(mean_square + 1e-05))
+    position = (where[1] * 2 + where[0]) * rows + lax.broadcasted_iota(jnp.int32, (1, rows), 1)
+    rolls = lengths.shape[0]
+    mean = reward[0]
+    for index in range(1, rolls):
+        mean = mean + reward[index]
+    mean = mean / rolls
+    begin = jnp.zeros((1, rows), jnp.int32)
+    prompt = jnp.zeros((1, rows), jnp.int32) + prompt_len[0]
+    advantage = jnp.zeros((1, rows), jnp.float32) + (reward[0] - mean)
+    start = jnp.int32(0)
+    for index in range(1, rolls):
+        start = start + lengths[index - 1]
+        inside = position >= start
+        begin = jnp.where(inside, start, begin)
+        prompt = jnp.where(inside, prompt_len[index], prompt)
+        advantage = jnp.where(inside, reward[index] - mean, advantage)
+    answer = jnp.where(position - begin >= prompt, 1.0, 0.0)
+    gap = scores[1] - scores[0]
+    term = answer * (jnp.exp(gap) - gap - 1.0)
+    kl_term[...] = term
+    objective[...] = answer * advantage - BETA * term
+
+
+def products(held, weights, low, front, store):
+    wide = GROUP * HEAD_SIZE
+    query_w, key_w, value_w = weights
+    for turn in range(2):
+        first = pl.multiple_of((low + (front ^ turn)) * wide, HEAD_SIZE)
+        total = jnp.dot(
+            held, query_w[0, :, pl.ds(first, wide)], preferred_element_type=jnp.float32
+        )
+        store(turn, 0, total * LINK_SCALE)
+    for index, weight in enumerate((key_w, value_w)):
+        first = pl.multiple_of(low * HEAD_SIZE, HEAD_SIZE)
+        total = jnp.dot(
+            held, weight[0, :, pl.ds(first, 2 * HEAD_SIZE)], preferred_element_type=jnp.float32
+        )
+        total = total * LINK_SCALE
+        lower, upper = total[:, :HEAD_SIZE], total[:, HEAD_SIZE:]
+        for turn, (one, two) in enumerate(((lower, upper), (upper, lower))):
+            store(turn, wide + index * HEAD_SIZE, jnp.where(front == 0, one, two))
+
+
+def own_kernel(plan, own, other, query_w, key_w, value_w, out, sources):
+    held = jnp.concatenate([own[...], other[...]], axis=0)
+    for pair in range(2):
+
+        def store(turn, start, total):
+            out[2 * pair + turn, :, start : start + total.shape[1]] = total
+
+        low, front = plan[sources + 2 * pair], plan[sources + 2 * pair + 1]
+        products(held, (query_w, key_w, value_w), low, front, store)
+
+
+def rest_kernel(plan, *refs, pair):
+    pieces = refs[:-7]
+    own, query_w, key_w, value_w, *outs, tokens = refs[-7:]
+    rows = pieces[0].shape[0]
+    chip = 2 * rows
+    sources = len(pieces) // 2
+
+    def place(slot):
+        return pl.ds(pl.multiple_of(plan[slot] * chip, chip), chip)
+
+    for index, piece in enumerate(pieces):
+        tokens[index * rows : (index + 1) * rows, :] = piece[...]
+    for turn in range(2):
+        outs[turn][place(sources), :] = own[2 * pair + turn]
+
+    def store(turn, start, total):
+        for slot in range(sources):
+            part = total[slot * chip : (slot + 1) * chip, :]
+            outs[turn][place(slot), start : start + total.shape[1]] = part
+
+    low, front = plan[sources + 1 + 2 * pair], plan[sources + 2 + 2 * pair]
+    products(tokens[...], (query_w, key_w, value_w), low, front, store)
+
+
+def partial_call(kernel, shapes, operands, scratch, tokens, owners):
+    vmem = pl.BlockSpec(memory_space=pltpu.VMEM)
+    smem = pl.BlockSpec(memory_space=pltpu.SMEM)
+    depth = operands[1].shape[1]
+    cols = (GROUP + 2) * HEAD_SIZE
+    return pl.pallas_call(
+        kernel,
+        out_shape=[jax.ShapeDtypeStruct(shape, jnp.float32) for shape in shapes],
+        in_specs=[vmem if operand.ndim > 1 else smem for operand in operands],
+        out_specs=[vmem for _ in shapes],
+        scratch_shapes=scratch,
+        compiler_params=pltpu.CompilerParams(vmem_limit_bytes=GRANT * 1024 * 1024),
+        cost_estimate=pl.CostEstimate(
+            flops=int(PRICE * 2 * owners * tokens * depth * cols),
+            bytes_accessed=int(PRICE * 2 * (tokens * depth + owners * cols * (depth + 2 * tokens))),
+            transcendentals=0,
+        ),
+    )(*operands)
+
+
+def split_shards(
+    hidden, w_query, key_projection, value_projection, score_head, lengths, prompt_len, reward
+):
+    rows = hidden.shape[0]
+    depth = w_query.shape[1]
+    ctx = lax.axis_index("ctx")
+    section = lax.axis_index("sec")
+    count = 4
+    f16, f32 = jnp.float16, jnp.float32
+
+    def columns(target):
+        return lax.dynamic_slice_in_dim(hidden, (target % count) * depth, depth, 1)
+
+    steps = (2, 1, 3)
+    pieces = []
+    for step in steps:
+        pairs = [(i, (i + step) % count) for i in range(count)]
+        pieces.append(lax.ppermute(columns(ctx + step), "ctx", pairs))
+    mine = columns(ctx)
+    weights = (w_query, key_projection, value_projection)
+    cols = (GROUP + 2) * HEAD_SIZE
+    chip = 2 * rows
+    left = ctx < 2
+    low = jnp.where(left, 2, 0)
+    plan = jnp.stack(
+        [*((ctx - step) % count for step in steps), ctx]
+        + [low, jnp.where(left, 1, 0), 2 - low, 1 - ctx % 2]
+    ).astype(jnp.int32)
+    (own,) = partial_call(
+        lambda *refs: own_kernel(*refs, sources=count),
+        [(count, chip, cols)],
+        (plan, mine, swapped(mine, "sec", 0), *weights),
+        [],
+        chip,
+        count,
+    )
+
+    *pieces, own = lax.optimization_barrier((*pieces, own))
+    pieces = [part for piece in pieces for part in (piece, swapped(piece, "sec", 0))]
+
+    def rest(pair):
+        return partial_call(
+            lambda *refs: rest_kernel(*refs, pair=pair),
+            [(count * chip, cols)] * 2,
+            (plan, *pieces, own, *weights),
+            [pltpu.VMEM((len(pieces) * rows, depth), jnp.bfloat16)],
+            len(pieces) * rows,
+            2,
+        )
+
+    first = rest(0)
+    second = rest(1)
+
+    def reduced(first, second):
+        far = first[0].astype(f16)
+        fold = lax.ppermute(far, "ctx", [(0, 1), (3, 2)])
+        inner = first[1].astype(f16)
+        middle = lax.ppermute(inner, "ctx", [(1, 2), (2, 1)])
+        skip = lax.ppermute(inner, "ctx", [(0, 2), (3, 1)])
+        folded = (far.astype(f32) + fold.astype(f32)).astype(f16)
+        ends = lax.ppermute(folded, "ctx", [(1, 3), (2, 0)])
+        beside, _ = lax.optimization_barrier((second[0].astype(f16), folded))
+        near = lax.ppermute(beside, "ctx", [(0, 1), (1, 0), (2, 3), (3, 2)])
+        total = second[1].astype(f16).astype(f32)
+        for part in (middle, skip, near, ends):
+            total = total + part.astype(f32)
+        return (total * (1.0 / LINK_SCALE)).astype(jnp.bfloat16)
+
+    mine = reduced(first, second)
+    wide = GROUP * HEAD_SIZE
+    smem = pl.BlockSpec(memory_space=pltpu.SMEM)
+    where = jnp.stack([section, ctx]).astype(jnp.int32)
+    sums = pl.pallas_call(
+        lambda plan, *refs: attention_kernel(*refs, rows),
+        out_shape=jax.ShapeDtypeStruct((4 * count, 1, 2 * rows), f32),
+        grid_spec=pltpu.PrefetchScalarGridSpec(
+            num_scalar_prefetch=1,
+            grid=(1,),
+            in_specs=[
+                smem,
+                smem,
+                pl.BlockSpec(mine.shape, lambda i, plan: (0, 0)),
+                pl.BlockSpec((1, wide), lambda i, plan: (0, plan[1])),
+            ],
+            out_specs=pl.BlockSpec((4 * count, 1, 2 * rows), lambda i, plan: (0, 0, 0)),
+        ),
+        compiler_params=pltpu.CompilerParams(vmem_limit_bytes=12 * 1024 * 1024),
+    )(where, lengths, where, mine, score_head)
+
+    spread = lax.all_to_all(sums, ("ctx", "sec", "tp"), 0, 0, tiled=True)
+    vmem = pl.BlockSpec(memory_space=pltpu.VMEM)
+    kl_term, objective = pl.pallas_call(
+        final_kernel,
+        out_shape=[jax.ShapeDtypeStruct((1, rows), f32)] * 2,
+        in_specs=[smem, smem, smem, smem, vmem],
+        out_specs=[vmem, vmem],
+    )(lengths, prompt_len, reward, where, spread)
+    return (kl_term.reshape(rows), objective.reshape(rows))
+
+
 def solution(mesh):
     placed = (
         P(("grp", "ctx", "sec"), None),
@@ -140,8 +411,10 @@
         P("grp"),
         P("grp"),
     )
+    own_heads = KEY_VALUE_HEADS // mesh.shape["tp"]
+    by_heads = mesh.shape["ctx"] == 4 and own_heads == 4
     return jax.shard_map(
-        shards,
+        split_shards if by_heads else gathered_shards,
         mesh=mesh,
         in_specs=placed,
         out_specs=(P(("grp", "ctx", "sec")), P(("grp", "ctx", "sec"))),

time: 929 us -> 115 us (0.12)
  waiting for transfers between devices: 828 us -> 52.1 us
  blocking collectives: 47.2 us -> 11.2 us
  matrix products: 25.2 us -> 0 us
  starting transfers between devices: 0.15 us -> 24.9 us
  between operations: 14.6 us -> 0.84 us
  Pallas kernels: 0 us -> 13.7 us
    all_gather x4 -> x0, waiting for transfers between devices: 824 us -> none  [the longest x1 539 us: shards(): query_rows = add_rows(lax.all_gather(query_w, 'ctx', axis=0, tiled=True))]
    ppermute x0 -> x8, waiting for transfers between devices: none -> 50.4 us  [the longest x1 15.9 us: reduced(): near = lax.ppermute(beside, 'ctx', [(0, 1), (1, 0), (2, 3), (3, 2)])]
    all_gather x2 -> x0, blocking collectives: 42.2 us -> none  [the longest x1 25.3 us: shards(): value_piece = lax.all_gather(value_rows, 'ctx', axis=0, tiled=True)]
    dot_general x6 -> x0, matrix products: 25.2 us -> none  [the longest x3 23.7 us: add_rows(): return jnp.dot(row_block, piece, preferred_element_type=jnp.float32)]
    ppermute x0 -> x8, starting transfers between devices: none -> 23.9 us  [the longest x3 7.41 us: split_shards(): pieces.append(lax.ppermute(columns(ctx + step), 'ctx', pairs))]
    pallas_call x0 -> x5, Pallas kernels: none -> 13.7 us  [the longest x3 8.73 us: partial_call(): pl.pallas_call(kernel, out_shape=[jax.ShapeDtypeStruct(shape, jnp.float32...]
    all_to_all x0 -> x1, blocking collectives: none -> 11.2 us  [split_shards(): spread = lax.all_to_all(sums, ('ctx', 'sec', 'tp'), 0, 0, tiled=True)]
  transfers between devices with their start and end apart: 5 -> 12, of which waited for: 5 -> 9; matrix products, arithmetic and copies ran while one was open for 1% -> 1% of each run, Pallas kernels for 0% -> 5%
where the time goes in v3:
time: 115 us; the launch traced here: 114 us
  waiting for transfers between devices  52.1 us (45%)
  starting transfers between devices  24.9 us (22%)
  Pallas kernels  13.7 us (12%)
  blocking collectives  11.2 us (10%)
  local copies, waits for them, and re-layouts  7.31 us (6%)
  other arithmetic  4.06 us (4%)
    ppermute x1, waiting for transfers between devices, reduced(): near = lax.ppermute(beside, 'ctx', [(0, 1), (1, 0), (2, 3), (3, 2)])  15.9 us
    ppermute x1, waiting for transfers between devices, reduced(): skip = lax.ppermute(inner, 'ctx', [(0, 2), (3, 1)])  12.9 us
    all_to_all x1, blocking collectives, split_shards(): spread = lax.all_to_all(sums, ('ctx', 'sec', 'tp'), 0, 0, tiled=True)  11.2 us
    ppermute x3, waiting for transfers between devices, split_shards(): pieces.append(lax.ppermute(columns(ctx + step), 'ctx', pairs))  8.74 us
    pallas_call x3, Pallas kernels, partial_call(): pl.pallas_call(kernel, out_shape=[jax.ShapeDtypeStruct(shape, jnp.float32...  8.73 us
    ppermute x1, waiting for transfers between devices, reduced(): fold = lax.ppermute(far, 'ctx', [(0, 1), (3, 2)])  7.71 us
    ppermute x3, starting transfers between devices, split_shards(): pieces.append(lax.ppermute(columns(ctx + step), 'ctx', pairs))  7.41 us
    ppermute x1, starting transfers between devices, reduced(): fold = lax.ppermute(far, 'ctx', [(0, 1), (3, 2)])  6.81 us
  transfers between devices with their start and end apart: 12, of which 9 were waited for; matrix products, arithmetic and copies ran while one was open for 1% of the time, Pallas kernels for 5%

profile of v3, /device:TPU:0, one launch (start us, length us, event | category | flops | bytes accessed | tf_op | source)
XLA Modules:
  0.0 114.2 jit_solution(1027971381439487712)
XLA Ops:
  0.6 0.0 copy-start.2
  0.7 2.2 %constant_dynamic-slice_fusion = (bf16[64,2048]{1,0:T(8,128)(2,1)S(1)}, bf16[64,2048]{1,0:T(8,128)(2,1)}, bf16[64,2048]{1,0:T(8,128)(2,1)}, bf16[64,2048]{1,0:T(8,128)(2,1)}) fusion(bf16[64,8192]{1,0:T(8,128)(2,1)} %param.8, s32[]{:T(128)S(6)} %select_n.67, s32[]{:T(128)S(6)} %select_n.63, s32[]{:T(128)S(6)} %select_n.61, s32[]{:T(128)S(6)} %select_n.65), kind=kLoop, calls=%fused_computation.2 | loop fusion | bytes 2097168 | tf_op jit(solution)/shard_map/dynamic_slice | solution.py:314
  2.9 0.5 collective-permute-start.3
  3.4 3.6 %collective-permute-start = (bf16[64,2048]{1,0:T(8,128)(2,1)}, bf16[64,2048]{1,0:T(8,128)(2,1)S(1)}, u32[]{:S(2)}, u32[]{:S(2)}) collective-permute-start(bf16[64,2048]{1,0:T(8,128)(2,1)} %get-tuple-element.26), channel_id=1, source_target_pairs={{0,8},{4,12},{8,0},{12,4},{1,9},{5,13},{9,1},{13,5},{2,10},{6,14},... | collective-permute-start | bytes 786440 | tf_op jit(solution)/shard_map/ppermute | solution.py:320
  7.0 1.6 %collective-permute-start.1 = (bf16[64,2048]{1,0:T(8,128)(2,1)}, bf16[64,2048]{1,0:T(8,128)(2,1)S(1)}, u32[]{:S(2)}, u32[]{:S(2)}) collective-permute-start(bf16[64,2048]{1,0:T(8,128)(2,1)} %get-tuple-element.25), channel_id=1, source_target_pairs={{0,4},{4,8},{8,12},{12,0},{1,5},{5,9},{9,13},{13,1},{2,6},{6,10},{... | collective-permute-start | bytes 786440 | tf_op jit(solution)/shard_map/ppermute | solution.py:320
  8.5 2.2 %collective-permute-start.2 = (bf16[64,2048]{1,0:T(8,128)(2,1)}, bf16[64,2048]{1,0:T(8,128)(2,1)S(1)}, u32[]{:S(2)}, u32[]{:S(2)}) collective-permute-start(bf16[64,2048]{1,0:T(8,128)(2,1)} %get-tuple-element.27), channel_id=1, source_target_pairs={{0,12},{4,0},{8,4},{12,8},{1,13},{5,1},{9,5},{13,9},{2,14},{6,2},{... | collective-permute-start | bytes 786440 | tf_op jit(solution)/shard_map/ppermute | solution.py:320
  10.8 0.1 stack.44.refs_0_
  10.9 0.0 collective-permute-done.3.refs_2_
  10.9 0.0 copy-done.2
  10.9 0.0 copy-start
  10.9 3.4 %copy-done = bf16[1,2048,2048]{2,1,0:T(8,128)(2,1)S(1)} copy-done((bf16[1,2048,2048]{2,1,0:T(8,128)(2,1)S(1)}, bf16[1,2048,2048]{2,1,0:T(8,128)(2,1)}, u32[]{:S(2)}) %copy-start) | copy-done | bytes 8388632
  14.3 1.6 %copy-done.3 = bf16[1,2048,512]{2,1,0:T(8,128)(2,1)S(1)} copy-done((bf16[1,2048,512]{2,1,0:T(8,128)(2,1)S(1)}, bf16[1,2048,512]{2,1,0:T(8,128)(2,1)}, u32[]{:S(2)}) %copy-start.3) | copy-done | bytes 2097176
  15.9 2.4 %shard_map.95.refs_7_ = f32[4,128,768]{2,1,0:T(8,128)S(1)} custom-call(s32[8]{0:T(128)S(1)} %stack.44.refs_0_, bf16[64,2048]{1,0:T(8,128)(2,1)S(1)} %get-tuple-element.24.refs_1_, bf16[64,2048]{1,0:T(8,128)(2,1)S(1)} %collective-permute-done.3.refs_2_, bf16[1,2048,2048]{2,1,0:T(8,128)(2,1)S(1)} %copy-done, bf16[1,2048,512]{2,1,0:T(8,128)(2,1)S(1)} %copy-done.2, ...), custom_call_target="tpu_custom_call" | custom-call | flops 1610612736 | bytes 14680064 | tf_op jit(solution)/shard_map/pallas_call | solution.py:288
  18.2 7.4 %collective-permute-done.refs_1_ = bf16[64,2048]{1,0:T(8,128)(2,1)S(1)} collective-permute-done((bf16[64,2048]{1,0:T(8,128)(2,1)}, bf16[64,2048]{1,0:T(8,128)(2,1)S(1)}, u32[]{:S(2)}, u32[]{:S(2)}) %collective-permute-start) | collective-permute-done | bytes 262176 | tf_op jit(solution)/shard_map/ppermute | solution.py:320
  25.6 0.0 collective-permute-done.1.refs_3_
  25.6 1.4 %collective-permute-done.2.refs_5_ = bf16[64,2048]{1,0:T(8,128)(2,1)S(1)} collective-permute-done((bf16[64,2048]{1,0:T(8,128)(2,1)}, bf16[64,2048]{1,0:T(8,128)(2,1)S(1)}, u32[]{:S(2)}, u32[]{:S(2)}) %collective-permute-start.2) | collective-permute-done | bytes 262176 | tf_op jit(solution)/shard_map/ppermute | solution.py:320
  27.0 0.0 collective-permute-start.4
  27.0 0.5 collective-permute-start.5
  27.5 0.0 collective-permute-start.6
  27.5 1.0 collective-permute-done.4.refs_2_
  28.5 0.4 collective-permute-done.5.refs_4_
  28.9 0.4 collective-permute-done.6.refs_6_
  29.3 0.0 copy-done.1
  29.3 3.2 %shard_map.97 = (f32[512,768]{1,0:T(8,128)S(1)}, f32[512,768]{1,0:T(8,128)S(1)}) custom-call(s32[8]{0:T(128)S(1)} %stack.44.refs_0_, bf16[64,2048]{1,0:T(8,128)(2,1)S(1)} %collective-permute-done.refs_1_, bf16[64,2048]{1,0:T(8,128)(2,1)S(1)} %collective-permute-done.4.refs_2_, bf16[64,2048]{1,0:T(8,128)(2,1)S(1)} %collective-permute-done.1.refs_3_, ...), custom_call_target="tpu_custom_call" | custom-call | flops 2415919104 | bytes 10223616 | tf_op jit(solution)/shard_map/pallas_call | solution.py:288
  32.5 0.1 convert_element_type.45
  32.6 6.8 %collective-permute-start.9 = (f16[512,768]{1,0:T(8,128)(2,1)S(1)}, f16[512,768]{1,0:T(8,128)(2,1)S(1)}, u32[]{:S(2)}, u32[]{:S(2)}) collective-permute-start(f16[512,768]{1,0:T(8,128)(2,1)S(1)} %convert_element_type.45), channel_id=1, source_target_pairs={{0,4},{12,8},{1,5},{13,9},{2,6},{14,10},{3,7},{15,11},{16,20},{28,... | collective-permute-start | bytes 2359304 | tf_op jit(solution)/shard_map/ppermute | solution.py:358
  39.4 1.0 convert_element_type.41
  40.4 1.6 %collective-permute-start.7 = (f16[512,768]{1,0:T(8,128)(2,1)}, f16[512,768]{1,0:T(8,128)(2,1)}, u32[]{:S(2)}, u32[]{:S(2)}) collective-permute-start(f16[512,768]{1,0:T(8,128)(2,1)} %convert_element_type.41), channel_id=1, source_target_pairs={{4,8},{8,4},{5,9},{9,5},{6,10},{10,6},{7,11},{11,7},{20,24},{24,20... | collective-permute-start | bytes 2359304 | tf_op jit(solution)/shard_map/ppermute | solution.py:360
  41.9 4.3 %collective-permute-start.8 = (f16[512,768]{1,0:T(8,128)(2,1)}, f16[512,768]{1,0:T(8,128)(2,1)}, u32[]{:S(2)}, u32[]{:S(2)}) collective-permute-start(f16[512,768]{1,0:T(8,128)(2,1)} %convert_element_type.41), channel_id=1, source_target_pairs={{0,8},{12,4},{1,9},{13,5},{2,10},{14,6},{3,11},{15,7},{16,24},{28,... | collective-permute-start | bytes 2359304 | tf_op jit(solution)/shard_map/ppermute | solution.py:361
  46.2 3.2 %shard_map.96 = (f32[512,768]{1,0:T(8,128)S(1)}, f32[512,768]{1,0:T(8,128)S(1)}) custom-call(s32[8]{0:T(128)S(1)} %stack.44.refs_0_, bf16[64,2048]{1,0:T(8,128)(2,1)S(1)} %collective-permute-done.refs_1_, bf16[64,2048]{1,0:T(8,128)(2,1)S(1)} %collective-permute-done.4.refs_2_, bf16[64,2048]{1,0:T(8,128)(2,1)S(1)} %collective-permute-done.1.refs_3_, ...), custom_call_target="tpu_custom_call" | custom-call | flops 2415919104 | bytes 10223616 | tf_op jit(solution)/shard_map/pallas_call | solution.py:288
  49.4 0.0 copy-start.4
  49.4 0.1 convert_element_type.44
  49.5 7.7 %collective-permute-done.9 = f16[512,768]{1,0:T(8,128)(2,1)S(1)} collective-permute-done((f16[512,768]{1,0:T(8,128)(2,1)S(1)}, f16[512,768]{1,0:T(8,128)(2,1)S(1)}, u32[]{:S(2)}, u32[]{:S(2)}) %collective-permute-start.9) | collective-permute-done | bytes 786464 | tf_op jit(solution)/shard_map/ppermute | solution.py:358
  57.2 0.2 add_convert_fusion
  57.4 0.0 copy-done.4
  57.4 2.5 %collective-permute-start.10 = (f16[512,768]{1,0:T(8,128)(2,1)S(1)}, f16[512,768]{1,0:T(8,128)(2,1)S(1)}, u32[]{:S(2)}, u32[]{:S(2)}) collective-permute-start(f16[512,768]{1,0:T(8,128)(2,1)S(1)} %convert_element_type.44), channel_id=1, source_target_pairs={{0,4},{4,0},{8,12},{12,8},{1,5},{5,1},{9,13},{13,9},{2,6},{6,2},{1... | collective-permute-start | bytes 2359304 | tf_op jit(solution)/shard_map/ppermute | solution.py:365
  60.0 1.3 %collective-permute-start.11 = (f16[512,768]{1,0:T(8,128)(2,1)S(1)}, f16[512,768]{1,0:T(8,128)(2,1)}, u32[]{:S(2)}, u32[]{:S(2)}) collective-permute-start(f16[512,768]{1,0:T(8,128)(2,1)S(1)} %add_convert_fusion), channel_id=1, source_target_pairs={{4,12},{8,0},{5,13},{9,1},{6,14},{10,2},{7,15},{11,3},{20,28},{24,... | collective-permute-start | bytes 2359304 | tf_op jit(solution)/shard_map/ppermute | solution.py:363
  61.3 0.1 pad_add_fusion.plan.refs_1_.where
  61.4 0.0 collective-permute-done.7
  61.4 12.9 %collective-permute-done.8 = f16[512,768]{1,0:T(8,128)(2,1)} collective-permute-done((f16[512,768]{1,0:T(8,128)(2,1)}, f16[512,768]{1,0:T(8,128)(2,1)}, u32[]{:S(2)}, u32[]{:S(2)}) %collective-permute-start.8) | collective-permute-done | bytes 786464 | tf_op jit(solution)/shard_map/ppermute | solution.py:361
  74.2 15.9 %collective-permute-done.10 = f16[512,768]{1,0:T(8,128)(2,1)S(1)} collective-permute-done((f16[512,768]{1,0:T(8,128)(2,1)S(1)}, f16[512,768]{1,0:T(8,128)(2,1)S(1)}, u32[]{:S(2)}, u32[]{:S(2)}) %collective-permute-start.10) | collective-permute-done | bytes 786464 | tf_op jit(solution)/shard_map/ppermute | solution.py:365
  90.2 5.1 %collective-permute-done.11 = f16[512,768]{1,0:T(8,128)(2,1)} collective-permute-done((f16[512,768]{1,0:T(8,128)(2,1)S(1)}, f16[512,768]{1,0:T(8,128)(2,1)}, u32[]{:S(2)}, u32[]{:S(2)}) %collective-permute-start.11) | collective-permute-done | bytes 786464 | tf_op jit(solution)/shard_map/ppermute | solution.py:363
  95.3 2.6 %multiply_convert_fusion.refs_2_ = bf16[512,768]{1,0:T(8,128)(2,1)S(1)} fusion(f16[512,768]{1,0:T(8,128)(2,1)} %collective-permute-done.11, f16[512,768]{1,0:T(8,128)(2,1)S(1)} %collective-permute-done.10, f16[512,768]{1,0:T(8,128)(2,1)} %collective-permute-done.8, f16[512,768]{1,0:T(8,128)(2,1)} %collective-permute-done.7, f32[512,768]{1,0:T(8,128)} %copy-done.4), kind=kLoop, calls=%fused_computation | loop fusion | flops 4718592 | bytes 5505024 | tf_op jit(solution)/shard_map/convert_element_type | solution.py:369
  97.9 0.0 copy-done.6
  97.9 0.0 copy-done.5
  97.9 3.7 %shard_map.98 = f32[16,1,128]{2,1,0:T(1,128)S(1)} custom-call(s32[2]{0:T(128)S(1)} %pad_add_fusion.plan.refs_1_.where, s32[4]{0:T(128)S(1)} %copy-done.7, s32[2]{0:T(128)S(1)} %pad_add_fusion.plan.refs_1_.where, bf16[512,768]{1,0:T(8,128)(2,1)S(1)} %multiply_convert_fusion.refs_2_, bf16[1,2048]{1,0:T(2,128)(2,1)S(1)} %copy-done.5), custom_call_target="tpu_custom_call" | custom-call | tf_op jit(solution)/shard_map/pallas_call | solution.py:375
  101.6 11.2 %all_to_all.5.parts = f32[16,1,128]{2,1,0:T(1,128)} all-to-all(f32[16,1,128]{2,1,0:T(1,128)S(1)} %shard_map.98), channel_id=1, replica_groups=mesh['grp'=2,'ctx'=4,'sec'=2,'tp'=2] {'ctx','sec','tp'}, dimensions={0} | all-to-all | bytes 16384 | tf_op jit(solution)/shard_map/all_to_all | solution.py:392
  112.9 1.3 %shard_map.99 = (f32[1,64]{1,0:T(1,128)}, f32[1,64]{1,0:T(1,128)}) custom-call(s32[4]{0:T(128)} %lengths.1, s32[4]{0:T(128)} %prompt_len.1, f32[4]{0:T(128)} %reward.1, s32[2]{0:T(128)} %copy-done.6, f32[16,1,128]{2,1,0:T(1,128)} %all_to_all.5.parts), custom_call_target="tpu_custom_call" | custom-call | tf_op jit(solution)/shard_map/pallas_call | solution.py:394
  (6 shorter events, 0.0 us)
Async XLA Ops:
  0.6 10.3 %copy-start.2 = (bf16[1,2048,512]{2,1,0:T(8,128)(2,1)S(1)}, bf16[1,2048,512]{2,1,0:T(8,128)(2,1)}, u32[]{:S(2)}) copy-start(bf16[1,2048,512]{2,1,0:T(8,128)(2,1)} %refs_9_.3) | copy-start | bytes 6291460
  2.9 8.0 %collective-permute-start.3 = (bf16[64,2048]{1,0:T(8,128)(2,1)S(1)}, bf16[64,2048]{1,0:T(8,128)(2,1)S(1)}, u32[]{:S(2)}, u32[]{:S(2)}) collective-permute-start(bf16[64,2048]{1,0:T(8,128)(2,1)S(1)} %get-tuple-element.24.refs_1_), channel_id=1, source_target_pairs={{0,2},{2,0},{1,3},{3,1},{4,6},{6,4},{5,7},{7,5},{8,10},{10,8},{9,1... | collective-permute-start | bytes 786440 | tf_op jit(solution)/shard_map/ppermute | solution.py:22
  3.4 22.2 %collective-permute-start = (bf16[64,2048]{1,0:T(8,128)(2,1)}, bf16[64,2048]{1,0:T(8,128)(2,1)S(1)}, u32[]{:S(2)}, u32[]{:S(2)}) collective-permute-start(bf16[64,2048]{1,0:T(8,128)(2,1)} %get-tuple-element.26), channel_id=1, source_target_pairs={{0,8},{4,12},{8,0},{12,4},{1,9},{5,13},{9,1},{13,5},{2,10},{6,14},... | collective-permute-start | bytes 786440 | tf_op jit(solution)/shard_map/ppermute | solution.py:320
  7.0 18.6 %collective-permute-start.1 = (bf16[64,2048]{1,0:T(8,128)(2,1)}, bf16[64,2048]{1,0:T(8,128)(2,1)S(1)}, u32[]{:S(2)}, u32[]{:S(2)}) collective-permute-start(bf16[64,2048]{1,0:T(8,128)(2,1)} %get-tuple-element.25), channel_id=1, source_target_pairs={{0,4},{4,8},{8,12},{12,0},{1,5},{5,9},{9,13},{13,1},{2,6},{6,10},{... | collective-permute-start | bytes 786440 | tf_op jit(solution)/shard_map/ppermute | solution.py:320
  8.5 18.4 %collective-permute-start.2 = (bf16[64,2048]{1,0:T(8,128)(2,1)}, bf16[64,2048]{1,0:T(8,128)(2,1)S(1)}, u32[]{:S(2)}, u32[]{:S(2)}) collective-permute-start(bf16[64,2048]{1,0:T(8,128)(2,1)} %get-tuple-element.27), channel_id=1, source_target_pairs={{0,12},{4,0},{8,4},{12,8},{1,13},{5,1},{9,5},{13,9},{2,14},{6,2},{... | collective-permute-start | bytes 786440 | tf_op jit(solution)/shard_map/ppermute | solution.py:320
  10.9 3.4 %copy-start = (bf16[1,2048,2048]{2,1,0:T(8,128)(2,1)S(1)}, bf16[1,2048,2048]{2,1,0:T(8,128)(2,1)}, u32[]{:S(2)}) copy-start(bf16[1,2048,2048]{2,1,0:T(8,128)(2,1)} %refs_8_.3) | copy-start | bytes 25165828
  14.3 1.6 %copy-start.3 = (bf16[1,2048,512]{2,1,0:T(8,128)(2,1)S(1)}, bf16[1,2048,512]{2,1,0:T(8,128)(2,1)}, u32[]{:S(2)}) copy-start(bf16[1,2048,512]{2,1,0:T(8,128)(2,1)} %refs_10_.3) | copy-start | bytes 6291460
  15.9 13.4 %copy-start.1 = (bf16[1,2048,2048]{2,1,0:T(8,128)(2,1)S(1)}, bf16[1,2048,2048]{2,1,0:T(8,128)(2,1)}, u32[]{:S(2)}) copy-start(bf16[1,2048,2048]{2,1,0:T(8,128)(2,1)} %refs_8_.3) | copy-start | bytes 25165828
  27.0 1.5 %collective-permute-start.4 = (bf16[64,2048]{1,0:T(8,128)(2,1)S(1)}, bf16[64,2048]{1,0:T(8,128)(2,1)S(1)}, u32[]{:S(2)}, u32[]{:S(2)}) collective-permute-start(bf16[64,2048]{1,0:T(8,128)(2,1)S(1)} %collective-permute-done.refs_1_), channel_id=1, source_target_pairs={{0,2},{2,0},{1,3},{3,1},{4,6},{6,4},{5,7},{7,5},{8,10},{10,8},{9,1... | collective-permute-start | bytes 786440 | tf_op jit(solution)/shard_map/ppermute | solution.py:22
  27.0 1.9 %collective-permute-start.5 = (bf16[64,2048]{1,0:T(8,128)(2,1)S(1)}, bf16[64,2048]{1,0:T(8,128)(2,1)S(1)}, u32[]{:S(2)}, u32[]{:S(2)}) collective-permute-start(bf16[64,2048]{1,0:T(8,128)(2,1)S(1)} %collective-permute-done.1.refs_3_), channel_id=1, source_target_pairs={{0,2},{2,0},{1,3},{3,1},{4,6},{6,4},{5,7},{7,5},{8,10},{10,8},{9,1... | collective-permute-start | bytes 786440 | tf_op jit(solution)/shard_map/ppermute | solution.py:22
  27.5 1.8 %collective-permute-start.6 = (bf16[64,2048]{1,0:T(8,128)(2,1)S(1)}, bf16[64,2048]{1,0:T(8,128)(2,1)S(1)}, u32[]{:S(2)}, u32[]{:S(2)}) collective-permute-start(bf16[64,2048]{1,0:T(8,128)(2,1)S(1)} %collective-permute-done.2.refs_5_), channel_id=1, source_target_pairs={{0,2},{2,0},{1,3},{3,1},{4,6},{6,4},{5,7},{7,5},{8,10},{10,8},{9,1... | collective-permute-start | bytes 786440 | tf_op jit(solution)/shard_map/ppermute | solution.py:22
  32.6 24.7 %collective-permute-start.9 = (f16[512,768]{1,0:T(8,128)(2,1)S(1)}, f16[512,768]{1,0:T(8,128)(2,1)S(1)}, u32[]{:S(2)}, u32[]{:S(2)}) collective-permute-start(f16[512,768]{1,0:T(8,128)(2,1)S(1)} %convert_element_type.45), channel_id=1, source_target_pairs={{0,4},{12,8},{1,5},{13,9},{2,6},{14,10},{3,7},{15,11},{16,20},{28,... | collective-permute-start | bytes 2359304 | tf_op jit(solution)/shard_map/ppermute | solution.py:358
  40.4 21.0 %collective-permute-start.7 = (f16[512,768]{1,0:T(8,128)(2,1)}, f16[512,768]{1,0:T(8,128)(2,1)}, u32[]{:S(2)}, u32[]{:S(2)}) collective-permute-start(f16[512,768]{1,0:T(8,128)(2,1)} %convert_element_type.41), channel_id=1, source_target_pairs={{4,8},{8,4},{5,9},{9,5},{6,10},{10,6},{7,11},{11,7},{20,24},{24,20... | collective-permute-start | bytes 2359304 | tf_op jit(solution)/shard_map/ppermute | solution.py:360
  41.9 32.3 %collective-permute-start.8 = (f16[512,768]{1,0:T(8,128)(2,1)}, f16[512,768]{1,0:T(8,128)(2,1)}, u32[]{:S(2)}, u32[]{:S(2)}) collective-permute-start(f16[512,768]{1,0:T(8,128)(2,1)} %convert_element_type.41), channel_id=1, source_target_pairs={{0,8},{12,4},{1,9},{13,5},{2,10},{14,6},{3,11},{15,7},{16,24},{28,... | collective-permute-start | bytes 2359304 | tf_op jit(solution)/shard_map/ppermute | solution.py:361
  49.4 8.0 %copy-start.4 = (f32[512,768]{1,0:T(8,128)}, f32[512,768]{1,0:T(8,128)S(1)}, u32[]{:S(2)}) copy-start(f32[512,768]{1,0:T(8,128)S(1)} %get-tuple-element.17) | copy-start | bytes 4718596
  57.4 32.7 %collective-permute-start.10 = (f16[512,768]{1,0:T(8,128)(2,1)S(1)}, f16[512,768]{1,0:T(8,128)(2,1)S(1)}, u32[]{:S(2)}, u32[]{:S(2)}) collective-permute-start(f16[512,768]{1,0:T(8,128)(2,1)S(1)} %convert_element_type.44), channel_id=1, source_target_pairs={{0,4},{4,0},{8,12},{12,8},{1,5},{5,1},{9,13},{13,9},{2,6},{6,2},{1... | collective-permute-start | bytes 2359304 | tf_op jit(solution)/shard_map/ppermute | solution.py:365
  60.0 35.3 %collective-permute-start.11 = (f16[512,768]{1,0:T(8,128)(2,1)S(1)}, f16[512,768]{1,0:T(8,128)(2,1)}, u32[]{:S(2)}, u32[]{:S(2)}) collective-permute-start(f16[512,768]{1,0:T(8,128)(2,1)S(1)} %add_convert_fusion), channel_id=1, source_target_pairs={{4,12},{8,0},{5,13},{9,1},{6,14},{10,2},{7,15},{11,3},{20,28},{24,... | collective-permute-start | bytes 2359304 | tf_op jit(solution)/shard_map/ppermute | solution.py:363
  61.3 36.6 %copy-start.6 = (s32[2]{0:T(128)}, s32[2]{0:T(128)S(1)}, u32[]{:S(2)}) copy-start(s32[2]{0:T(128)S(1)} %pad_add_fusion.plan.refs_1_.where) | copy-start | bytes 28
  95.3 2.7 %copy-start.5 = (bf16[1,2048]{1,0:T(2,128)(2,1)S(1)}, bf16[1,2048]{1,0:T(2,128)(2,1)}, u32[]{:S(2)}) copy-start(bf16[1,2048]{1,0:T(2,128)(2,1)} %refs_3_.3) | copy-start | bytes 12292
  95.3 2.7 %copy-start.7 = (s32[4]{0:T(128)S(1)}, s32[4]{0:T(128)}, u32[]{:S(2)}) copy-start(s32[4]{0:T(128)} %lengths.1) | copy-start | bytes 52

commit v4 on v3

--- a/solution.py
+++ b/solution.py
@@ -15,7 +15,6 @@
 LINK_SCALE = 16.0
 GROUP = QUERY_HEAD_COUNT // KEY_VALUE_HEADS
 GRANT = 12
-PRICE = 1.0
 
 
 def swapped(array, axis, distance):
@@ -256,25 +255,27 @@
         products(held, (query_w, key_w, value_w), low, front, store)
 
 
-def rest_kernel(plan, *refs, pair):
-    pieces = refs[:-7]
-    own, query_w, key_w, value_w, *outs, tokens = refs[-7:]
-    rows = pieces[0].shape[0]
-    chip = 2 * rows
-    sources = len(pieces) // 2
+def rest_kernel(plan, *refs, pair, layout):
+    pieces = refs[: len(layout)]
+    own, query_w, key_w, value_w, outs, tokens = refs[len(layout) :]
+    chip = own.shape[1]
+    sources = tokens.shape[0] // chip
 
     def place(slot):
         return pl.ds(pl.multiple_of(plan[slot] * chip, chip), chip)
 
-    for index, piece in enumerate(pieces):
-        tokens[index * rows : (index + 1) * rows, :] = piece[...]
+    for piece, (base, half) in zip(pieces, layout):
+        rows = piece.shape[0]
+        if half is not None:
+            base = pl.multiple_of(base + (plan[sources + 5] ^ half) * rows, rows)
+        tokens[pl.ds(base, rows), :] = piece[...]
     for turn in range(2):
-        outs[turn][place(sources), :] = own[2 * pair + turn]
+        outs[turn, place(sources), :] = own[2 * pair + turn]
 
     def store(turn, start, total):
         for slot in range(sources):
             part = total[slot * chip : (slot + 1) * chip, :]
-            outs[turn][place(slot), start : start + total.shape[1]] = part
+            outs[turn, place(slot), start : start + total.shape[1]] = part
 
     low, front = plan[sources + 1 + 2 * pair], plan[sources + 2 + 2 * pair]
     products(tokens[...], (query_w, key_w, value_w), low, front, store)
@@ -293,8 +294,8 @@
         scratch_shapes=scratch,
         compiler_params=pltpu.CompilerParams(vmem_limit_bytes=GRANT * 1024 * 1024),
         cost_estimate=pl.CostEstimate(
-            flops=int(PRICE * 2 * owners * tokens * depth * cols),
-            bytes_accessed=int(PRICE * 2 * (tokens * depth + owners * cols * (depth + 2 * tokens))),
+            flops=int(2 * owners * tokens * depth * cols),
+            bytes_accessed=int(2 * (tokens * depth + owners * cols * (depth + 2 * tokens))),
             transcendentals=0,
         ),
     )(*operands)
@@ -307,18 +308,22 @@
     depth = w_query.shape[1]
     ctx = lax.axis_index("ctx")
     section = lax.axis_index("sec")
+    share = lax.axis_index("tp")
     count = 4
     f16, f32 = jnp.float16, jnp.float32
 
-    def columns(target):
-        return lax.dynamic_slice_in_dim(hidden, (target % count) * depth, depth, 1)
-
     steps = (2, 1, 3)
-    pieces = []
+    half_rows = rows // 2
+    sent = {}
     for step in steps:
         pairs = [(i, (i + step) % count) for i in range(count)]
-        pieces.append(lax.ppermute(columns(ctx + step), "ctx", pairs))
-    mine = columns(ctx)
+        start = ((ctx + step) % count) * depth
+        if step == 2:
+            piece = lax.dynamic_slice(hidden, (share * half_rows, start), (half_rows, depth))
+        else:
+            piece = lax.dynamic_slice_in_dim(hidden, start, depth, 1)
+        sent[step] = lax.ppermute(piece, "ctx", pairs)
+    mine = lax.dynamic_slice_in_dim(hidden, ctx * depth, depth, 1)
     weights = (w_query, key_projection, value_projection)
     cols = (GROUP + 2) * HEAD_SIZE
     chip = 2 * rows
@@ -326,7 +331,7 @@
     low = jnp.where(left, 2, 0)
     plan = jnp.stack(
         [*((ctx - step) % count for step in steps), ctx]
-        + [low, jnp.where(left, 1, 0), 2 - low, 1 - ctx % 2]
+        + [low, jnp.where(left, 1, 0), 2 - low, 1 - ctx % 2, share]
     ).astype(jnp.int32)
     (own,) = partial_call(
         lambda *refs: own_kernel(*refs, sources=count),
@@ -337,33 +342,41 @@
         count,
     )
 
-    *pieces, own = lax.optimization_barrier((*pieces, own))
-    pieces = [part for piece in pieces for part in (piece, swapped(piece, "sec", 0))]
+    sent[2], own = lax.optimization_barrier((sent[2], own))
+    swap = swapped(sent[2], "tp", 0)
+    sent[1], sent[3], swap, own = lax.optimization_barrier((sent[1], sent[3], swap, own))
+    pieces, layout = [], []
+    for slot, step in enumerate(steps):
+        parts = [(sent[step], None)]
+        if step == 2:
+            parts = [(sent[step], 0), (swap, 1)]
+        for part, half in parts:
+            pieces += [part, swapped(part, "sec", 0)]
+            layout += [(slot * chip, half), (slot * chip + rows, half)]
 
     def rest(pair):
         return partial_call(
-            lambda *refs: rest_kernel(*refs, pair=pair),
-            [(count * chip, cols)] * 2,
+            lambda *refs: rest_kernel(*refs, pair=pair, layout=layout),
+            [(2, count * chip, cols)],
             (plan, *pieces, own, *weights),
-            [pltpu.VMEM((len(pieces) * rows, depth), jnp.bfloat16)],
-            len(pieces) * rows,
+            [pltpu.VMEM((len(steps) * chip, depth), jnp.bfloat16)],
+            len(steps) * chip,
             2,
-        )
+        )[0]
 
     first = rest(0)
     second = rest(1)
 
     def reduced(first, second):
-        far = first[0].astype(f16)
-        fold = lax.ppermute(far, "ctx", [(0, 1), (3, 2)])
+        fold = lax.ppermute(first[0].astype(f16), "ctx", [(0, 1), (3, 2)])
         inner = first[1].astype(f16)
         middle = lax.ppermute(inner, "ctx", [(1, 2), (2, 1)])
         skip = lax.ppermute(inner, "ctx", [(0, 2), (3, 1)])
-        folded = (far.astype(f32) + fold.astype(f32)).astype(f16)
+        folded = (first[0] + fold.astype(f32)).astype(f16)
         ends = lax.ppermute(folded, "ctx", [(1, 3), (2, 0)])
         beside, _ = lax.optimization_barrier((second[0].astype(f16), folded))
         near = lax.ppermute(beside, "ctx", [(0, 1), (1, 0), (2, 3), (3, 2)])
-        total = second[1].astype(f16).astype(f32)
+        total = second[1]
         for part in (middle, skip, near, ends):
             total = total + part.astype(f32)
         return (total * (1.0 / LINK_SCALE)).astype(jnp.bfloat16)

time: 115 us -> 110 us (0.957)
  waiting for transfers between devices: 52.1 us -> 45.2 us
  local copies, waits for them, and re-layouts: 7.31 us -> 9.7 us
  starting transfers between devices: 24.9 us -> 23.1 us
  other arithmetic: 4.06 us -> 5.59 us
    ppermute x4, waiting for transfers between devices: 16.4 us -> 9.38 us  [the longest x1 6.99 us: reduced(): fold = lax.ppermute(first[0].astype(f16), 'ctx', [(0, 1), (3, 2)])]
    ppermute x4, starting transfers between devices: 14.2 us -> 10.5 us  [the longest x3 7.51 us: split_shards(): sent[step] = lax.ppermute(piece, 'ctx', pairs)]
    unnamed x16 -> x22, local copies, waits for them, and re-layouts: 4.99 us -> 7.53 us
    ppermute x4 -> x6, starting transfers between devices: 0.97 us -> 3.19 us  [swapped(): lax.ppermute(array, axis, [(i, i ^ 1 << distance) for i in range(lax.axis...]
    ppermute x4 -> x6, waiting for transfers between devices: 1.77 us -> 2.32 us  [swapped(): lax.ppermute(array, axis, [(i, i ^ 1 << distance) for i in range(lax.axis...]
  transfers between devices with their start and end apart: 12 -> 14, of which waited for: 9 -> 8; matrix products, arithmetic and copies ran while one was open for 1% -> 3% of each run, Pallas kernels for 5% -> 5%
where the time goes in v4:
time: 110 us; the launch traced here: 109 us
  waiting for transfers between devices  45.2 us (41%)
  starting transfers between devices  23.1 us (21%)
  Pallas kernels  13.9 us (13%)
  blocking collectives  11.1 us (10%)
  local copies, waits for them, and re-layouts  9.7 us (9%)
  other arithmetic  5.59 us (5%)
    ppermute x1, waiting for transfers between devices, reduced(): near = lax.ppermute(beside, 'ctx', [(0, 1), (1, 0), (2, 3), (3, 2)])  16 us
    ppermute x1, waiting for transfers between devices, reduced(): skip = lax.ppermute(inner, 'ctx', [(0, 2), (3, 1)])  12.1 us
    all_to_all x1, blocking collectives, split_shards(): spread = lax.all_to_all(sums, ('ctx', 'sec', 'tp'), 0, 0, tiled=True)  11.1 us
    pallas_call x3, Pallas kernels, partial_call(): pl.pallas_call(kernel, out_shape=[jax.ShapeDtypeStruct(shape, jnp.float32...  8.9 us
    unnamed x22, local copies, waits for them, and re-layouts  7.53 us
    ppermute x3, starting transfers between devices, split_shards(): sent[step] = lax.ppermute(piece, 'ctx', pairs)  7.51 us
    ppermute x1, waiting for transfers between devices, reduced(): fold = lax.ppermute(first[0].astype(f16), 'ctx', [(0, 1), (3, 2)])  6.99 us
    ppermute x1, waiting for transfers between devices, reduced(): ends = lax.ppermute(folded, 'ctx', [(1, 3), (2, 0)])  5.43 us
  transfers between devices with their start and end apart: 14, of which 8 were waited for; matrix products, arithmetic and copies ran while one was open for 3% of the time, Pallas kernels for 5%

profile of v4, /device:TPU:0, one launch (start us, length us, event | category | flops | bytes accessed | tf_op | source)
XLA Modules:
  0.0 109.4 jit_solution(1147554148025212472)
XLA Ops:
  0.7 1.2 %constant_dynamic-slice_fusion = (bf16[64,2048]{1,0:T(8,128)(2,1)S(1)}, bf16[64,2048]{1,0:T(8,128)(2,1)S(1)}, bf16[64,2048]{1,0:T(8,128)(2,1)S(1)}) fusion(bf16[64,8192]{1,0:T(8,128)(2,1)} %param.8, s32[]{:T(128)S(6)} %select_n.66, s32[]{:T(128)S(6)} %select_n.62, s32[]{:T(128)S(6)} %select_n.64), kind=kLoop, calls=%fused_computation.14 | loop fusion | bytes 1572876 | tf_op jit(solution)/shard_map/dynamic_slice | solution.py:324
  1.8 0.5 collective-permute-start.1
  2.4 0.9 dynamic_slice.12
  3.3 3.7 %collective-permute-start = (bf16[32,2048]{1,0:T(8,128)(2,1)S(1)}, bf16[32,2048]{1,0:T(8,128)(2,1)S(1)}, u32[]{:S(2)}, u32[]{:S(2)}) collective-permute-start(bf16[32,2048]{1,0:T(8,128)(2,1)S(1)} %dynamic_slice.12), channel_id=1, source_target_pairs={{0,8},{4,12},{8,0},{12,4},{1,9},{5,13},{9,1},{13,5},{2,10},{6,14},... | collective-permute-start | bytes 393224 | tf_op jit(solution)/shard_map/ppermute | solution.py:325
  7.0 1.6 %collective-permute-start.3 = (bf16[64,2048]{1,0:T(8,128)(2,1)S(1)}, bf16[64,2048]{1,0:T(8,128)(2,1)S(1)}, u32[]{:S(2)}, u32[]{:S(2)}) collective-permute-start(bf16[64,2048]{1,0:T(8,128)(2,1)S(1)} %get-tuple-element.24), channel_id=1, source_target_pairs={{0,4},{4,8},{8,12},{12,0},{1,5},{5,9},{9,13},{13,1},{2,6},{6,10},{... | collective-permute-start | bytes 786440 | tf_op jit(solution)/shard_map/ppermute | solution.py:325
  8.5 2.2 %collective-permute-start.4 = (bf16[64,2048]{1,0:T(8,128)(2,1)S(1)}, bf16[64,2048]{1,0:T(8,128)(2,1)S(1)}, u32[]{:S(2)}, u32[]{:S(2)}) collective-permute-start(bf16[64,2048]{1,0:T(8,128)(2,1)S(1)} %get-tuple-element.22), channel_id=1, source_target_pairs={{0,12},{4,0},{8,4},{12,8},{1,13},{5,1},{9,5},{13,9},{2,14},{6,2},{... | collective-permute-start | bytes 786440 | tf_op jit(solution)/shard_map/ppermute | solution.py:325
  10.8 0.1 stack.48.refs_0_
  10.9 0.0 collective-permute-done.1.refs_2_
  10.9 0.0 copy-start
  10.9 3.4 %copy-done = bf16[1,2048,2048]{2,1,0:T(8,128)(2,1)S(1)} copy-done((bf16[1,2048,2048]{2,1,0:T(8,128)(2,1)S(1)}, bf16[1,2048,2048]{2,1,0:T(8,128)(2,1)}, u32[]{:S(2)}) %copy-start) | copy-done | bytes 8388632
  14.3 1.6 %copy-done.2 = bf16[1,2048,512]{2,1,0:T(8,128)(2,1)S(1)} copy-done((bf16[1,2048,512]{2,1,0:T(8,128)(2,1)S(1)}, bf16[1,2048,512]{2,1,0:T(8,128)(2,1)}, u32[]{:S(2)}) %copy-start.2) | copy-done | bytes 2097176
  15.9 1.6 %copy-done.4 = bf16[1,2048,512]{2,1,0:T(8,128)(2,1)S(1)} copy-done((bf16[1,2048,512]{2,1,0:T(8,128)(2,1)S(1)}, bf16[1,2048,512]{2,1,0:T(8,128)(2,1)}, u32[]{:S(2)}) %copy-start.4) | copy-done | bytes 2097176
  17.5 2.4 %shard_map.95.refs_9_ = f32[4,128,768]{2,1,0:T(8,128)S(1)} custom-call(s32[9]{0:T(128)S(1)} %stack.48.refs_0_, bf16[64,2048]{1,0:T(8,128)(2,1)S(1)} %get-tuple-element.23.refs_1_, bf16[64,2048]{1,0:T(8,128)(2,1)S(1)} %collective-permute-done.1.refs_2_, bf16[1,2048,2048]{2,1,0:T(8,128)(2,1)S(1)} %copy-done, bf16[1,2048,512]{2,1,0:T(8,128)(2,1)S(1)} %copy-done.2, ...), custom_call_target="tpu_custom_call" | custom-call | flops 1610612736 | bytes 14680064 | tf_op jit(solution)/shard_map/pallas_call | solution.py:289
  19.9 0.0 collective-permute-done.refs_1_
  19.9 1.7 %collective-permute-start.5 = (bf16[32,2048]{1,0:T(8,128)(2,1)S(1)}, bf16[32,2048]{1,0:T(8,128)(2,1)S(1)}, u32[]{:S(2)}, u32[]{:S(2)}) collective-permute-start(bf16[32,2048]{1,0:T(8,128)(2,1)S(1)} %collective-permute-done.refs_1_), channel_id=1, source_target_pairs={{0,1},{1,0},{2,3},{3,2},{4,5},{5,4},{6,7},{7,6},{8,9},{9,8},{10,11... | collective-permute-start | bytes 393224 | tf_op jit(solution)/shard_map/ppermute | solution.py:21
  21.5 0.0 collective-permute-done.3.refs_5_
  21.5 2.4 %collective-permute-done.4.refs_7_ = bf16[64,2048]{1,0:T(8,128)(2,1)S(1)} collective-permute-done((bf16[64,2048]{1,0:T(8,128)(2,1)S(1)}, bf16[64,2048]{1,0:T(8,128)(2,1)S(1)}, u32[]{:S(2)}, u32[]{:S(2)}) %collective-permute-start.4) | collective-permute-done | bytes 262176 | tf_op jit(solution)/shard_map/ppermute | solution.py:325
  23.9 1.0 collective-permute-done.5.refs_3_
  25.0 0.0 collective-permute-start.7
  25.0 0.5 collective-permute-start.8
  25.5 0.0 collective-permute-start.2
  25.5 0.5 collective-permute-start.6
  26.0 1.1 collective-permute-done.2.refs_2_
  27.1 0.2 collective-permute-done.6.refs_4_
  27.3 0.0 collective-permute-done.7.refs_6_
  27.3 0.0 collective-permute-done.8.refs_8_
  27.3 3.2 %shard_map.97 = f32[2,512,768]{2,1,0:T(8,128)S(1)} custom-call(s32[9]{0:T(128)S(1)} %stack.48.refs_0_, bf16[32,2048]{1,0:T(8,128)(2,1)S(1)} %collective-permute-done.refs_1_, bf16[32,2048]{1,0:T(8,128)(2,1)S(1)} %collective-permute-done.2.refs_2_, bf16[32,2048]{1,0:T(8,128)(2,1)S(1)} %collective-permute-done.5.refs_3_, ...), custom_call_target="tpu_custom_call" | custom-call | flops 2415919104 | bytes 10223616 | tf_op jit(solution)/shard_map/pallas_call | solution.py:289
  30.5 0.0 copy-done.6
  30.6 1.1 %fusion.7 = (f16[512,768]{1,0:T(8,128)(2,1)}, f16[512,768]{1,0:T(8,128)(2,1)S(1)}) fusion(f32[2,512,768]{2,1,0:T(8,128)S(1)} %shard_map.97), kind=kLoop, calls=%fused_computation.12 | loop fusion | flops 786432 | bytes 4718592 | tf_op jit(solution)/shard_map/convert_element_type | solution.py:372
  31.7 3.0 %collective-permute-start.11 = (f16[512,768]{1,0:T(8,128)(2,1)S(1)}, f16[512,768]{1,0:T(8,128)(2,1)S(1)}, u32[]{:S(2)}, u32[]{:S(2)}) collective-permute-start(f16[512,768]{1,0:T(8,128)(2,1)S(1)} %get-tuple-element.21), channel_id=1, source_target_pairs={{0,4},{12,8},{1,5},{13,9},{2,6},{14,10},{3,7},{15,11},{16,20},{28,... | collective-permute-start | bytes 2359304 | tf_op jit(solution)/shard_map/ppermute | solution.py:371
  34.6 4.1 %collective-permute-start.10 = (f16[512,768]{1,0:T(8,128)(2,1)}, f16[512,768]{1,0:T(8,128)(2,1)}, u32[]{:S(2)}, u32[]{:S(2)}) collective-permute-start(f16[512,768]{1,0:T(8,128)(2,1)} %get-tuple-element.20), channel_id=1, source_target_pairs={{0,8},{12,4},{1,9},{13,5},{2,10},{14,6},{3,11},{15,7},{16,24},{28,... | collective-permute-start | bytes 2359304 | tf_op jit(solution)/shard_map/ppermute | solution.py:374
  38.7 1.6 %collective-permute-start.9 = (f16[512,768]{1,0:T(8,128)(2,1)}, f16[512,768]{1,0:T(8,128)(2,1)}, u32[]{:S(2)}, u32[]{:S(2)}) collective-permute-start(f16[512,768]{1,0:T(8,128)(2,1)} %get-tuple-element.20), channel_id=1, source_target_pairs={{4,8},{8,4},{5,9},{9,5},{6,10},{10,6},{7,11},{11,7},{20,24},{24,20... | collective-permute-start | bytes 2359304 | tf_op jit(solution)/shard_map/ppermute | solution.py:373
  40.3 0.9 copy-done.7
  41.2 3.2 %shard_map.96 = f32[2,512,768]{2,1,0:T(8,128)S(1)} custom-call(s32[9]{0:T(128)S(1)} %stack.48.refs_0_, bf16[32,2048]{1,0:T(8,128)(2,1)S(1)} %collective-permute-done.refs_1_, bf16[32,2048]{1,0:T(8,128)(2,1)S(1)} %collective-permute-done.2.refs_2_, bf16[32,2048]{1,0:T(8,128)(2,1)S(1)} %collective-permute-done.5.refs_3_, ...), custom_call_target="tpu_custom_call" | custom-call | flops 2415919104 | bytes 10223616 | tf_op jit(solution)/shard_map/pallas_call | solution.py:289
  44.5 1.0 fusion.8
  45.5 7.0 %collective-permute-done.11 = f16[512,768]{1,0:T(8,128)(2,1)S(1)} collective-permute-done((f16[512,768]{1,0:T(8,128)(2,1)S(1)}, f16[512,768]{1,0:T(8,128)(2,1)S(1)}, u32[]{:S(2)}, u32[]{:S(2)}) %collective-permute-start.11) | collective-permute-done | bytes 786464 | tf_op jit(solution)/shard_map/ppermute | solution.py:371
  52.5 1.1 add_convert_fusion
  53.5 2.5 %collective-permute-start.12 = (f16[512,768]{1,0:T(8,128)(2,1)}, f16[512,768]{1,0:T(8,128)(2,1)}, u32[]{:S(2)}, u32[]{:S(2)}) collective-permute-start(f16[512,768]{1,0:T(8,128)(2,1)} %fusion.8), channel_id=1, source_target_pairs={{0,4},{4,0},{8,12},{12,8},{1,5},{5,1},{9,13},{13,9},{2,6},{6,2},{1... | collective-permute-start | bytes 2359304 | tf_op jit(solution)/shard_map/ppermute | solution.py:378
  56.0 1.3 %collective-permute-start.13 = (f16[512,768]{1,0:T(8,128)(2,1)}, f16[512,768]{1,0:T(8,128)(2,1)}, u32[]{:S(2)}, u32[]{:S(2)}) collective-permute-start(f16[512,768]{1,0:T(8,128)(2,1)} %add_convert_fusion), channel_id=1, source_target_pairs={{4,12},{8,0},{5,13},{9,1},{6,14},{10,2},{7,15},{11,3},{20,28},{24,... | collective-permute-start | bytes 2359304 | tf_op jit(solution)/shard_map/ppermute | solution.py:376
  57.3 0.1 pad_add_fusion.plan.refs_1_.where
  57.4 12.1 %collective-permute-done.10 = f16[512,768]{1,0:T(8,128)(2,1)} collective-permute-done((f16[512,768]{1,0:T(8,128)(2,1)}, f16[512,768]{1,0:T(8,128)(2,1)}, u32[]{:S(2)}, u32[]{:S(2)}) %collective-permute-start.10) | collective-permute-done | bytes 786464 | tf_op jit(solution)/shard_map/ppermute | solution.py:374
  69.5 0.0 collective-permute-done.9
  69.5 16.0 %collective-permute-done.12 = f16[512,768]{1,0:T(8,128)(2,1)} collective-permute-done((f16[512,768]{1,0:T(8,128)(2,1)}, f16[512,768]{1,0:T(8,128)(2,1)}, u32[]{:S(2)}, u32[]{:S(2)}) %collective-permute-start.12) | collective-permute-done | bytes 786464 | tf_op jit(solution)/shard_map/ppermute | solution.py:378
  85.5 5.4 %collective-permute-done.13 = f16[512,768]{1,0:T(8,128)(2,1)} collective-permute-done((f16[512,768]{1,0:T(8,128)(2,1)}, f16[512,768]{1,0:T(8,128)(2,1)}, u32[]{:S(2)}, u32[]{:S(2)}) %collective-permute-start.13) | collective-permute-done | bytes 786464 | tf_op jit(solution)/shard_map/ppermute | solution.py:376
  91.0 2.3 %fusion.5.refs_2_ = bf16[512,768]{1,0:T(8,128)(2,1)S(1)} fusion(f32[2,512,768]{2,1,0:T(8,128)S(1)} %shard_map.96, f16[512,768]{1,0:T(8,128)(2,1)} %collective-permute-done.13, f16[512,768]{1,0:T(8,128)(2,1)} %collective-permute-done.12, f16[512,768]{1,0:T(8,128)(2,1)} %collective-permute-done.10, f16[512,768]{1,0:T(8,128)(2,1)} %collective-permute-done.9), kind=kLoop, calls=%fused_computation.9 | loop fusion | flops 3932160 | bytes 5505024 | tf_op jit(solution)/shard_map/convert_element_type | solution.py:382
  93.3 3.7 %shard_map.98 = f32[16,1,128]{2,1,0:T(1,128)S(1)} custom-call(s32[2]{0:T(128)S(1)} %pad_add_fusion.plan.refs_1_.where, s32[4]{0:T(128)S(1)} %copy-done.10, s32[2]{0:T(128)S(1)} %pad_add_fusion.plan.refs_1_.where, bf16[512,768]{1,0:T(8,128)(2,1)S(1)} %fusion.5.refs_2_, bf16[1,2048]{1,0:T(2,128)(2,1)S(1)} %copy-done.8), custom_call_target="tpu_custom_call" | custom-call | tf_op jit(solution)/shard_map/pallas_call | solution.py:388
  97.0 11.1 %all_to_all.5.parts = f32[16,1,128]{2,1,0:T(1,128)} all-to-all(f32[16,1,128]{2,1,0:T(1,128)S(1)} %shard_map.98), channel_id=1, replica_groups=mesh['grp'=2,'ctx'=4,'sec'=2,'tp'=2] {'ctx','sec','tp'}, dimensions={0} | all-to-all | bytes 16384 | tf_op jit(solution)/shard_map/all_to_all | solution.py:405
  108.1 1.3 %shard_map.99 = (f32[1,64]{1,0:T(1,128)}, f32[1,64]{1,0:T(1,128)}) custom-call(s32[4]{0:T(128)} %lengths.1, s32[4]{0:T(128)} %prompt_len.1, f32[4]{0:T(128)} %reward.1, s32[2]{0:T(128)} %copy-done.9, f32[16,1,128]{2,1,0:T(1,128)} %all_to_all.5.parts), custom_call_target="tpu_custom_call" | custom-call | tf_op jit(solution)/shard_map/pallas_call | solution.py:407
  (16 shorter events, 0.0 us)
Async XLA Ops:
  1.8 9.0 %collective-permute-start.1 = (bf16[64,2048]{1,0:T(8,128)(2,1)S(1)}, bf16[64,2048]{1,0:T(8,128)(2,1)S(1)}, u32[]{:S(2)}, u32[]{:S(2)}) collective-permute-start(bf16[64,2048]{1,0:T(8,128)(2,1)S(1)} %get-tuple-element.23.refs_1_), channel_id=1, source_target_pairs={{0,2},{2,0},{1,3},{3,1},{4,6},{6,4},{5,7},{7,5},{8,10},{10,8},{9,1... | collective-permute-start | bytes 786440 | tf_op jit(solution)/shard_map/ppermute | solution.py:21
  3.3 16.6 %collective-permute-start = (bf16[32,2048]{1,0:T(8,128)(2,1)S(1)}, bf16[32,2048]{1,0:T(8,128)(2,1)S(1)}, u32[]{:S(2)}, u32[]{:S(2)}) collective-permute-start(bf16[32,2048]{1,0:T(8,128)(2,1)S(1)} %dynamic_slice.12), channel_id=1, source_target_pairs={{0,8},{4,12},{8,0},{12,4},{1,9},{5,13},{9,1},{13,5},{2,10},{6,14},... | collective-permute-start | bytes 393224 | tf_op jit(solution)/shard_map/ppermute | solution.py:325
  7.0 14.6 %collective-permute-start.3 = (bf16[64,2048]{1,0:T(8,128)(2,1)S(1)}, bf16[64,2048]{1,0:T(8,128)(2,1)S(1)}, u32[]{:S(2)}, u32[]{:S(2)}) collective-permute-start(bf16[64,2048]{1,0:T(8,128)(2,1)S(1)} %get-tuple-element.24), channel_id=1, source_target_pairs={{0,4},{4,8},{8,12},{12,0},{1,5},{5,9},{9,13},{13,1},{2,6},{6,10},{... | collective-permute-start | bytes 786440 | tf_op jit(solution)/shard_map/ppermute | solution.py:325
  8.5 15.4 %collective-permute-start.4 = (bf16[64,2048]{1,0:T(8,128)(2,1)S(1)}, bf16[64,2048]{1,0:T(8,128)(2,1)S(1)}, u32[]{:S(2)}, u32[]{:S(2)}) collective-permute-start(bf16[64,2048]{1,0:T(8,128)(2,1)S(1)} %get-tuple-element.22), channel_id=1, source_target_pairs={{0,12},{4,0},{8,4},{12,8},{1,13},{5,1},{9,5},{13,9},{2,14},{6,2},{... | collective-permute-start | bytes 786440 | tf_op jit(solution)/shard_map/ppermute | solution.py:325
  10.9 3.4 %copy-start = (bf16[1,2048,2048]{2,1,0:T(8,128)(2,1)S(1)}, bf16[1,2048,2048]{2,1,0:T(8,128)(2,1)}, u32[]{:S(2)}) copy-start(bf16[1,2048,2048]{2,1,0:T(8,128)(2,1)} %refs_10_.3) | copy-start | bytes 25165828
  14.3 1.6 %copy-start.2 = (bf16[1,2048,512]{2,1,0:T(8,128)(2,1)S(1)}, bf16[1,2048,512]{2,1,0:T(8,128)(2,1)}, u32[]{:S(2)}) copy-start(bf16[1,2048,512]{2,1,0:T(8,128)(2,1)} %refs_11_.3) | copy-start | bytes 6291460
  15.9 1.6 %copy-start.4 = (bf16[1,2048,512]{2,1,0:T(8,128)(2,1)S(1)}, bf16[1,2048,512]{2,1,0:T(8,128)(2,1)}, u32[]{:S(2)}) copy-start(bf16[1,2048,512]{2,1,0:T(8,128)(2,1)} %refs_12_.3) | copy-start | bytes 6291460
  17.4 9.8 %copy-start.1 = (bf16[1,2048,2048]{2,1,0:T(8,128)(2,1)S(1)}, bf16[1,2048,2048]{2,1,0:T(8,128)(2,1)}, u32[]{:S(2)}) copy-start(bf16[1,2048,2048]{2,1,0:T(8,128)(2,1)} %refs_10_.3) | copy-start | bytes 25165828
  17.4 9.8 %copy-start.3 = (bf16[1,2048,512]{2,1,0:T(8,128)(2,1)S(1)}, bf16[1,2048,512]{2,1,0:T(8,128)(2,1)}, u32[]{:S(2)}) copy-start(bf16[1,2048,512]{2,1,0:T(8,128)(2,1)} %refs_11_.3) | copy-start | bytes 6291460
  17.4 9.8 %copy-start.5 = (bf16[1,2048,512]{2,1,0:T(8,128)(2,1)S(1)}, bf16[1,2048,512]{2,1,0:T(8,128)(2,1)}, u32[]{:S(2)}) copy-start(bf16[1,2048,512]{2,1,0:T(8,128)(2,1)} %refs_12_.3) | copy-start | bytes 6291460
  19.9 5.1 %collective-permute-start.5 = (bf16[32,2048]{1,0:T(8,128)(2,1)S(1)}, bf16[32,2048]{1,0:T(8,128)(2,1)S(1)}, u32[]{:S(2)}, u32[]{:S(2)}) collective-permute-start(bf16[32,2048]{1,0:T(8,128)(2,1)S(1)} %collective-permute-done.refs_1_), channel_id=1, source_target_pairs={{0,1},{1,0},{2,3},{3,2},{4,5},{5,4},{6,7},{7,6},{8,9},{9,8},{10,11... | collective-permute-start | bytes 393224 | tf_op jit(solution)/shard_map/ppermute | solution.py:21
  23.9 6.6 %copy-start.6 = (bf16[64,2048]{1,0:T(8,128)(2,1)}, bf16[64,2048]{1,0:T(8,128)(2,1)S(1)}, u32[]{:S(2)}) copy-start(bf16[64,2048]{1,0:T(8,128)(2,1)S(1)} %collective-permute-done.4.refs_7_) | copy-start | bytes 786436
  25.0 2.3 %collective-permute-start.7 = (bf16[64,2048]{1,0:T(8,128)(2,1)S(1)}, bf16[64,2048]{1,0:T(8,128)(2,1)S(1)}, u32[]{:S(2)}, u32[]{:S(2)}) collective-permute-start(bf16[64,2048]{1,0:T(8,128)(2,1)S(1)} %collective-permute-done.3.refs_5_), channel_id=1, source_target_pairs={{0,2},{2,0},{1,3},{3,1},{4,6},{6,4},{5,7},{7,5},{8,10},{10,8},{9,1... | collective-permute-start | bytes 786440 | tf_op jit(solution)/shard_map/ppermute | solution.py:21
  25.0 2.3 %collective-permute-start.8 = (bf16[64,2048]{1,0:T(8,128)(2,1)S(1)}, bf16[64,2048]{1,0:T(8,128)(2,1)S(1)}, u32[]{:S(2)}, u32[]{:S(2)}) collective-permute-start(bf16[64,2048]{1,0:T(8,128)(2,1)S(1)} %collective-permute-done.4.refs_7_), channel_id=1, source_target_pairs={{0,2},{2,0},{1,3},{3,1},{4,6},{6,4},{5,7},{7,5},{8,10},{10,8},{9,1... | collective-permute-start | bytes 786440 | tf_op jit(solution)/shard_map/ppermute | solution.py:21
  25.5 1.6 %collective-permute-start.2 = (bf16[32,2048]{1,0:T(8,128)(2,1)S(1)}, bf16[32,2048]{1,0:T(8,128)(2,1)S(1)}, u32[]{:S(2)}, u32[]{:S(2)}) collective-permute-start(bf16[32,2048]{1,0:T(8,128)(2,1)S(1)} %collective-permute-done.refs_1_), channel_id=1, source_target_pairs={{0,2},{2,0},{1,3},{3,1},{4,6},{6,4},{5,7},{7,5},{8,10},{10,8},{9,1... | collective-permute-start | bytes 393224 | tf_op jit(solution)/shard_map/ppermute | solution.py:21
  25.5 1.8 %collective-permute-start.6 = (bf16[32,2048]{1,0:T(8,128)(2,1)S(1)}, bf16[32,2048]{1,0:T(8,128)(2,1)S(1)}, u32[]{:S(2)}, u32[]{:S(2)}) collective-permute-start(bf16[32,2048]{1,0:T(8,128)(2,1)S(1)} %collective-permute-done.5.refs_3_), channel_id=1, source_target_pairs={{0,2},{2,0},{1,3},{3,1},{4,6},{6,4},{5,7},{7,5},{8,10},{10,8},{9,1... | collective-permute-start | bytes 393224 | tf_op jit(solution)/shard_map/ppermute | solution.py:21
  31.7 20.8 %collective-permute-start.11 = (f16[512,768]{1,0:T(8,128)(2,1)S(1)}, f16[512,768]{1,0:T(8,128)(2,1)S(1)}, u32[]{:S(2)}, u32[]{:S(2)}) collective-permute-start(f16[512,768]{1,0:T(8,128)(2,1)S(1)} %get-tuple-element.21), channel_id=1, source_target_pairs={{0,4},{12,8},{1,5},{13,9},{2,6},{14,10},{3,7},{15,11},{16,20},{28,... | collective-permute-start | bytes 2359304 | tf_op jit(solution)/shard_map/ppermute | solution.py:371
  34.6 34.8 %collective-permute-start.10 = (f16[512,768]{1,0:T(8,128)(2,1)}, f16[512,768]{1,0:T(8,128)(2,1)}, u32[]{:S(2)}, u32[]{:S(2)}) collective-permute-start(f16[512,768]{1,0:T(8,128)(2,1)} %get-tuple-element.20), channel_id=1, source_target_pairs={{0,8},{12,4},{1,9},{13,5},{2,10},{14,6},{3,11},{15,7},{16,24},{28,... | collective-permute-start | bytes 2359304 | tf_op jit(solution)/shard_map/ppermute | solution.py:374
  38.7 30.8 %collective-permute-start.9 = (f16[512,768]{1,0:T(8,128)(2,1)}, f16[512,768]{1,0:T(8,128)(2,1)}, u32[]{:S(2)}, u32[]{:S(2)}) collective-permute-start(f16[512,768]{1,0:T(8,128)(2,1)} %get-tuple-element.20), channel_id=1, source_target_pairs={{4,8},{8,4},{5,9},{9,5},{6,10},{10,6},{7,11},{11,7},{20,24},{24,20... | collective-permute-start | bytes 2359304 | tf_op jit(solution)/shard_map/ppermute | solution.py:373
  40.3 0.9 copy-start.7
  53.5 32.0 %collective-permute-start.12 = (f16[512,768]{1,0:T(8,128)(2,1)}, f16[512,768]{1,0:T(8,128)(2,1)}, u32[]{:S(2)}, u32[]{:S(2)}) collective-permute-start(f16[512,768]{1,0:T(8,128)(2,1)} %fusion.8), channel_id=1, source_target_pairs={{0,4},{4,0},{8,12},{12,8},{1,5},{5,1},{9,13},{13,9},{2,6},{6,2},{1... | collective-permute-start | bytes 2359304 | tf_op jit(solution)/shard_map/ppermute | solution.py:378
  56.0 34.9 %collective-permute-start.13 = (f16[512,768]{1,0:T(8,128)(2,1)}, f16[512,768]{1,0:T(8,128)(2,1)}, u32[]{:S(2)}, u32[]{:S(2)}) collective-permute-start(f16[512,768]{1,0:T(8,128)(2,1)} %add_convert_fusion), channel_id=1, source_target_pairs={{4,12},{8,0},{5,13},{9,1},{6,14},{10,2},{7,15},{11,3},{20,28},{24,... | collective-permute-start | bytes 2359304 | tf_op jit(solution)/shard_map/ppermute | solution.py:376
  57.4 35.9 %copy-start.9 = (s32[2]{0:T(128)}, s32[2]{0:T(128)S(1)}, u32[]{:S(2)}) copy-start(s32[2]{0:T(128)S(1)} %pad_add_fusion.plan.refs_1_.where) | copy-start | bytes 28
  57.4 35.9 %copy-start.8 = (bf16[1,2048]{1,0:T(2,128)(2,1)S(1)}, bf16[1,2048]{1,0:T(2,128)(2,1)}, u32[]{:S(2)}) copy-start(bf16[1,2048]{1,0:T(2,128)(2,1)} %refs_3_.3) | copy-start | bytes 12292
  57.4 35.9 %copy-start.10 = (s32[4]{0:T(128)S(1)}, s32[4]{0:T(128)}, u32[]{:S(2)}) copy-start(s32[4]{0:T(128)} %lengths.1) | copy-start | bytes 52

commit v5 on v4

--- a/solution.py
+++ b/solution.py
@@ -1,3 +1,5 @@
+import math
+
 import jax
 import jax.numpy as jnp
 from jax import lax
@@ -146,27 +148,33 @@
     def place(shape, axis):
         return token_places(lax.broadcasted_iota(jnp.int32, shape, axis), section, rows)
 
+    wide = GROUP * HEAD_SIZE
+    columns = [
+        jnp.broadcast_to(head[:, cols].astype(jnp.float32), (HEAD_SIZE, HEAD_SIZE)).T[:, :1]
+        for cols in (slice(at, at + HEAD_SIZE) for at in range(0, wide, HEAD_SIZE))
+    ]
     query_pos = place((1, tokens), 1)
+    key_pos = place((tokens, 1), 0)
     begin = jnp.zeros((1, tokens), jnp.int32)
     start = jnp.int32(0)
     for index in range(lengths.shape[0] - 1):
         start = start + lengths[index]
         begin = jnp.where(query_pos >= start, start, begin)
-    key_pos = place((tokens, 1), 0)
     valid = (key_pos <= query_pos) & (key_pos >= begin)
-    wide = GROUP * HEAD_SIZE
     key = block[:, wide : wide + HEAD_SIZE]
     value = block[:, wide + HEAD_SIZE :]
     numerator = jnp.zeros((1, tokens), jnp.float32)
     squares = jnp.zeros((1, tokens), jnp.float32)
     for index in range(GROUP):
-        cols = slice(index * HEAD_SIZE, (index + 1) * HEAD_SIZE)
         logits = lax.dot_general(
-            key, block[:, cols], (((1,), (1,)), ((), ())), preferred_element_type=jnp.float32
-        ) * (HEAD_SIZE ** (-0.5))
+            key,
+            block[:, index * HEAD_SIZE : (index + 1) * HEAD_SIZE],
+            (((1,), (1,)), ((), ())),
+            preferred_element_type=jnp.float32,
+        )
         masked = jnp.where(valid, logits, NEGATIVE)
         peak = jnp.max(masked, axis=0, keepdims=True)
-        weights = jnp.exp(masked - peak)
+        weights = jnp.exp2((masked - peak) * (HEAD_SIZE ** (-0.5) * math.log2(math.e)))
         total = jnp.sum(weights, axis=0, keepdims=True)
         mixed = lax.dot_general(
             value,
@@ -174,9 +182,8 @@
             (((0,), (0,)), ((), ())),
             preferred_element_type=jnp.float32,
         )
-        attended = mixed / total
-        column = jnp.broadcast_to(head[:, cols].astype(jnp.float32), (HEAD_SIZE, HEAD_SIZE)).T
-        numerator += jnp.sum(attended * column[:, :1], axis=0, keepdims=True)
+        attended = mixed * (1.0 / total)
+        numerator += jnp.sum(attended * columns[index], axis=0, keepdims=True)
         squares += jnp.sum(attended * attended, axis=0, keepdims=True)
     for ctx in range(tokens // (2 * rows)):
         own = slice(2 * ctx * rows, (2 * ctx + 1) * rows)
@@ -244,6 +251,23 @@
             store(turn, wide + index * HEAD_SIZE, jnp.where(front == 0, one, two))
 
 
+def cut_kernel(plan, hidden, *refs):
+    outs, done = refs[:-1], refs[-1]
+    copies = []
+    for index, out in enumerate(outs):
+        rows, depth = out.shape
+        first = 0
+        if rows < hidden.shape[0]:
+            first = pl.multiple_of(plan[0] * rows, rows)
+        start = pl.multiple_of(plan[1 + index] * depth, HEAD_SIZE)
+        part = hidden.at[pl.ds(first, rows), pl.ds(start, depth)]
+        copies.append(pltpu.make_async_copy(part, out, done.at[index]))
+    for copy in copies:
+        copy.start()
+    for copy in copies:
+        copy.wait()
+
+
 def own_kernel(plan, own, other, query_w, key_w, value_w, out, sources):
     held = jnp.concatenate([own[...], other[...]], axis=0)
     for pair in range(2):
@@ -314,16 +338,26 @@
 
     steps = (2, 1, 3)
     half_rows = rows // 2
+    targets = [(ctx + step) % count for step in (*steps, 0)]
+    cuts = pl.pallas_call(
+        cut_kernel,
+        out_shape=[
+            jax.ShapeDtypeStruct((half_rows if step == 2 else rows, depth), hidden.dtype)
+            for step in (*steps, 0)
+        ],
+        in_specs=[
+            pl.BlockSpec(memory_space=pltpu.SMEM),
+            pl.BlockSpec(memory_space=pl.ANY),
+        ],
+        out_specs=[pl.BlockSpec(memory_space=pltpu.VMEM)] * 4,
+        scratch_shapes=[pltpu.SemaphoreType.DMA((4,))],
+        compiler_params=pltpu.CompilerParams(vmem_limit_bytes=4 * 1024 * 1024),
+    )(jnp.stack([share, *targets]).astype(jnp.int32), hidden)
+    mine = cuts[3]
     sent = {}
-    for step in steps:
+    for step, piece in zip(steps, cuts):
         pairs = [(i, (i + step) % count) for i in range(count)]
-        start = ((ctx + step) % count) * depth
-        if step == 2:
-            piece = lax.dynamic_slice(hidden, (share * half_rows, start), (half_rows, depth))
-        else:
-            piece = lax.dynamic_slice_in_dim(hidden, start, depth, 1)
         sent[step] = lax.ppermute(piece, "ctx", pairs)
-    mine = lax.dynamic_slice_in_dim(hidden, ctx * depth, depth, 1)
     weights = (w_query, key_projection, value_projection)
     cols = (GROUP + 2) * HEAD_SIZE
     chip = 2 * rows
@@ -368,7 +402,8 @@
     second = rest(1)
 
     def reduced(first, second):
-        fold = lax.ppermute(first[0].astype(f16), "ctx", [(0, 1), (3, 2)])
+        far, first = lax.optimization_barrier((first[0].astype(f16), first))
+        fold = lax.ppermute(far, "ctx", [(0, 1), (3, 2)])
         inner = first[1].astype(f16)
         middle = lax.ppermute(inner, "ctx", [(1, 2), (2, 1)])
         skip = lax.ppermute(inner, "ctx", [(0, 2), (3, 1)])
@@ -376,9 +411,9 @@
         ends = lax.ppermute(folded, "ctx", [(1, 3), (2, 0)])
         beside, _ = lax.optimization_barrier((second[0].astype(f16), folded))
         near = lax.ppermute(beside, "ctx", [(0, 1), (1, 0), (2, 3), (3, 2)])
-        total = second[1]
-        for part in (middle, skip, near, ends):
-            total = total + part.astype(f32)
+        total = second[1] + middle.astype(f32) + skip.astype(f32)
+        total, near, ends = lax.optimization_barrier((total, near, ends))
+        total = total + near.astype(f32) + ends.astype(f32)
         return (total * (1.0 / LINK_SCALE)).astype(jnp.bfloat16)
 
     mine = reduced(first, second)
@@ -409,6 +444,7 @@
         out_shape=[jax.ShapeDtypeStruct((1, rows), f32)] * 2,
         in_specs=[smem, smem, smem, smem, vmem],
         out_specs=[vmem, vmem],
+        compiler_params=pltpu.CompilerParams(vmem_limit_bytes=4 * 1024 * 1024),
     )(lengths, prompt_len, reward, where, spread)
     return (kl_term.reshape(rows), objective.reshape(rows))
 

time: 110 us -> 109 us (level)
  local copies, waits for them, and re-layouts: 9.7 us -> 8 us
    dynamic_slice x2 -> x0, local copies, waits for them, and re-layouts: 2.08 us -> none  [the longest x1 1.17 us: split_shards(): piece = lax.dynamic_slice_in_dim(hidden, start, depth, 1)]
    ppermute x1, waiting for transfers between devices: 16 us -> 14.4 us  [reduced(): near = lax.ppermute(beside, 'ctx', [(0, 1), (1, 0), (2, 3), (3, 2)])]
    add x0 -> x1, other arithmetic: none -> 1.58 us  [reduced(): total = second[1] + middle.astype(f32) + skip.astype(f32)]
    unnamed x22 -> x26, local copies, waits for them, and re-layouts: 7.53 us -> 7.83 us
  transfers between devices with their start and end apart: 14 -> 14, of which waited for: 8 -> 8; matrix products, arithmetic and copies ran while one was open for 3% -> 4% of each run, Pallas kernels for 5% -> 5%
where the time goes in v5:
time: 109 us
  waiting for transfers between devices  44.5 us (41%)
  starting transfers between devices  23.2 us (21%)
  Pallas kernels  14.3 us (13%)
  blocking collectives  11.1 us (10%)
  local copies, waits for them, and re-layouts  8 us (7%)
  other arithmetic  6.59 us (6%)
    ppermute x1, waiting for transfers between devices, reduced(): near = lax.ppermute(beside, 'ctx', [(0, 1), (1, 0), (2, 3), (3, 2)])  14.4 us
    ppermute x1, waiting for transfers between devices, reduced(): skip = lax.ppermute(inner, 'ctx', [(0, 2), (3, 1)])  12 us
    all_to_all x1, blocking collectives, split_shards(): spread = lax.all_to_all(sums, ('ctx', 'sec', 'tp'), 0, 0, tiled=True)  11.1 us
    pallas_call x3, Pallas kernels, partial_call(): pl.pallas_call(kernel, out_shape=[jax.ShapeDtypeStruct(shape, jnp.float32...  8.9 us
    unnamed x26, local copies, waits for them, and re-layouts  7.83 us
    ppermute x3, starting transfers between devices, split_shards(): sent[step] = lax.ppermute(piece, 'ctx', pairs)  7.49 us
    ppermute x1, waiting for transfers between devices, reduced(): fold = lax.ppermute(far, 'ctx', [(0, 1), (3, 2)])  6.95 us
    ppermute x1, waiting for transfers between devices, reduced(): ends = lax.ppermute(folded, 'ctx', [(1, 3), (2, 0)])  6.41 us
  transfers between devices with their start and end apart: 14, of which 8 were waited for; matrix products, arithmetic and copies ran while one was open for 4% of the time, Pallas kernels for 5%

profile of v5, /device:TPU:0, one launch (start us, length us, event | category | flops | bytes accessed | tf_op | source)
XLA Modules:
  0.0 108.6 jit_solution(7381658756375784216)
XLA Ops:
  0.7 0.1 stack.69.plan
  0.8 1.2 %copy-done.8 = bf16[64,8192]{1,0:T(8,128)(2,1)S(1)} copy-done((bf16[64,8192]{1,0:T(8,128)(2,1)S(1)}, bf16[64,8192]{1,0:T(8,128)(2,1)}, u32[]{:S(2)}) %copy-start.8) | copy-done | bytes 1048600
  2.0 0.7 shard_map.95
  2.7 0.5 collective-permute-start.1
  3.2 3.7 %collective-permute-start = (bf16[32,2048]{1,0:T(8,128)(2,1)S(1)}, bf16[32,2048]{1,0:T(8,128)(2,1)S(1)}, u32[]{:S(2)}, u32[]{:S(2)}) collective-permute-start(bf16[32,2048]{1,0:T(8,128)(2,1)S(1)} %get-tuple-element.20), channel_id=1, source_target_pairs={{0,8},{4,12},{8,0},{12,4},{1,9},{5,13},{9,1},{13,5},{2,10},{6,14},... | collective-permute-start | bytes 393224 | tf_op jit(solution)/shard_map/ppermute | solution.py:360
  6.9 1.6 %collective-permute-start.3 = (bf16[64,2048]{1,0:T(8,128)(2,1)S(1)}, bf16[64,2048]{1,0:T(8,128)(2,1)S(1)}, u32[]{:S(2)}, u32[]{:S(2)}) collective-permute-start(bf16[64,2048]{1,0:T(8,128)(2,1)S(1)} %get-tuple-element.23), channel_id=1, source_target_pairs={{0,4},{4,8},{8,12},{12,0},{1,5},{5,9},{9,13},{13,1},{2,6},{6,10},{... | collective-permute-start | bytes 786440 | tf_op jit(solution)/shard_map/ppermute | solution.py:360
  8.4 2.2 %collective-permute-start.4 = (bf16[64,2048]{1,0:T(8,128)(2,1)S(1)}, bf16[64,2048]{1,0:T(8,128)(2,1)S(1)}, u32[]{:S(2)}, u32[]{:S(2)}) collective-permute-start(bf16[64,2048]{1,0:T(8,128)(2,1)S(1)} %get-tuple-element.24), channel_id=1, source_target_pairs={{0,12},{4,0},{8,4},{12,8},{1,13},{5,1},{9,5},{13,9},{2,14},{6,2},{... | collective-permute-start | bytes 786440 | tf_op jit(solution)/shard_map/ppermute | solution.py:360
  10.7 0.1 stack.64.refs_0_
  10.8 0.0 copy-start
  10.8 3.4 %copy-done = bf16[1,2048,2048]{2,1,0:T(8,128)(2,1)S(1)} copy-done((bf16[1,2048,2048]{2,1,0:T(8,128)(2,1)S(1)}, bf16[1,2048,2048]{2,1,0:T(8,128)(2,1)}, u32[]{:S(2)}) %copy-start) | copy-done | bytes 8388632
  14.2 1.6 %copy-done.2 = bf16[1,2048,512]{2,1,0:T(8,128)(2,1)S(1)} copy-done((bf16[1,2048,512]{2,1,0:T(8,128)(2,1)S(1)}, bf16[1,2048,512]{2,1,0:T(8,128)(2,1)}, u32[]{:S(2)}) %copy-start.2) | copy-done | bytes 2097176
  15.8 1.6 %copy-done.4 = bf16[1,2048,512]{2,1,0:T(8,128)(2,1)S(1)} copy-done((bf16[1,2048,512]{2,1,0:T(8,128)(2,1)S(1)}, bf16[1,2048,512]{2,1,0:T(8,128)(2,1)}, u32[]{:S(2)}) %copy-start.4) | copy-done | bytes 2097176
  17.3 2.4 %shard_map.96.refs_9_ = f32[4,128,768]{2,1,0:T(8,128)S(1)} custom-call(s32[9]{0:T(128)S(1)} %stack.64.refs_0_, bf16[64,2048]{1,0:T(8,128)(2,1)S(1)} %get-tuple-element.21.refs_1_, bf16[64,2048]{1,0:T(8,128)(2,1)S(1)} %collective-permute-done.1.refs_2_, bf16[1,2048,2048]{2,1,0:T(8,128)(2,1)S(1)} %copy-done, bf16[1,2048,512]{2,1,0:T(8,128)(2,1)S(1)} %copy-done.2, ...), custom_call_target="tpu_custom_call" | custom-call | flops 1610612736 | bytes 14680064 | tf_op jit(solution)/shard_map/pallas_call | solution.py:313
  19.8 1.7 %collective-permute-start.5 = (bf16[32,2048]{1,0:T(8,128)(2,1)S(1)}, bf16[32,2048]{1,0:T(8,128)(2,1)S(1)}, u32[]{:S(2)}, u32[]{:S(2)}) collective-permute-start(bf16[32,2048]{1,0:T(8,128)(2,1)S(1)} %collective-permute-done.refs_1_), channel_id=1, source_target_pairs={{0,1},{1,0},{2,3},{3,2},{4,5},{5,4},{6,7},{7,6},{8,9},{9,8},{10,11... | collective-permute-start | bytes 393224 | tf_op jit(solution)/shard_map/ppermute | solution.py:23
  21.4 0.0 collective-permute-done.3.refs_5_
  21.4 2.3 %collective-permute-done.4.refs_7_ = bf16[64,2048]{1,0:T(8,128)(2,1)S(1)} collective-permute-done((bf16[64,2048]{1,0:T(8,128)(2,1)S(1)}, bf16[64,2048]{1,0:T(8,128)(2,1)S(1)}, u32[]{:S(2)}, u32[]{:S(2)}) %collective-permute-start.4) | collective-permute-done | bytes 262176 | tf_op jit(solution)/shard_map/ppermute | solution.py:360
  23.8 1.1 collective-permute-done.5.refs_3_
  24.8 0.5 collective-permute-start.8
  25.4 0.0 collective-permute-start.2
  25.4 0.5 collective-permute-start.6
  25.9 1.1 collective-permute-done.2.refs_2_
  26.9 0.2 collective-permute-done.6.refs_4_
  27.1 0.0 collective-permute-done.7.refs_6_
  27.2 3.2 %shard_map.98 = f32[2,512,768]{2,1,0:T(8,128)S(1)} custom-call(s32[9]{0:T(128)S(1)} %stack.64.refs_0_, bf16[32,2048]{1,0:T(8,128)(2,1)S(1)} %collective-permute-done.refs_1_, bf16[32,2048]{1,0:T(8,128)(2,1)S(1)} %collective-permute-done.2.refs_2_, bf16[32,2048]{1,0:T(8,128)(2,1)S(1)} %collective-permute-done.5.refs_3_, ...), custom_call_target="tpu_custom_call" | custom-call | flops 2415919104 | bytes 10223616 | tf_op jit(solution)/shard_map/pallas_call | solution.py:313
  30.4 0.1 fusion.3
  30.5 3.1 %collective-permute-start.11 = (f16[512,768]{1,0:T(8,128)(2,1)S(1)}, f16[512,768]{1,0:T(8,128)(2,1)S(1)}, u32[]{:S(2)}, u32[]{:S(2)}) collective-permute-start(f16[512,768]{1,0:T(8,128)(2,1)S(1)} %fusion.3), channel_id=1, source_target_pairs={{0,4},{12,8},{1,5},{13,9},{2,6},{14,10},{3,7},{15,11},{16,20},{28,... | collective-permute-start | bytes 2359304 | tf_op jit(solution)/shard_map/ppermute | solution.py:406
  33.6 1.0 fusion.4
  34.6 4.1 %collective-permute-start.10 = (f16[512,768]{1,0:T(8,128)(2,1)}, f16[512,768]{1,0:T(8,128)(2,1)}, u32[]{:S(2)}, u32[]{:S(2)}) collective-permute-start(f16[512,768]{1,0:T(8,128)(2,1)} %fusion.4), channel_id=1, source_target_pairs={{0,8},{12,4},{1,9},{13,5},{2,10},{14,6},{3,11},{15,7},{16,24},{28,... | collective-permute-start | bytes 2359304 | tf_op jit(solution)/shard_map/ppermute | solution.py:409
  38.7 1.6 %collective-permute-start.9 = (f16[512,768]{1,0:T(8,128)(2,1)}, f16[512,768]{1,0:T(8,128)(2,1)}, u32[]{:S(2)}, u32[]{:S(2)}) collective-permute-start(f16[512,768]{1,0:T(8,128)(2,1)} %fusion.4), channel_id=1, source_target_pairs={{4,8},{8,4},{5,9},{9,5},{6,10},{10,6},{7,11},{11,7},{20,24},{24,20... | collective-permute-start | bytes 2359304 | tf_op jit(solution)/shard_map/ppermute | solution.py:408
  40.3 3.2 %shard_map.97 = f32[2,512,768]{2,1,0:T(8,128)S(1)} custom-call(s32[9]{0:T(128)S(1)} %stack.64.refs_0_, bf16[32,2048]{1,0:T(8,128)(2,1)S(1)} %collective-permute-done.refs_1_, bf16[32,2048]{1,0:T(8,128)(2,1)S(1)} %collective-permute-done.2.refs_2_, bf16[32,2048]{1,0:T(8,128)(2,1)S(1)} %collective-permute-done.5.refs_3_, ...), custom_call_target="tpu_custom_call" | custom-call | flops 2415919104 | bytes 10223616 | tf_op jit(solution)/shard_map/pallas_call | solution.py:313
  43.5 1.0 fusion.5
  44.5 7.0 %collective-permute-done.11 = f16[512,768]{1,0:T(8,128)(2,1)S(1)} collective-permute-done((f16[512,768]{1,0:T(8,128)(2,1)S(1)}, f16[512,768]{1,0:T(8,128)(2,1)S(1)}, u32[]{:S(2)}, u32[]{:S(2)}) %collective-permute-start.11) | collective-permute-done | bytes 786464 | tf_op jit(solution)/shard_map/ppermute | solution.py:406
  51.5 1.1 %fusion.2 = f16[512,768]{1,0:T(8,128)(2,1)} fusion(f16[512,768]{1,0:T(8,128)(2,1)S(1)} %collective-permute-done.11, f32[2,512,768]{2,1,0:T(8,128)S(1)} %shard_map.98), kind=kLoop, calls=%fused_computation.7 | loop fusion | flops 1179648 | bytes 3145728 | tf_op jit(solution)/shard_map/convert_element_type | solution.py:410
  52.6 2.5 %collective-permute-start.12 = (f16[512,768]{1,0:T(8,128)(2,1)}, f16[512,768]{1,0:T(8,128)(2,1)}, u32[]{:S(2)}, u32[]{:S(2)}) collective-permute-start(f16[512,768]{1,0:T(8,128)(2,1)} %fusion.5), channel_id=1, source_target_pairs={{0,4},{4,0},{8,12},{12,8},{1,5},{5,1},{9,13},{13,9},{2,6},{6,2},{1... | collective-permute-start | bytes 2359304 | tf_op jit(solution)/shard_map/ppermute | solution.py:413
  55.1 1.3 %collective-permute-start.13 = (f16[512,768]{1,0:T(8,128)(2,1)}, f16[512,768]{1,0:T(8,128)(2,1)}, u32[]{:S(2)}, u32[]{:S(2)}) collective-permute-start(f16[512,768]{1,0:T(8,128)(2,1)} %fusion.2), channel_id=1, source_target_pairs={{4,12},{8,0},{5,13},{9,1},{6,14},{10,2},{7,15},{11,3},{20,28},{24,... | collective-permute-start | bytes 2359304 | tf_op jit(solution)/shard_map/ppermute | solution.py:411
  56.4 0.1 pad_add_fusion.plan.refs_1_.where
  56.5 12.0 %collective-permute-done.10 = f16[512,768]{1,0:T(8,128)(2,1)} collective-permute-done((f16[512,768]{1,0:T(8,128)(2,1)}, f16[512,768]{1,0:T(8,128)(2,1)}, u32[]{:S(2)}, u32[]{:S(2)}) %collective-permute-start.10) | collective-permute-done | bytes 786464 | tf_op jit(solution)/shard_map/ppermute | solution.py:409
  68.5 1.6 %fusion.1 = f32[512,768]{1,0:T(8,128)S(1)} fusion(f32[2,512,768]{2,1,0:T(8,128)S(1)} %shard_map.97, f16[512,768]{1,0:T(8,128)(2,1)} %collective-permute-done.10, f16[512,768]{1,0:T(8,128)(2,1)} %collective-permute-done.9), kind=kLoop, calls=%fused_computation.5 | loop fusion | flops 1572864 | bytes 4718592 | tf_op jit(solution)/shard_map/add | solution.py:414
  70.1 0.0 copy-start.9
  70.1 0.0 copy-start.10
  70.1 0.0 copy-start.11
  70.1 0.0 copy-start.12
  70.1 14.4 %collective-permute-done.12 = f16[512,768]{1,0:T(8,128)(2,1)} collective-permute-done((f16[512,768]{1,0:T(8,128)(2,1)}, f16[512,768]{1,0:T(8,128)(2,1)}, u32[]{:S(2)}, u32[]{:S(2)}) %collective-permute-start.12) | collective-permute-done | bytes 786464 | tf_op jit(solution)/shard_map/ppermute | solution.py:413
  84.5 6.4 %collective-permute-done.13 = f16[512,768]{1,0:T(8,128)(2,1)} collective-permute-done((f16[512,768]{1,0:T(8,128)(2,1)}, f16[512,768]{1,0:T(8,128)(2,1)}, u32[]{:S(2)}, u32[]{:S(2)}) %collective-permute-start.13) | collective-permute-done | bytes 786464 | tf_op jit(solution)/shard_map/ppermute | solution.py:411
  90.9 1.7 %multiply_convert_fusion.refs_2_ = bf16[512,768]{1,0:T(8,128)(2,1)S(1)} fusion(f16[512,768]{1,0:T(8,128)(2,1)} %collective-permute-done.13, f32[512,768]{1,0:T(8,128)S(1)} %fusion.1, f16[512,768]{1,0:T(8,128)(2,1)} %collective-permute-done.12), kind=kLoop, calls=%fused_computation.8 | loop fusion | flops 2359296 | bytes 3932160 | tf_op jit(solution)/shard_map/convert_element_type | solution.py:417
  92.7 3.6 %shard_map.99 = f32[16,1,128]{2,1,0:T(1,128)S(1)} custom-call(s32[2]{0:T(128)S(1)} %pad_add_fusion.plan.refs_1_.where, s32[4]{0:T(128)S(1)} %copy-done.10, s32[2]{0:T(128)S(1)} %pad_add_fusion.plan.refs_1_.where, bf16[512,768]{1,0:T(8,128)(2,1)S(1)} %multiply_convert_fusion.refs_2_, bf16[1,2048]{1,0:T(2,128)(2,1)S(1)} %copy-done.9), custom_call_target="tpu_custom_call" | custom-call | tf_op jit(solution)/shard_map/pallas_call | solution.py:423
  96.3 11.1 %all_to_all.5.parts = f32[16,1,128]{2,1,0:T(1,128)S(1)} all-to-all(f32[16,1,128]{2,1,0:T(1,128)S(1)} %shard_map.99), channel_id=1, replica_groups=mesh['grp'=2,'ctx'=4,'sec'=2,'tp'=2] {'ctx','sec','tp'}, dimensions={0} | all-to-all | bytes 16384 | tf_op jit(solution)/shard_map/all_to_all | solution.py:440
  107.4 1.2 %shard_map.100 = (f32[1,64]{1,0:T(1,128)}, f32[1,64]{1,0:T(1,128)}) custom-call(s32[4]{0:T(128)S(1)} %copy-done.10, s32[4]{0:T(128)S(1)} %copy-done.11, f32[4]{0:T(128)S(1)} %copy-done.12, s32[2]{0:T(128)S(1)} %pad_add_fusion.plan.refs_1_.where, f32[16,1,128]{2,1,0:T(1,128)S(1)} %all_to_all.5.parts), custom_call_target="tpu_custom_call" | custom-call | tf_op jit(solution)/shard_map/pallas_call | solution.py:442
  (22 shorter events, 0.0 us)
Async XLA Ops:
  0.8 1.2 %copy-start.8 = (bf16[64,8192]{1,0:T(8,128)(2,1)S(1)}, bf16[64,8192]{1,0:T(8,128)(2,1)}, u32[]{:S(2)}) copy-start(bf16[64,8192]{1,0:T(8,128)(2,1)} %hidden.1) | copy-start | bytes 3145732
  2.7 8.1 %collective-permute-start.1 = (bf16[64,2048]{1,0:T(8,128)(2,1)S(1)}, bf16[64,2048]{1,0:T(8,128)(2,1)S(1)}, u32[]{:S(2)}, u32[]{:S(2)}) collective-permute-start(bf16[64,2048]{1,0:T(8,128)(2,1)S(1)} %get-tuple-element.21.refs_1_), channel_id=1, source_target_pairs={{0,2},{2,0},{1,3},{3,1},{4,6},{6,4},{5,7},{7,5},{8,10},{10,8},{9,1... | collective-permute-start | bytes 786440 | tf_op jit(solution)/shard_map/ppermute | solution.py:23
  3.2 16.6 %collective-permute-start = (bf16[32,2048]{1,0:T(8,128)(2,1)S(1)}, bf16[32,2048]{1,0:T(8,128)(2,1)S(1)}, u32[]{:S(2)}, u32[]{:S(2)}) collective-permute-start(bf16[32,2048]{1,0:T(8,128)(2,1)S(1)} %get-tuple-element.20), channel_id=1, source_target_pairs={{0,8},{4,12},{8,0},{12,4},{1,9},{5,13},{9,1},{13,5},{2,10},{6,14},... | collective-permute-start | bytes 393224 | tf_op jit(solution)/shard_map/ppermute | solution.py:360
  6.9 14.6 %collective-permute-start.3 = (bf16[64,2048]{1,0:T(8,128)(2,1)S(1)}, bf16[64,2048]{1,0:T(8,128)(2,1)S(1)}, u32[]{:S(2)}, u32[]{:S(2)}) collective-permute-start(bf16[64,2048]{1,0:T(8,128)(2,1)S(1)} %get-tuple-element.23), channel_id=1, source_target_pairs={{0,4},{4,8},{8,12},{12,0},{1,5},{5,9},{9,13},{13,1},{2,6},{6,10},{... | collective-permute-start | bytes 786440 | tf_op jit(solution)/shard_map/ppermute | solution.py:360
  8.4 15.3 %collective-permute-start.4 = (bf16[64,2048]{1,0:T(8,128)(2,1)S(1)}, bf16[64,2048]{1,0:T(8,128)(2,1)S(1)}, u32[]{:S(2)}, u32[]{:S(2)}) collective-permute-start(bf16[64,2048]{1,0:T(8,128)(2,1)S(1)} %get-tuple-element.24), channel_id=1, source_target_pairs={{0,12},{4,0},{8,4},{12,8},{1,13},{5,1},{9,5},{13,9},{2,14},{6,2},{... | collective-permute-start | bytes 786440 | tf_op jit(solution)/shard_map/ppermute | solution.py:360
  10.8 3.4 %copy-start = (bf16[1,2048,2048]{2,1,0:T(8,128)(2,1)S(1)}, bf16[1,2048,2048]{2,1,0:T(8,128)(2,1)}, u32[]{:S(2)}) copy-start(bf16[1,2048,2048]{2,1,0:T(8,128)(2,1)} %refs_10_.3) | copy-start | bytes 25165828
  14.2 1.6 %copy-start.2 = (bf16[1,2048,512]{2,1,0:T(8,128)(2,1)S(1)}, bf16[1,2048,512]{2,1,0:T(8,128)(2,1)}, u32[]{:S(2)}) copy-start(bf16[1,2048,512]{2,1,0:T(8,128)(2,1)} %refs_11_.3) | copy-start | bytes 6291460
  15.7 1.6 %copy-start.4 = (bf16[1,2048,512]{2,1,0:T(8,128)(2,1)S(1)}, bf16[1,2048,512]{2,1,0:T(8,128)(2,1)}, u32[]{:S(2)}) copy-start(bf16[1,2048,512]{2,1,0:T(8,128)(2,1)} %refs_12_.3) | copy-start | bytes 6291460
  17.3 9.8 %copy-start.1 = (bf16[1,2048,2048]{2,1,0:T(8,128)(2,1)S(1)}, bf16[1,2048,2048]{2,1,0:T(8,128)(2,1)}, u32[]{:S(2)}) copy-start(bf16[1,2048,2048]{2,1,0:T(8,128)(2,1)} %refs_10_.3) | copy-start | bytes 25165828
  17.3 9.8 %copy-start.3 = (bf16[1,2048,512]{2,1,0:T(8,128)(2,1)S(1)}, bf16[1,2048,512]{2,1,0:T(8,128)(2,1)}, u32[]{:S(2)}) copy-start(bf16[1,2048,512]{2,1,0:T(8,128)(2,1)} %refs_11_.3) | copy-start | bytes 6291460
  17.3 9.8 %copy-start.5 = (bf16[1,2048,512]{2,1,0:T(8,128)(2,1)S(1)}, bf16[1,2048,512]{2,1,0:T(8,128)(2,1)}, u32[]{:S(2)}) copy-start(bf16[1,2048,512]{2,1,0:T(8,128)(2,1)} %refs_12_.3) | copy-start | bytes 6291460
  19.8 5.1 %collective-permute-start.5 = (bf16[32,2048]{1,0:T(8,128)(2,1)S(1)}, bf16[32,2048]{1,0:T(8,128)(2,1)S(1)}, u32[]{:S(2)}, u32[]{:S(2)}) collective-permute-start(bf16[32,2048]{1,0:T(8,128)(2,1)S(1)} %collective-permute-done.refs_1_), channel_id=1, source_target_pairs={{0,1},{1,0},{2,3},{3,2},{4,5},{5,4},{6,7},{7,6},{8,9},{9,8},{10,11... | collective-permute-start | bytes 393224 | tf_op jit(solution)/shard_map/ppermute | solution.py:23
  23.8 6.6 %copy-start.6 = (bf16[64,2048]{1,0:T(8,128)(2,1)}, bf16[64,2048]{1,0:T(8,128)(2,1)S(1)}, u32[]{:S(2)}) copy-start(bf16[64,2048]{1,0:T(8,128)(2,1)S(1)} %collective-permute-done.4.refs_7_) | copy-start | bytes 786436
  24.8 2.3 %collective-permute-start.7 = (bf16[64,2048]{1,0:T(8,128)(2,1)S(1)}, bf16[64,2048]{1,0:T(8,128)(2,1)S(1)}, u32[]{:S(2)}, u32[]{:S(2)}) collective-permute-start(bf16[64,2048]{1,0:T(8,128)(2,1)S(1)} %collective-permute-done.3.refs_5_), channel_id=1, source_target_pairs={{0,2},{2,0},{1,3},{3,1},{4,6},{6,4},{5,7},{7,5},{8,10},{10,8},{9,1... | collective-permute-start | bytes 786440 | tf_op jit(solution)/shard_map/ppermute | solution.py:23
  24.8 2.3 %collective-permute-start.8 = (bf16[64,2048]{1,0:T(8,128)(2,1)S(1)}, bf16[64,2048]{1,0:T(8,128)(2,1)S(1)}, u32[]{:S(2)}, u32[]{:S(2)}) collective-permute-start(bf16[64,2048]{1,0:T(8,128)(2,1)S(1)} %collective-permute-done.4.refs_7_), channel_id=1, source_target_pairs={{0,2},{2,0},{1,3},{3,1},{4,6},{6,4},{5,7},{7,5},{8,10},{10,8},{9,1... | collective-permute-start | bytes 786440 | tf_op jit(solution)/shard_map/ppermute | solution.py:23
  25.4 1.6 %collective-permute-start.2 = (bf16[32,2048]{1,0:T(8,128)(2,1)S(1)}, bf16[32,2048]{1,0:T(8,128)(2,1)S(1)}, u32[]{:S(2)}, u32[]{:S(2)}) collective-permute-start(bf16[32,2048]{1,0:T(8,128)(2,1)S(1)} %collective-permute-done.refs_1_), channel_id=1, source_target_pairs={{0,2},{2,0},{1,3},{3,1},{4,6},{6,4},{5,7},{7,5},{8,10},{10,8},{9,1... | collective-permute-start | bytes 393224 | tf_op jit(solution)/shard_map/ppermute | solution.py:23
  25.4 1.8 %collective-permute-start.6 = (bf16[32,2048]{1,0:T(8,128)(2,1)S(1)}, bf16[32,2048]{1,0:T(8,128)(2,1)S(1)}, u32[]{:S(2)}, u32[]{:S(2)}) collective-permute-start(bf16[32,2048]{1,0:T(8,128)(2,1)S(1)} %collective-permute-done.5.refs_3_), channel_id=1, source_target_pairs={{0,2},{2,0},{1,3},{3,1},{4,6},{6,4},{5,7},{7,5},{8,10},{10,8},{9,1... | collective-permute-start | bytes 393224 | tf_op jit(solution)/shard_map/ppermute | solution.py:23
  30.5 9.8 %copy-start.7 = (bf16[64,2048]{1,0:T(8,128)(2,1)S(1)}, bf16[64,2048]{1,0:T(8,128)(2,1)}, u32[]{:S(2)}) copy-start(bf16[64,2048]{1,0:T(8,128)(2,1)} %copy-done.6) | copy-start | bytes 786436
  30.5 20.9 %collective-permute-start.11 = (f16[512,768]{1,0:T(8,128)(2,1)S(1)}, f16[512,768]{1,0:T(8,128)(2,1)S(1)}, u32[]{:S(2)}, u32[]{:S(2)}) collective-permute-start(f16[512,768]{1,0:T(8,128)(2,1)S(1)} %fusion.3), channel_id=1, source_target_pairs={{0,4},{12,8},{1,5},{13,9},{2,6},{14,10},{3,7},{15,11},{16,20},{28,... | collective-permute-start | bytes 2359304 | tf_op jit(solution)/shard_map/ppermute | solution.py:406
  34.6 33.9 %collective-permute-start.10 = (f16[512,768]{1,0:T(8,128)(2,1)}, f16[512,768]{1,0:T(8,128)(2,1)}, u32[]{:S(2)}, u32[]{:S(2)}) collective-permute-start(f16[512,768]{1,0:T(8,128)(2,1)} %fusion.4), channel_id=1, source_target_pairs={{0,8},{12,4},{1,9},{13,5},{2,10},{14,6},{3,11},{15,7},{16,24},{28,... | collective-permute-start | bytes 2359304 | tf_op jit(solution)/shard_map/ppermute | solution.py:409
  38.7 29.8 %collective-permute-start.9 = (f16[512,768]{1,0:T(8,128)(2,1)}, f16[512,768]{1,0:T(8,128)(2,1)}, u32[]{:S(2)}, u32[]{:S(2)}) collective-permute-start(f16[512,768]{1,0:T(8,128)(2,1)} %fusion.4), channel_id=1, source_target_pairs={{4,8},{8,4},{5,9},{9,5},{6,10},{10,6},{7,11},{11,7},{20,24},{24,20... | collective-permute-start | bytes 2359304 | tf_op jit(solution)/shard_map/ppermute | solution.py:408
  52.6 31.9 %collective-permute-start.12 = (f16[512,768]{1,0:T(8,128)(2,1)}, f16[512,768]{1,0:T(8,128)(2,1)}, u32[]{:S(2)}, u32[]{:S(2)}) collective-permute-start(f16[512,768]{1,0:T(8,128)(2,1)} %fusion.5), channel_id=1, source_target_pairs={{0,4},{4,0},{8,12},{12,8},{1,5},{5,1},{9,13},{13,9},{2,6},{6,2},{1... | collective-permute-start | bytes 2359304 | tf_op jit(solution)/shard_map/ppermute | solution.py:413
  55.1 35.8 %collective-permute-start.13 = (f16[512,768]{1,0:T(8,128)(2,1)}, f16[512,768]{1,0:T(8,128)(2,1)}, u32[]{:S(2)}, u32[]{:S(2)}) collective-permute-start(f16[512,768]{1,0:T(8,128)(2,1)} %fusion.2), channel_id=1, source_target_pairs={{4,12},{8,0},{5,13},{9,1},{6,14},{10,2},{7,15},{11,3},{20,28},{24,... | collective-permute-start | bytes 2359304 | tf_op jit(solution)/shard_map/ppermute | solution.py:411
  70.1 22.6 %copy-start.9 = (bf16[1,2048]{1,0:T(2,128)(2,1)S(1)}, bf16[1,2048]{1,0:T(2,128)(2,1)}, u32[]{:S(2)}) copy-start(bf16[1,2048]{1,0:T(2,128)(2,1)} %refs_3_.3) | copy-start | bytes 12292
  70.1 22.6 %copy-start.10 = (s32[4]{0:T(128)S(1)}, s32[4]{0:T(128)}, u32[]{:S(2)}) copy-start(s32[4]{0:T(128)} %lengths.1) | copy-start | bytes 52
  70.1 37.3 %copy-start.11 = (s32[4]{0:T(128)S(1)}, s32[4]{0:T(128)}, u32[]{:S(2)}) copy-start(s32[4]{0:T(128)} %prompt_len.1) | copy-start | bytes 52
  70.1 37.3 %copy-start.12 = (f32[4]{0:T(128)S(1)}, f32[4]{0:T(128)}, u32[]{:S(2)}) copy-start(f32[4]{0:T(128)} %reward.1) | copy-start | bytes 52

commit v6 on v5

--- a/solution.py
+++ b/solution.py
@@ -336,7 +336,7 @@
     count = 4
     f16, f32 = jnp.float16, jnp.float32
 
-    steps = (2, 1, 3)
+    steps = (2, 3, 1)
     half_rows = rows // 2
     targets = [(ctx + step) % count for step in (*steps, 0)]
     cuts = pl.pallas_call(
@@ -412,8 +412,9 @@
         beside, _ = lax.optimization_barrier((second[0].astype(f16), folded))
         near = lax.ppermute(beside, "ctx", [(0, 1), (1, 0), (2, 3), (3, 2)])
         total = second[1] + middle.astype(f32) + skip.astype(f32)
-        total, near, ends = lax.optimization_barrier((total, near, ends))
-        total = total + near.astype(f32) + ends.astype(f32)
+        total, near = lax.optimization_barrier((total, near))
+        total, ends = lax.optimization_barrier((total + near.astype(f32), ends))
+        total = total + ends.astype(f32)
         return (total * (1.0 / LINK_SCALE)).astype(jnp.bfloat16)
 
     mine = reduced(first, second)

time: 109 us -> 109 us (level)
  waiting for transfers between devices: 44.5 us -> 43.2 us
    ppermute x1, waiting for transfers between devices: 6.41 us -> 5.07 us  [reduced(): ends = lax.ppermute(folded, 'ctx', [(1, 3), (2, 0)])]
    add x0 -> x1, other arithmetic: none -> 1.29 us  [reduced(): total, ends = lax.optimization_barrier((total + near.astype(f32), ends))]
  transfers between devices with their start and end apart: 14 -> 14, of which waited for: 8 -> 8; matrix products, arithmetic and copies ran while one was open for 4% -> 6% of each run, Pallas kernels for 5% -> 5%
where the time goes in v6:
time: 109 us; the launch traced here: 108 us
  waiting for transfers between devices  43.2 us (40%)
  starting transfers between devices  23.2 us (21%)
  Pallas kernels  14.3 us (13%)
  blocking collectives  11.1 us (10%)
  local copies, waits for them, and re-layouts  8 us (7%)
  other arithmetic  7.46 us (7%)
    ppermute x1, waiting for transfers between devices, reduced(): near = lax.ppermute(beside, 'ctx', [(0, 1), (1, 0), (2, 3), (3, 2)])  14.5 us
    ppermute x1, waiting for transfers between devices, reduced(): skip = lax.ppermute(inner, 'ctx', [(0, 2), (3, 1)])  12 us
    all_to_all x1, blocking collectives, split_shards(): spread = lax.all_to_all(sums, ('ctx', 'sec', 'tp'), 0, 0, tiled=True)  11.1 us
    pallas_call x3, Pallas kernels, partial_call(): pl.pallas_call(kernel, out_shape=[jax.ShapeDtypeStruct(shape, jnp.float32...  8.9 us
    unnamed x26, local copies, waits for them, and re-layouts  7.83 us
    ppermute x3, starting transfers between devices, split_shards(): sent[step] = lax.ppermute(piece, 'ctx', pairs)  7.49 us
    ppermute x1, waiting for transfers between devices, reduced(): fold = lax.ppermute(far, 'ctx', [(0, 1), (3, 2)])  6.96 us
    ppermute x1, waiting for transfers between devices, reduced(): ends = lax.ppermute(folded, 'ctx', [(1, 3), (2, 0)])  5.07 us
  transfers between devices with their start and end apart: 14, of which 8 were waited for; matrix products, arithmetic and copies ran while one was open for 6% of the time, Pallas kernels for 5%

profile of v6, /device:TPU:0, one launch (start us, length us, event | category | flops | bytes accessed | tf_op | source)
XLA Modules:
  0.0 108.2 jit_solution(4122482905004584657)
XLA Ops:
  0.7 0.1 stack.69.plan
  0.8 1.2 %copy-done.8 = bf16[64,8192]{1,0:T(8,128)(2,1)S(1)} copy-done((bf16[64,8192]{1,0:T(8,128)(2,1)S(1)}, bf16[64,8192]{1,0:T(8,128)(2,1)}, u32[]{:S(2)}) %copy-start.8) | copy-done | bytes 1048600
  2.0 0.7 shard_map.95
  2.7 0.5 collective-permute-start.1
  3.2 3.7 %collective-permute-start = (bf16[32,2048]{1,0:T(8,128)(2,1)S(1)}, bf16[32,2048]{1,0:T(8,128)(2,1)S(1)}, u32[]{:S(2)}, u32[]{:S(2)}) collective-permute-start(bf16[32,2048]{1,0:T(8,128)(2,1)S(1)} %get-tuple-element.21), channel_id=1, source_target_pairs={{0,8},{4,12},{8,0},{12,4},{1,9},{5,13},{9,1},{13,5},{2,10},{6,14},... | collective-permute-start | bytes 393224 | tf_op jit(solution)/shard_map/ppermute | solution.py:360
  6.9 1.6 %collective-permute-start.3 = (bf16[64,2048]{1,0:T(8,128)(2,1)S(1)}, bf16[64,2048]{1,0:T(8,128)(2,1)S(1)}, u32[]{:S(2)}, u32[]{:S(2)}) collective-permute-start(bf16[64,2048]{1,0:T(8,128)(2,1)S(1)} %get-tuple-element.24), channel_id=1, source_target_pairs={{0,4},{4,8},{8,12},{12,0},{1,5},{5,9},{9,13},{13,1},{2,6},{6,10},{... | collective-permute-start | bytes 786440 | tf_op jit(solution)/shard_map/ppermute | solution.py:360
  8.4 2.2 %collective-permute-start.4 = (bf16[64,2048]{1,0:T(8,128)(2,1)S(1)}, bf16[64,2048]{1,0:T(8,128)(2,1)S(1)}, u32[]{:S(2)}, u32[]{:S(2)}) collective-permute-start(bf16[64,2048]{1,0:T(8,128)(2,1)S(1)} %get-tuple-element.25), channel_id=1, source_target_pairs={{0,12},{4,0},{8,4},{12,8},{1,13},{5,1},{9,5},{13,9},{2,14},{6,2},{... | collective-permute-start | bytes 786440 | tf_op jit(solution)/shard_map/ppermute | solution.py:360
  10.7 0.1 stack.64.refs_0_
  10.8 0.0 collective-permute-done.1.refs_2_
  10.8 0.0 copy-start
  10.8 3.4 %copy-done = bf16[1,2048,2048]{2,1,0:T(8,128)(2,1)S(1)} copy-done((bf16[1,2048,2048]{2,1,0:T(8,128)(2,1)S(1)}, bf16[1,2048,2048]{2,1,0:T(8,128)(2,1)}, u32[]{:S(2)}) %copy-start) | copy-done | bytes 8388632
  14.2 1.6 %copy-done.2 = bf16[1,2048,512]{2,1,0:T(8,128)(2,1)S(1)} copy-done((bf16[1,2048,512]{2,1,0:T(8,128)(2,1)S(1)}, bf16[1,2048,512]{2,1,0:T(8,128)(2,1)}, u32[]{:S(2)}) %copy-start.2) | copy-done | bytes 2097176
  15.8 1.6 %copy-done.4 = bf16[1,2048,512]{2,1,0:T(8,128)(2,1)S(1)} copy-done((bf16[1,2048,512]{2,1,0:T(8,128)(2,1)S(1)}, bf16[1,2048,512]{2,1,0:T(8,128)(2,1)}, u32[]{:S(2)}) %copy-start.4) | copy-done | bytes 2097176
  17.3 2.4 %shard_map.96.refs_9_ = f32[4,128,768]{2,1,0:T(8,128)S(1)} custom-call(s32[9]{0:T(128)S(1)} %stack.64.refs_0_, bf16[64,2048]{1,0:T(8,128)(2,1)S(1)} %get-tuple-element.22.refs_1_, bf16[64,2048]{1,0:T(8,128)(2,1)S(1)} %collective-permute-done.1.refs_2_, bf16[1,2048,2048]{2,1,0:T(8,128)(2,1)S(1)} %copy-done, bf16[1,2048,512]{2,1,0:T(8,128)(2,1)S(1)} %copy-done.2, ...), custom_call_target="tpu_custom_call" | custom-call | flops 1610612736 | bytes 14680064 | tf_op jit(solution)/shard_map/pallas_call | solution.py:313
  19.8 1.7 %collective-permute-start.5 = (bf16[32,2048]{1,0:T(8,128)(2,1)S(1)}, bf16[32,2048]{1,0:T(8,128)(2,1)S(1)}, u32[]{:S(2)}, u32[]{:S(2)}) collective-permute-start(bf16[32,2048]{1,0:T(8,128)(2,1)S(1)} %collective-permute-done.refs_1_), channel_id=1, source_target_pairs={{0,1},{1,0},{2,3},{3,2},{4,5},{5,4},{6,7},{7,6},{8,9},{9,8},{10,11... | collective-permute-start | bytes 393224 | tf_op jit(solution)/shard_map/ppermute | solution.py:23
  21.4 2.3 %collective-permute-done.4.refs_5_ = bf16[64,2048]{1,0:T(8,128)(2,1)S(1)} collective-permute-done((bf16[64,2048]{1,0:T(8,128)(2,1)S(1)}, bf16[64,2048]{1,0:T(8,128)(2,1)S(1)}, u32[]{:S(2)}, u32[]{:S(2)}) %collective-permute-start.4) | collective-permute-done | bytes 262176 | tf_op jit(solution)/shard_map/ppermute | solution.py:360
  23.8 1.1 collective-permute-done.5.refs_3_
  24.8 0.5 collective-permute-start.8
  25.4 0.0 collective-permute-start.2
  25.4 0.5 collective-permute-start.6
  25.9 1.1 collective-permute-done.2.refs_2_
  26.9 0.2 collective-permute-done.6.refs_4_
  27.2 3.2 %shard_map.98 = f32[2,512,768]{2,1,0:T(8,128)S(1)} custom-call(s32[9]{0:T(128)S(1)} %stack.64.refs_0_, bf16[32,2048]{1,0:T(8,128)(2,1)S(1)} %collective-permute-done.refs_1_, bf16[32,2048]{1,0:T(8,128)(2,1)S(1)} %collective-permute-done.2.refs_2_, bf16[32,2048]{1,0:T(8,128)(2,1)S(1)} %collective-permute-done.5.refs_3_, ...), custom_call_target="tpu_custom_call" | custom-call | flops 2415919104 | bytes 10223616 | tf_op jit(solution)/shard_map/pallas_call | solution.py:313
  30.4 0.1 fusion.3
  30.5 3.1 %collective-permute-start.11 = (f16[512,768]{1,0:T(8,128)(2,1)S(1)}, f16[512,768]{1,0:T(8,128)(2,1)S(1)}, u32[]{:S(2)}, u32[]{:S(2)}) collective-permute-start(f16[512,768]{1,0:T(8,128)(2,1)S(1)} %fusion.3), channel_id=1, source_target_pairs={{0,4},{12,8},{1,5},{13,9},{2,6},{14,10},{3,7},{15,11},{16,20},{28,... | collective-permute-start | bytes 2359304 | tf_op jit(solution)/shard_map/ppermute | solution.py:406
  33.6 1.0 fusion.4
  34.6 4.1 %collective-permute-start.10 = (f16[512,768]{1,0:T(8,128)(2,1)}, f16[512,768]{1,0:T(8,128)(2,1)}, u32[]{:S(2)}, u32[]{:S(2)}) collective-permute-start(f16[512,768]{1,0:T(8,128)(2,1)} %fusion.4), channel_id=1, source_target_pairs={{0,8},{12,4},{1,9},{13,5},{2,10},{14,6},{3,11},{15,7},{16,24},{28,... | collective-permute-start | bytes 2359304 | tf_op jit(solution)/shard_map/ppermute | solution.py:409
  38.7 1.6 %collective-permute-start.9 = (f16[512,768]{1,0:T(8,128)(2,1)}, f16[512,768]{1,0:T(8,128)(2,1)}, u32[]{:S(2)}, u32[]{:S(2)}) collective-permute-start(f16[512,768]{1,0:T(8,128)(2,1)} %fusion.4), channel_id=1, source_target_pairs={{4,8},{8,4},{5,9},{9,5},{6,10},{10,6},{7,11},{11,7},{20,24},{24,20... | collective-permute-start | bytes 2359304 | tf_op jit(solution)/shard_map/ppermute | solution.py:408
  40.3 3.2 %shard_map.97 = f32[2,512,768]{2,1,0:T(8,128)S(1)} custom-call(s32[9]{0:T(128)S(1)} %stack.64.refs_0_, bf16[32,2048]{1,0:T(8,128)(2,1)S(1)} %collective-permute-done.refs_1_, bf16[32,2048]{1,0:T(8,128)(2,1)S(1)} %collective-permute-done.2.refs_2_, bf16[32,2048]{1,0:T(8,128)(2,1)S(1)} %collective-permute-done.5.refs_3_, ...), custom_call_target="tpu_custom_call" | custom-call | flops 2415919104 | bytes 10223616 | tf_op jit(solution)/shard_map/pallas_call | solution.py:313
  43.5 1.0 fusion.5
  44.5 7.0 %collective-permute-done.11 = f16[512,768]{1,0:T(8,128)(2,1)S(1)} collective-permute-done((f16[512,768]{1,0:T(8,128)(2,1)S(1)}, f16[512,768]{1,0:T(8,128)(2,1)S(1)}, u32[]{:S(2)}, u32[]{:S(2)}) %collective-permute-start.11) | collective-permute-done | bytes 786464 | tf_op jit(solution)/shard_map/ppermute | solution.py:406
  51.5 1.1 %fusion.2 = f16[512,768]{1,0:T(8,128)(2,1)} fusion(f16[512,768]{1,0:T(8,128)(2,1)S(1)} %collective-permute-done.11, f32[2,512,768]{2,1,0:T(8,128)S(1)} %shard_map.98), kind=kLoop, calls=%fused_computation.7 | loop fusion | flops 1179648 | bytes 3145728 | tf_op jit(solution)/shard_map/convert_element_type | solution.py:410
  52.6 2.5 %collective-permute-start.12 = (f16[512,768]{1,0:T(8,128)(2,1)}, f16[512,768]{1,0:T(8,128)(2,1)}, u32[]{:S(2)}, u32[]{:S(2)}) collective-permute-start(f16[512,768]{1,0:T(8,128)(2,1)} %fusion.5), channel_id=1, source_target_pairs={{0,4},{4,0},{8,12},{12,8},{1,5},{5,1},{9,13},{13,9},{2,6},{6,2},{1... | collective-permute-start | bytes 2359304 | tf_op jit(solution)/shard_map/ppermute | solution.py:413
  55.1 1.3 %collective-permute-start.13 = (f16[512,768]{1,0:T(8,128)(2,1)}, f16[512,768]{1,0:T(8,128)(2,1)}, u32[]{:S(2)}, u32[]{:S(2)}) collective-permute-start(f16[512,768]{1,0:T(8,128)(2,1)} %fusion.2), channel_id=1, source_target_pairs={{4,12},{8,0},{5,13},{9,1},{6,14},{10,2},{7,15},{11,3},{20,28},{24,... | collective-permute-start | bytes 2359304 | tf_op jit(solution)/shard_map/ppermute | solution.py:411
  56.4 0.1 pad_add_fusion.plan.refs_1_.where
  56.5 12.0 %collective-permute-done.10 = f16[512,768]{1,0:T(8,128)(2,1)} collective-permute-done((f16[512,768]{1,0:T(8,128)(2,1)}, f16[512,768]{1,0:T(8,128)(2,1)}, u32[]{:S(2)}, u32[]{:S(2)}) %collective-permute-start.10) | collective-permute-done | bytes 786464 | tf_op jit(solution)/shard_map/ppermute | solution.py:409
  68.5 1.6 %fusion.1 = f32[512,768]{1,0:T(8,128)S(1)} fusion(f32[2,512,768]{2,1,0:T(8,128)S(1)} %shard_map.97, f16[512,768]{1,0:T(8,128)(2,1)} %collective-permute-done.10, f16[512,768]{1,0:T(8,128)(2,1)} %collective-permute-done.9), kind=kLoop, calls=%fused_computation.5 | loop fusion | flops 1572864 | bytes 4718592 | tf_op jit(solution)/shard_map/add | solution.py:414
  70.1 14.5 %collective-permute-done.12 = f16[512,768]{1,0:T(8,128)(2,1)} collective-permute-done((f16[512,768]{1,0:T(8,128)(2,1)}, f16[512,768]{1,0:T(8,128)(2,1)}, u32[]{:S(2)}, u32[]{:S(2)}) %collective-permute-start.12) | collective-permute-done | bytes 786464 | tf_op jit(solution)/shard_map/ppermute | solution.py:413
  84.5 1.3 %convert_add_fusion = f32[512,768]{1,0:T(8,128)S(1)} fusion(f32[512,768]{1,0:T(8,128)S(1)} %fusion.1, f16[512,768]{1,0:T(8,128)(2,1)} %collective-permute-done.12), kind=kLoop, calls=%fused_computation.9 | loop fusion | flops 786432 | bytes 3932160 | tf_op jit(solution)/shard_map/add | solution.py:416
  85.8 0.0 copy-start.9
  85.8 0.0 copy-start.10
  85.8 0.0 copy-start.11
  85.9 0.0 copy-start.12
  85.9 5.1 %collective-permute-done.13 = f16[512,768]{1,0:T(8,128)(2,1)} collective-permute-done((f16[512,768]{1,0:T(8,128)(2,1)}, f16[512,768]{1,0:T(8,128)(2,1)}, u32[]{:S(2)}, u32[]{:S(2)}) %collective-permute-start.13) | collective-permute-done | bytes 786464 | tf_op jit(solution)/shard_map/ppermute | solution.py:411
  90.9 1.3 %multiply_convert_fusion.refs_2_ = bf16[512,768]{1,0:T(8,128)(2,1)S(1)} fusion(f32[512,768]{1,0:T(8,128)S(1)} %convert_add_fusion, f16[512,768]{1,0:T(8,128)(2,1)} %collective-permute-done.13), kind=kLoop, calls=%fused_computation.8 | loop fusion | flops 1572864 | bytes 3145728 | tf_op jit(solution)/shard_map/convert_element_type | solution.py:418
  92.3 3.6 %shard_map.99 = f32[16,1,128]{2,1,0:T(1,128)S(1)} custom-call(s32[2]{0:T(128)S(1)} %pad_add_fusion.plan.refs_1_.where, s32[4]{0:T(128)S(1)} %copy-done.10, s32[2]{0:T(128)S(1)} %pad_add_fusion.plan.refs_1_.where, bf16[512,768]{1,0:T(8,128)(2,1)S(1)} %multiply_convert_fusion.refs_2_, bf16[1,2048]{1,0:T(2,128)(2,1)S(1)} %copy-done.9), custom_call_target="tpu_custom_call" | custom-call | tf_op jit(solution)/shard_map/pallas_call | solution.py:424
  95.9 11.1 %all_to_all.5.parts = f32[16,1,128]{2,1,0:T(1,128)S(1)} all-to-all(f32[16,1,128]{2,1,0:T(1,128)S(1)} %shard_map.99), channel_id=1, replica_groups=mesh['grp'=2,'ctx'=4,'sec'=2,'tp'=2] {'ctx','sec','tp'}, dimensions={0} | all-to-all | bytes 16384 | tf_op jit(solution)/shard_map/all_to_all | solution.py:441
  107.0 1.2 %shard_map.100 = (f32[1,64]{1,0:T(1,128)}, f32[1,64]{1,0:T(1,128)}) custom-call(s32[4]{0:T(128)S(1)} %copy-done.10, s32[4]{0:T(128)S(1)} %copy-done.11, f32[4]{0:T(128)S(1)} %copy-done.12, s32[2]{0:T(128)S(1)} %pad_add_fusion.plan.refs_1_.where, f32[16,1,128]{2,1,0:T(1,128)S(1)} %all_to_all.5.parts), custom_call_target="tpu_custom_call" | custom-call | tf_op jit(solution)/shard_map/pallas_call | solution.py:443
  (23 shorter events, 0.0 us)
Async XLA Ops:
  0.8 1.2 %copy-start.8 = (bf16[64,8192]{1,0:T(8,128)(2,1)S(1)}, bf16[64,8192]{1,0:T(8,128)(2,1)}, u32[]{:S(2)}) copy-start(bf16[64,8192]{1,0:T(8,128)(2,1)} %hidden.1) | copy-start | bytes 3145732
  2.7 8.1 %collective-permute-start.1 = (bf16[64,2048]{1,0:T(8,128)(2,1)S(1)}, bf16[64,2048]{1,0:T(8,128)(2,1)S(1)}, u32[]{:S(2)}, u32[]{:S(2)}) collective-permute-start(bf16[64,2048]{1,0:T(8,128)(2,1)S(1)} %get-tuple-element.22.refs_1_), channel_id=1, source_target_pairs={{0,2},{2,0},{1,3},{3,1},{4,6},{6,4},{5,7},{7,5},{8,10},{10,8},{9,1... | collective-permute-start | bytes 786440 | tf_op jit(solution)/shard_map/ppermute | solution.py:23
  3.2 16.6 %collective-permute-start = (bf16[32,2048]{1,0:T(8,128)(2,1)S(1)}, bf16[32,2048]{1,0:T(8,128)(2,1)S(1)}, u32[]{:S(2)}, u32[]{:S(2)}) collective-permute-start(bf16[32,2048]{1,0:T(8,128)(2,1)S(1)} %get-tuple-element.21), channel_id=1, source_target_pairs={{0,8},{4,12},{8,0},{12,4},{1,9},{5,13},{9,1},{13,5},{2,10},{6,14},... | collective-permute-start | bytes 393224 | tf_op jit(solution)/shard_map/ppermute | solution.py:360
  6.9 14.6 %collective-permute-start.3 = (bf16[64,2048]{1,0:T(8,128)(2,1)S(1)}, bf16[64,2048]{1,0:T(8,128)(2,1)S(1)}, u32[]{:S(2)}, u32[]{:S(2)}) collective-permute-start(bf16[64,2048]{1,0:T(8,128)(2,1)S(1)} %get-tuple-element.24), channel_id=1, source_target_pairs={{0,4},{4,8},{8,12},{12,0},{1,5},{5,9},{9,13},{13,1},{2,6},{6,10},{... | collective-permute-start | bytes 786440 | tf_op jit(solution)/shard_map/ppermute | solution.py:360
  8.4 15.3 %collective-permute-start.4 = (bf16[64,2048]{1,0:T(8,128)(2,1)S(1)}, bf16[64,2048]{1,0:T(8,128)(2,1)S(1)}, u32[]{:S(2)}, u32[]{:S(2)}) collective-permute-start(bf16[64,2048]{1,0:T(8,128)(2,1)S(1)} %get-tuple-element.25), channel_id=1, source_target_pairs={{0,12},{4,0},{8,4},{12,8},{1,13},{5,1},{9,5},{13,9},{2,14},{6,2},{... | collective-permute-start | bytes 786440 | tf_op jit(solution)/shard_map/ppermute | solution.py:360
  10.8 3.4 %copy-start = (bf16[1,2048,2048]{2,1,0:T(8,128)(2,1)S(1)}, bf16[1,2048,2048]{2,1,0:T(8,128)(2,1)}, u32[]{:S(2)}) copy-start(bf16[1,2048,2048]{2,1,0:T(8,128)(2,1)} %refs_10_.3) | copy-start | bytes 25165828
  14.2 1.6 %copy-start.2 = (bf16[1,2048,512]{2,1,0:T(8,128)(2,1)S(1)}, bf16[1,2048,512]{2,1,0:T(8,128)(2,1)}, u32[]{:S(2)}) copy-start(bf16[1,2048,512]{2,1,0:T(8,128)(2,1)} %refs_11_.3) | copy-start | bytes 6291460
  15.7 1.6 %copy-start.4 = (bf16[1,2048,512]{2,1,0:T(8,128)(2,1)S(1)}, bf16[1,2048,512]{2,1,0:T(8,128)(2,1)}, u32[]{:S(2)}) copy-start(bf16[1,2048,512]{2,1,0:T(8,128)(2,1)} %refs_12_.3) | copy-start | bytes 6291460
  17.3 9.8 %copy-start.1 = (bf16[1,2048,2048]{2,1,0:T(8,128)(2,1)S(1)}, bf16[1,2048,2048]{2,1,0:T(8,128)(2,1)}, u32[]{:S(2)}) copy-start(bf16[1,2048,2048]{2,1,0:T(8,128)(2,1)} %refs_10_.3) | copy-start | bytes 25165828
  17.3 9.8 %copy-start.3 = (bf16[1,2048,512]{2,1,0:T(8,128)(2,1)S(1)}, bf16[1,2048,512]{2,1,0:T(8,128)(2,1)}, u32[]{:S(2)}) copy-start(bf16[1,2048,512]{2,1,0:T(8,128)(2,1)} %refs_11_.3) | copy-start | bytes 6291460
  17.3 9.8 %copy-start.5 = (bf16[1,2048,512]{2,1,0:T(8,128)(2,1)S(1)}, bf16[1,2048,512]{2,1,0:T(8,128)(2,1)}, u32[]{:S(2)}) copy-start(bf16[1,2048,512]{2,1,0:T(8,128)(2,1)} %refs_12_.3) | copy-start | bytes 6291460
  19.8 5.1 %collective-permute-start.5 = (bf16[32,2048]{1,0:T(8,128)(2,1)S(1)}, bf16[32,2048]{1,0:T(8,128)(2,1)S(1)}, u32[]{:S(2)}, u32[]{:S(2)}) collective-permute-start(bf16[32,2048]{1,0:T(8,128)(2,1)S(1)} %collective-permute-done.refs_1_), channel_id=1, source_target_pairs={{0,1},{1,0},{2,3},{3,2},{4,5},{5,4},{6,7},{7,6},{8,9},{9,8},{10,11... | collective-permute-start | bytes 393224 | tf_op jit(solution)/shard_map/ppermute | solution.py:23
  23.8 6.6 %copy-start.6 = (bf16[64,2048]{1,0:T(8,128)(2,1)}, bf16[64,2048]{1,0:T(8,128)(2,1)S(1)}, u32[]{:S(2)}) copy-start(bf16[64,2048]{1,0:T(8,128)(2,1)S(1)} %collective-permute-done.4.refs_5_) | copy-start | bytes 786436
  24.8 2.3 %collective-permute-start.7 = (bf16[64,2048]{1,0:T(8,128)(2,1)S(1)}, bf16[64,2048]{1,0:T(8,128)(2,1)S(1)}, u32[]{:S(2)}, u32[]{:S(2)}) collective-permute-start(bf16[64,2048]{1,0:T(8,128)(2,1)S(1)} %collective-permute-done.4.refs_5_), channel_id=1, source_target_pairs={{0,2},{2,0},{1,3},{3,1},{4,6},{6,4},{5,7},{7,5},{8,10},{10,8},{9,1... | collective-permute-start | bytes 786440 | tf_op jit(solution)/shard_map/ppermute | solution.py:23
  24.8 2.3 %collective-permute-start.8 = (bf16[64,2048]{1,0:T(8,128)(2,1)S(1)}, bf16[64,2048]{1,0:T(8,128)(2,1)S(1)}, u32[]{:S(2)}, u32[]{:S(2)}) collective-permute-start(bf16[64,2048]{1,0:T(8,128)(2,1)S(1)} %collective-permute-done.3.refs_7_), channel_id=1, source_target_pairs={{0,2},{2,0},{1,3},{3,1},{4,6},{6,4},{5,7},{7,5},{8,10},{10,8},{9,1... | collective-permute-start | bytes 786440 | tf_op jit(solution)/shard_map/ppermute | solution.py:23
  25.4 1.6 %collective-permute-start.2 = (bf16[32,2048]{1,0:T(8,128)(2,1)S(1)}, bf16[32,2048]{1,0:T(8,128)(2,1)S(1)}, u32[]{:S(2)}, u32[]{:S(2)}) collective-permute-start(bf16[32,2048]{1,0:T(8,128)(2,1)S(1)} %collective-permute-done.refs_1_), channel_id=1, source_target_pairs={{0,2},{2,0},{1,3},{3,1},{4,6},{6,4},{5,7},{7,5},{8,10},{10,8},{9,1... | collective-permute-start | bytes 393224 | tf_op jit(solution)/shard_map/ppermute | solution.py:23
  25.4 1.8 %collective-permute-start.6 = (bf16[32,2048]{1,0:T(8,128)(2,1)S(1)}, bf16[32,2048]{1,0:T(8,128)(2,1)S(1)}, u32[]{:S(2)}, u32[]{:S(2)}) collective-permute-start(bf16[32,2048]{1,0:T(8,128)(2,1)S(1)} %collective-permute-done.5.refs_3_), channel_id=1, source_target_pairs={{0,2},{2,0},{1,3},{3,1},{4,6},{6,4},{5,7},{7,5},{8,10},{10,8},{9,1... | collective-permute-start | bytes 393224 | tf_op jit(solution)/shard_map/ppermute | solution.py:23
  30.5 9.8 %copy-start.7 = (bf16[64,2048]{1,0:T(8,128)(2,1)S(1)}, bf16[64,2048]{1,0:T(8,128)(2,1)}, u32[]{:S(2)}) copy-start(bf16[64,2048]{1,0:T(8,128)(2,1)} %copy-done.6) | copy-start | bytes 786436
  30.5 20.9 %collective-permute-start.11 = (f16[512,768]{1,0:T(8,128)(2,1)S(1)}, f16[512,768]{1,0:T(8,128)(2,1)S(1)}, u32[]{:S(2)}, u32[]{:S(2)}) collective-permute-start(f16[512,768]{1,0:T(8,128)(2,1)S(1)} %fusion.3), channel_id=1, source_target_pairs={{0,4},{12,8},{1,5},{13,9},{2,6},{14,10},{3,7},{15,11},{16,20},{28,... | collective-permute-start | bytes 2359304 | tf_op jit(solution)/shard_map/ppermute | solution.py:406
  34.6 33.9 %collective-permute-start.10 = (f16[512,768]{1,0:T(8,128)(2,1)}, f16[512,768]{1,0:T(8,128)(2,1)}, u32[]{:S(2)}, u32[]{:S(2)}) collective-permute-start(f16[512,768]{1,0:T(8,128)(2,1)} %fusion.4), channel_id=1, source_target_pairs={{0,8},{12,4},{1,9},{13,5},{2,10},{14,6},{3,11},{15,7},{16,24},{28,... | collective-permute-start | bytes 2359304 | tf_op jit(solution)/shard_map/ppermute | solution.py:409
  38.7 29.8 %collective-permute-start.9 = (f16[512,768]{1,0:T(8,128)(2,1)}, f16[512,768]{1,0:T(8,128)(2,1)}, u32[]{:S(2)}, u32[]{:S(2)}) collective-permute-start(f16[512,768]{1,0:T(8,128)(2,1)} %fusion.4), channel_id=1, source_target_pairs={{4,8},{8,4},{5,9},{9,5},{6,10},{10,6},{7,11},{11,7},{20,24},{24,20... | collective-permute-start | bytes 2359304 | tf_op jit(solution)/shard_map/ppermute | solution.py:408
  52.6 31.9 %collective-permute-start.12 = (f16[512,768]{1,0:T(8,128)(2,1)}, f16[512,768]{1,0:T(8,128)(2,1)}, u32[]{:S(2)}, u32[]{:S(2)}) collective-permute-start(f16[512,768]{1,0:T(8,128)(2,1)} %fusion.5), channel_id=1, source_target_pairs={{0,4},{4,0},{8,12},{12,8},{1,5},{5,1},{9,13},{13,9},{2,6},{6,2},{1... | collective-permute-start | bytes 2359304 | tf_op jit(solution)/shard_map/ppermute | solution.py:413
  55.1 35.8 %collective-permute-start.13 = (f16[512,768]{1,0:T(8,128)(2,1)}, f16[512,768]{1,0:T(8,128)(2,1)}, u32[]{:S(2)}, u32[]{:S(2)}) collective-permute-start(f16[512,768]{1,0:T(8,128)(2,1)} %fusion.2), channel_id=1, source_target_pairs={{4,12},{8,0},{5,13},{9,1},{6,14},{10,2},{7,15},{11,3},{20,28},{24,... | collective-permute-start | bytes 2359304 | tf_op jit(solution)/shard_map/ppermute | solution.py:411
  85.8 6.4 %copy-start.9 = (bf16[1,2048]{1,0:T(2,128)(2,1)S(1)}, bf16[1,2048]{1,0:T(2,128)(2,1)}, u32[]{:S(2)}) copy-start(bf16[1,2048]{1,0:T(2,128)(2,1)} %refs_3_.3) | copy-start | bytes 12292
  85.8 6.4 %copy-start.10 = (s32[4]{0:T(128)S(1)}, s32[4]{0:T(128)}, u32[]{:S(2)}) copy-start(s32[4]{0:T(128)} %lengths.1) | copy-start | bytes 52
  85.8 21.1 %copy-start.11 = (s32[4]{0:T(128)S(1)}, s32[4]{0:T(128)}, u32[]{:S(2)}) copy-start(s32[4]{0:T(128)} %prompt_len.1) | copy-start | bytes 52
  85.9 21.1 %copy-start.12 = (f32[4]{0:T(128)S(1)}, f32[4]{0:T(128)}, u32[]{:S(2)}) copy-start(f32[4]{0:T(128)} %reward.1) | copy-start | bytes 52

commit v7 on v6

--- a/solution.py
+++ b/solution.py
@@ -402,7 +402,7 @@
     second = rest(1)
 
     def reduced(first, second):
-        far, first = lax.optimization_barrier((first[0].astype(f16), first))
+        far = first[0].astype(f16)
         fold = lax.ppermute(far, "ctx", [(0, 1), (3, 2)])
         inner = first[1].astype(f16)
         middle = lax.ppermute(inner, "ctx", [(1, 2), (2, 1)])

time: 109 us -> 109 us (level)
  transfers between devices with their start and end apart: 14 -> 14, of which waited for: 8 -> 8; matrix products, arithmetic and copies ran while one was open for 6% -> 5% of each run, Pallas kernels for 5% -> 5%
where the time goes in v7:
time: 109 us; the launch traced here: 108 us
  waiting for transfers between devices  42.3 us (39%)
  starting transfers between devices  23.1 us (21%)
  Pallas kernels  14.3 us (13%)
  blocking collectives  11.1 us (10%)
  local copies, waits for them, and re-layouts  8.94 us (8%)
  other arithmetic  7.41 us (7%)
    ppermute x1, waiting for transfers between devices, reduced(): near = lax.ppermute(beside, 'ctx', [(0, 1), (1, 0), (2, 3), (3, 2)])  14.5 us
    ppermute x1, waiting for transfers between devices, reduced(): skip = lax.ppermute(inner, 'ctx', [(0, 2), (3, 1)])  12.1 us
    all_to_all x1, blocking collectives, split_shards(): spread = lax.all_to_all(sums, ('ctx', 'sec', 'tp'), 0, 0, tiled=True)  11.1 us
    pallas_call x3, Pallas kernels, partial_call(): pl.pallas_call(kernel, out_shape=[jax.ShapeDtypeStruct(shape, jnp.float32...  8.9 us
    unnamed x26, local copies, waits for them, and re-layouts  8.77 us
    ppermute x3, starting transfers between devices, split_shards(): sent[step] = lax.ppermute(piece, 'ctx', pairs)  7.49 us
    ppermute x1, waiting for transfers between devices, reduced(): fold = lax.ppermute(far, 'ctx', [(0, 1), (3, 2)])  6.99 us
    ppermute x1, starting transfers between devices, reduced(): skip = lax.ppermute(inner, 'ctx', [(0, 2), (3, 1)])  4.11 us
  transfers between devices with their start and end apart: 14, of which 8 were waited for; matrix products, arithmetic and copies ran while one was open for 5% of the time, Pallas kernels for 5%

profile of v7, /device:TPU:0, one launch (start us, length us, event | category | flops | bytes accessed | tf_op | source)
XLA Modules:
  0.0 108.0 jit_solution(11970582694830240920)
XLA Ops:
  0.7 0.1 stack.69.plan
  0.8 1.2 %copy-done.8 = bf16[64,8192]{1,0:T(8,128)(2,1)S(1)} copy-done((bf16[64,8192]{1,0:T(8,128)(2,1)S(1)}, bf16[64,8192]{1,0:T(8,128)(2,1)}, u32[]{:S(2)}) %copy-start.8) | copy-done | bytes 1048600
  2.0 0.7 shard_map.95
  2.7 0.5 collective-permute-start.1
  3.2 3.7 %collective-permute-start = (bf16[32,2048]{1,0:T(8,128)(2,1)S(1)}, bf16[32,2048]{1,0:T(8,128)(2,1)S(1)}, u32[]{:S(2)}, u32[]{:S(2)}) collective-permute-start(bf16[32,2048]{1,0:T(8,128)(2,1)S(1)} %get-tuple-element.19), channel_id=1, source_target_pairs={{0,8},{4,12},{8,0},{12,4},{1,9},{5,13},{9,1},{13,5},{2,10},{6,14},... | collective-permute-start | bytes 393224 | tf_op jit(solution)/shard_map/ppermute | solution.py:360
  6.9 1.6 %collective-permute-start.3 = (bf16[64,2048]{1,0:T(8,128)(2,1)S(1)}, bf16[64,2048]{1,0:T(8,128)(2,1)S(1)}, u32[]{:S(2)}, u32[]{:S(2)}) collective-permute-start(bf16[64,2048]{1,0:T(8,128)(2,1)S(1)} %get-tuple-element.22), channel_id=1, source_target_pairs={{0,4},{4,8},{8,12},{12,0},{1,5},{5,9},{9,13},{13,1},{2,6},{6,10},{... | collective-permute-start | bytes 786440 | tf_op jit(solution)/shard_map/ppermute | solution.py:360
  8.4 2.2 %collective-permute-start.4 = (bf16[64,2048]{1,0:T(8,128)(2,1)S(1)}, bf16[64,2048]{1,0:T(8,128)(2,1)S(1)}, u32[]{:S(2)}, u32[]{:S(2)}) collective-permute-start(bf16[64,2048]{1,0:T(8,128)(2,1)S(1)} %get-tuple-element.23), channel_id=1, source_target_pairs={{0,12},{4,0},{8,4},{12,8},{1,13},{5,1},{9,5},{13,9},{2,14},{6,2},{... | collective-permute-start | bytes 786440 | tf_op jit(solution)/shard_map/ppermute | solution.py:360
  10.7 0.1 stack.64.refs_0_
  10.8 0.0 copy-start
  10.8 3.4 %copy-done = bf16[1,2048,2048]{2,1,0:T(8,128)(2,1)S(1)} copy-done((bf16[1,2048,2048]{2,1,0:T(8,128)(2,1)S(1)}, bf16[1,2048,2048]{2,1,0:T(8,128)(2,1)}, u32[]{:S(2)}) %copy-start) | copy-done | bytes 8388632
  14.2 1.6 %copy-done.2 = bf16[1,2048,512]{2,1,0:T(8,128)(2,1)S(1)} copy-done((bf16[1,2048,512]{2,1,0:T(8,128)(2,1)S(1)}, bf16[1,2048,512]{2,1,0:T(8,128)(2,1)}, u32[]{:S(2)}) %copy-start.2) | copy-done | bytes 2097176
  15.8 1.6 %copy-done.4 = bf16[1,2048,512]{2,1,0:T(8,128)(2,1)S(1)} copy-done((bf16[1,2048,512]{2,1,0:T(8,128)(2,1)S(1)}, bf16[1,2048,512]{2,1,0:T(8,128)(2,1)}, u32[]{:S(2)}) %copy-start.4) | copy-done | bytes 2097176
  17.3 2.4 %shard_map.96.refs_9_ = f32[4,128,768]{2,1,0:T(8,128)S(1)} custom-call(s32[9]{0:T(128)S(1)} %stack.64.refs_0_, bf16[64,2048]{1,0:T(8,128)(2,1)S(1)} %get-tuple-element.20.refs_1_, bf16[64,2048]{1,0:T(8,128)(2,1)S(1)} %collective-permute-done.1.refs_2_, bf16[1,2048,2048]{2,1,0:T(8,128)(2,1)S(1)} %copy-done, bf16[1,2048,512]{2,1,0:T(8,128)(2,1)S(1)} %copy-done.2, ...), custom_call_target="tpu_custom_call" | custom-call | flops 1610612736 | bytes 14680064 | tf_op jit(solution)/shard_map/pallas_call | solution.py:313
  19.8 0.0 collective-permute-done.refs_1_
  19.8 1.7 %collective-permute-start.5 = (bf16[32,2048]{1,0:T(8,128)(2,1)S(1)}, bf16[32,2048]{1,0:T(8,128)(2,1)S(1)}, u32[]{:S(2)}, u32[]{:S(2)}) collective-permute-start(bf16[32,2048]{1,0:T(8,128)(2,1)S(1)} %collective-permute-done.refs_1_), channel_id=1, source_target_pairs={{0,1},{1,0},{2,3},{3,2},{4,5},{5,4},{6,7},{7,6},{8,9},{9,8},{10,11... | collective-permute-start | bytes 393224 | tf_op jit(solution)/shard_map/ppermute | solution.py:23
  21.4 2.3 %collective-permute-done.4.refs_5_ = bf16[64,2048]{1,0:T(8,128)(2,1)S(1)} collective-permute-done((bf16[64,2048]{1,0:T(8,128)(2,1)S(1)}, bf16[64,2048]{1,0:T(8,128)(2,1)S(1)}, u32[]{:S(2)}, u32[]{:S(2)}) %collective-permute-start.4) | collective-permute-done | bytes 262176 | tf_op jit(solution)/shard_map/ppermute | solution.py:360
  23.8 1.1 collective-permute-done.5.refs_3_
  24.8 0.5 collective-permute-start.8
  25.4 0.0 collective-permute-start.2
  25.4 0.5 collective-permute-start.6
  25.9 1.1 collective-permute-done.2.refs_2_
  26.9 0.2 collective-permute-done.6.refs_4_
  27.2 3.2 %shard_map.98 = f32[2,512,768]{2,1,0:T(8,128)S(1)} custom-call(s32[9]{0:T(128)S(1)} %stack.64.refs_0_, bf16[32,2048]{1,0:T(8,128)(2,1)S(1)} %collective-permute-done.refs_1_, bf16[32,2048]{1,0:T(8,128)(2,1)S(1)} %collective-permute-done.2.refs_2_, bf16[32,2048]{1,0:T(8,128)(2,1)S(1)} %collective-permute-done.5.refs_3_, ...), custom_call_target="tpu_custom_call" | custom-call | flops 2415919104 | bytes 10223616 | tf_op jit(solution)/shard_map/pallas_call | solution.py:313
  30.4 1.1 %fusion.2 = (f16[512,768]{1,0:T(8,128)(2,1)S(1)}, f16[512,768]{1,0:T(8,128)(2,1)}) fusion(f32[2,512,768]{2,1,0:T(8,128)S(1)} %shard_map.98), kind=kLoop, calls=%fused_computation.9 | loop fusion | flops 786432 | bytes 4718592 | tf_op jit(solution)/shard_map/convert_element_type | solution.py:405
  31.5 3.0 %collective-permute-start.11 = (f16[512,768]{1,0:T(8,128)(2,1)S(1)}, f16[512,768]{1,0:T(8,128)(2,1)S(1)}, u32[]{:S(2)}, u32[]{:S(2)}) collective-permute-start(f16[512,768]{1,0:T(8,128)(2,1)S(1)} %get-tuple-element.36), channel_id=1, source_target_pairs={{0,4},{12,8},{1,5},{13,9},{2,6},{14,10},{3,7},{15,11},{16,20},{28,... | collective-permute-start | bytes 2359304 | tf_op jit(solution)/shard_map/ppermute | solution.py:406
  34.5 4.1 %collective-permute-start.10 = (f16[512,768]{1,0:T(8,128)(2,1)}, f16[512,768]{1,0:T(8,128)(2,1)}, u32[]{:S(2)}, u32[]{:S(2)}) collective-permute-start(f16[512,768]{1,0:T(8,128)(2,1)} %get-tuple-element.37), channel_id=1, source_target_pairs={{0,8},{12,4},{1,9},{13,5},{2,10},{14,6},{3,11},{15,7},{16,24},{28,... | collective-permute-start | bytes 2359304 | tf_op jit(solution)/shard_map/ppermute | solution.py:409
  38.6 1.6 %collective-permute-start.9 = (f16[512,768]{1,0:T(8,128)(2,1)}, f16[512,768]{1,0:T(8,128)(2,1)}, u32[]{:S(2)}, u32[]{:S(2)}) collective-permute-start(f16[512,768]{1,0:T(8,128)(2,1)} %get-tuple-element.37), channel_id=1, source_target_pairs={{4,8},{8,4},{5,9},{9,5},{6,10},{10,6},{7,11},{11,7},{20,24},{24,20... | collective-permute-start | bytes 2359304 | tf_op jit(solution)/shard_map/ppermute | solution.py:408
  40.2 0.9 copy-done.7
  41.1 3.2 %shard_map.97 = f32[2,512,768]{2,1,0:T(8,128)S(1)} custom-call(s32[9]{0:T(128)S(1)} %stack.64.refs_0_, bf16[32,2048]{1,0:T(8,128)(2,1)S(1)} %collective-permute-done.refs_1_, bf16[32,2048]{1,0:T(8,128)(2,1)S(1)} %collective-permute-done.2.refs_2_, bf16[32,2048]{1,0:T(8,128)(2,1)S(1)} %collective-permute-done.5.refs_3_, ...), custom_call_target="tpu_custom_call" | custom-call | flops 2415919104 | bytes 10223616 | tf_op jit(solution)/shard_map/pallas_call | solution.py:313
  44.4 1.0 fusion.4
  45.3 7.0 %collective-permute-done.11 = f16[512,768]{1,0:T(8,128)(2,1)S(1)} collective-permute-done((f16[512,768]{1,0:T(8,128)(2,1)S(1)}, f16[512,768]{1,0:T(8,128)(2,1)S(1)}, u32[]{:S(2)}, u32[]{:S(2)}) %collective-permute-start.11) | collective-permute-done | bytes 786464 | tf_op jit(solution)/shard_map/ppermute | solution.py:406
  52.3 1.1 add_convert_fusion
  53.4 2.5 %collective-permute-start.12 = (f16[512,768]{1,0:T(8,128)(2,1)}, f16[512,768]{1,0:T(8,128)(2,1)}, u32[]{:S(2)}, u32[]{:S(2)}) collective-permute-start(f16[512,768]{1,0:T(8,128)(2,1)} %fusion.4), channel_id=1, source_target_pairs={{0,4},{4,0},{8,12},{12,8},{1,5},{5,1},{9,13},{13,9},{2,6},{6,2},{1... | collective-permute-start | bytes 2359304 | tf_op jit(solution)/shard_map/ppermute | solution.py:413
  55.9 1.3 %collective-permute-start.13 = (f16[512,768]{1,0:T(8,128)(2,1)}, f16[512,768]{1,0:T(8,128)(2,1)}, u32[]{:S(2)}, u32[]{:S(2)}) collective-permute-start(f16[512,768]{1,0:T(8,128)(2,1)} %add_convert_fusion), channel_id=1, source_target_pairs={{4,12},{8,0},{5,13},{9,1},{6,14},{10,2},{7,15},{11,3},{20,28},{24,... | collective-permute-start | bytes 2359304 | tf_op jit(solution)/shard_map/ppermute | solution.py:411
  57.2 0.1 pad_add_fusion.plan.refs_1_.where
  57.3 12.1 %collective-permute-done.10 = f16[512,768]{1,0:T(8,128)(2,1)} collective-permute-done((f16[512,768]{1,0:T(8,128)(2,1)}, f16[512,768]{1,0:T(8,128)(2,1)}, u32[]{:S(2)}, u32[]{:S(2)}) %collective-permute-start.10) | collective-permute-done | bytes 786464 | tf_op jit(solution)/shard_map/ppermute | solution.py:409
  69.3 1.6 %fusion.1 = f32[512,768]{1,0:T(8,128)S(1)} fusion(f32[2,512,768]{2,1,0:T(8,128)S(1)} %shard_map.97, f16[512,768]{1,0:T(8,128)(2,1)} %collective-permute-done.10, f16[512,768]{1,0:T(8,128)(2,1)} %collective-permute-done.9), kind=kLoop, calls=%fused_computation.5 | loop fusion | flops 1572864 | bytes 4718592 | tf_op jit(solution)/shard_map/add | solution.py:414
  70.9 14.5 %collective-permute-done.12 = f16[512,768]{1,0:T(8,128)(2,1)} collective-permute-done((f16[512,768]{1,0:T(8,128)(2,1)}, f16[512,768]{1,0:T(8,128)(2,1)}, u32[]{:S(2)}, u32[]{:S(2)}) %collective-permute-start.12) | collective-permute-done | bytes 786464 | tf_op jit(solution)/shard_map/ppermute | solution.py:413
  85.4 1.3 %convert_add_fusion = f32[512,768]{1,0:T(8,128)S(1)} fusion(f32[512,768]{1,0:T(8,128)S(1)} %fusion.1, f16[512,768]{1,0:T(8,128)(2,1)} %collective-permute-done.12), kind=kLoop, calls=%fused_computation.7 | loop fusion | flops 786432 | bytes 3932160 | tf_op jit(solution)/shard_map/add | solution.py:416
  86.7 0.0 copy-start.9
  86.7 0.0 copy-start.10
  86.7 0.0 copy-start.11
  86.7 0.0 copy-start.12
  86.7 4.1 %collective-permute-done.13 = f16[512,768]{1,0:T(8,128)(2,1)} collective-permute-done((f16[512,768]{1,0:T(8,128)(2,1)}, f16[512,768]{1,0:T(8,128)(2,1)}, u32[]{:S(2)}, u32[]{:S(2)}) %collective-permute-start.13) | collective-permute-done | bytes 786464 | tf_op jit(solution)/shard_map/ppermute | solution.py:411
  90.8 1.3 %multiply_convert_fusion.refs_2_ = bf16[512,768]{1,0:T(8,128)(2,1)S(1)} fusion(f32[512,768]{1,0:T(8,128)S(1)} %convert_add_fusion, f16[512,768]{1,0:T(8,128)(2,1)} %collective-permute-done.13), kind=kLoop, calls=%fused_computation.6 | loop fusion | flops 1572864 | bytes 3145728 | tf_op jit(solution)/shard_map/convert_element_type | solution.py:418
  92.2 3.6 %shard_map.99 = f32[16,1,128]{2,1,0:T(1,128)S(1)} custom-call(s32[2]{0:T(128)S(1)} %pad_add_fusion.plan.refs_1_.where, s32[4]{0:T(128)S(1)} %copy-done.10, s32[2]{0:T(128)S(1)} %pad_add_fusion.plan.refs_1_.where, bf16[512,768]{1,0:T(8,128)(2,1)S(1)} %multiply_convert_fusion.refs_2_, bf16[1,2048]{1,0:T(2,128)(2,1)S(1)} %copy-done.9), custom_call_target="tpu_custom_call" | custom-call | tf_op jit(solution)/shard_map/pallas_call | solution.py:424
  95.7 11.1 %all_to_all.5.parts = f32[16,1,128]{2,1,0:T(1,128)S(1)} all-to-all(f32[16,1,128]{2,1,0:T(1,128)S(1)} %shard_map.99), channel_id=1, replica_groups=mesh['grp'=2,'ctx'=4,'sec'=2,'tp'=2] {'ctx','sec','tp'}, dimensions={0} | all-to-all | bytes 16384 | tf_op jit(solution)/shard_map/all_to_all | solution.py:441
  106.9 1.2 %shard_map.100 = (f32[1,64]{1,0:T(1,128)}, f32[1,64]{1,0:T(1,128)}) custom-call(s32[4]{0:T(128)S(1)} %copy-done.10, s32[4]{0:T(128)S(1)} %copy-done.11, f32[4]{0:T(128)S(1)} %copy-done.12, s32[2]{0:T(128)S(1)} %pad_add_fusion.plan.refs_1_.where, f32[16,1,128]{2,1,0:T(1,128)S(1)} %all_to_all.5.parts), custom_call_target="tpu_custom_call" | custom-call | tf_op jit(solution)/shard_map/pallas_call | solution.py:443
  (22 shorter events, 0.0 us)
Async XLA Ops:
  0.8 1.2 %copy-start.8 = (bf16[64,8192]{1,0:T(8,128)(2,1)S(1)}, bf16[64,8192]{1,0:T(8,128)(2,1)}, u32[]{:S(2)}) copy-start(bf16[64,8192]{1,0:T(8,128)(2,1)} %hidden.1) | copy-start | bytes 3145732
  2.7 8.1 %collective-permute-start.1 = (bf16[64,2048]{1,0:T(8,128)(2,1)S(1)}, bf16[64,2048]{1,0:T(8,128)(2,1)S(1)}, u32[]{:S(2)}, u32[]{:S(2)}) collective-permute-start(bf16[64,2048]{1,0:T(8,128)(2,1)S(1)} %get-tuple-element.20.refs_1_), channel_id=1, source_target_pairs={{0,2},{2,0},{1,3},{3,1},{4,6},{6,4},{5,7},{7,5},{8,10},{10,8},{9,1... | collective-permute-start | bytes 786440 | tf_op jit(solution)/shard_map/ppermute | solution.py:23
  3.2 16.6 %collective-permute-start = (bf16[32,2048]{1,0:T(8,128)(2,1)S(1)}, bf16[32,2048]{1,0:T(8,128)(2,1)S(1)}, u32[]{:S(2)}, u32[]{:S(2)}) collective-permute-start(bf16[32,2048]{1,0:T(8,128)(2,1)S(1)} %get-tuple-element.19), channel_id=1, source_target_pairs={{0,8},{4,12},{8,0},{12,4},{1,9},{5,13},{9,1},{13,5},{2,10},{6,14},... | collective-permute-start | bytes 393224 | tf_op jit(solution)/shard_map/ppermute | solution.py:360
  6.9 14.6 %collective-permute-start.3 = (bf16[64,2048]{1,0:T(8,128)(2,1)S(1)}, bf16[64,2048]{1,0:T(8,128)(2,1)S(1)}, u32[]{:S(2)}, u32[]{:S(2)}) collective-permute-start(bf16[64,2048]{1,0:T(8,128)(2,1)S(1)} %get-tuple-element.22), channel_id=1, source_target_pairs={{0,4},{4,8},{8,12},{12,0},{1,5},{5,9},{9,13},{13,1},{2,6},{6,10},{... | collective-permute-start | bytes 786440 | tf_op jit(solution)/shard_map/ppermute | solution.py:360
  8.4 15.3 %collective-permute-start.4 = (bf16[64,2048]{1,0:T(8,128)(2,1)S(1)}, bf16[64,2048]{1,0:T(8,128)(2,1)S(1)}, u32[]{:S(2)}, u32[]{:S(2)}) collective-permute-start(bf16[64,2048]{1,0:T(8,128)(2,1)S(1)} %get-tuple-element.23), channel_id=1, source_target_pairs={{0,12},{4,0},{8,4},{12,8},{1,13},{5,1},{9,5},{13,9},{2,14},{6,2},{... | collective-permute-start | bytes 786440 | tf_op jit(solution)/shard_map/ppermute | solution.py:360
  10.8 3.4 %copy-start = (bf16[1,2048,2048]{2,1,0:T(8,128)(2,1)S(1)}, bf16[1,2048,2048]{2,1,0:T(8,128)(2,1)}, u32[]{:S(2)}) copy-start(bf16[1,2048,2048]{2,1,0:T(8,128)(2,1)} %refs_10_.3) | copy-start | bytes 25165828
  14.2 1.6 %copy-start.2 = (bf16[1,2048,512]{2,1,0:T(8,128)(2,1)S(1)}, bf16[1,2048,512]{2,1,0:T(8,128)(2,1)}, u32[]{:S(2)}) copy-start(bf16[1,2048,512]{2,1,0:T(8,128)(2,1)} %refs_11_.3) | copy-start | bytes 6291460
  15.7 1.6 %copy-start.4 = (bf16[1,2048,512]{2,1,0:T(8,128)(2,1)S(1)}, bf16[1,2048,512]{2,1,0:T(8,128)(2,1)}, u32[]{:S(2)}) copy-start(bf16[1,2048,512]{2,1,0:T(8,128)(2,1)} %refs_12_.3) | copy-start | bytes 6291460
  17.3 9.8 %copy-start.1 = (bf16[1,2048,2048]{2,1,0:T(8,128)(2,1)S(1)}, bf16[1,2048,2048]{2,1,0:T(8,128)(2,1)}, u32[]{:S(2)}) copy-start(bf16[1,2048,2048]{2,1,0:T(8,128)(2,1)} %refs_10_.3) | copy-start | bytes 25165828
  17.3 9.8 %copy-start.3 = (bf16[1,2048,512]{2,1,0:T(8,128)(2,1)S(1)}, bf16[1,2048,512]{2,1,0:T(8,128)(2,1)}, u32[]{:S(2)}) copy-start(bf16[1,2048,512]{2,1,0:T(8,128)(2,1)} %refs_11_.3) | copy-start | bytes 6291460
  17.3 9.8 %copy-start.5 = (bf16[1,2048,512]{2,1,0:T(8,128)(2,1)S(1)}, bf16[1,2048,512]{2,1,0:T(8,128)(2,1)}, u32[]{:S(2)}) copy-start(bf16[1,2048,512]{2,1,0:T(8,128)(2,1)} %refs_12_.3) | copy-start | bytes 6291460
  19.8 5.1 %collective-permute-start.5 = (bf16[32,2048]{1,0:T(8,128)(2,1)S(1)}, bf16[32,2048]{1,0:T(8,128)(2,1)S(1)}, u32[]{:S(2)}, u32[]{:S(2)}) collective-permute-start(bf16[32,2048]{1,0:T(8,128)(2,1)S(1)} %collective-permute-done.refs_1_), channel_id=1, source_target_pairs={{0,1},{1,0},{2,3},{3,2},{4,5},{5,4},{6,7},{7,6},{8,9},{9,8},{10,11... | collective-permute-start | bytes 393224 | tf_op jit(solution)/shard_map/ppermute | solution.py:23
  23.8 6.6 %copy-start.6 = (bf16[64,2048]{1,0:T(8,128)(2,1)}, bf16[64,2048]{1,0:T(8,128)(2,1)S(1)}, u32[]{:S(2)}) copy-start(bf16[64,2048]{1,0:T(8,128)(2,1)S(1)} %collective-permute-done.4.refs_5_) | copy-start | bytes 786436
  24.8 2.3 %collective-permute-start.7 = (bf16[64,2048]{1,0:T(8,128)(2,1)S(1)}, bf16[64,2048]{1,0:T(8,128)(2,1)S(1)}, u32[]{:S(2)}, u32[]{:S(2)}) collective-permute-start(bf16[64,2048]{1,0:T(8,128)(2,1)S(1)} %collective-permute-done.4.refs_5_), channel_id=1, source_target_pairs={{0,2},{2,0},{1,3},{3,1},{4,6},{6,4},{5,7},{7,5},{8,10},{10,8},{9,1... | collective-permute-start | bytes 786440 | tf_op jit(solution)/shard_map/ppermute | solution.py:23
  24.8 2.3 %collective-permute-start.8 = (bf16[64,2048]{1,0:T(8,128)(2,1)S(1)}, bf16[64,2048]{1,0:T(8,128)(2,1)S(1)}, u32[]{:S(2)}, u32[]{:S(2)}) collective-permute-start(bf16[64,2048]{1,0:T(8,128)(2,1)S(1)} %collective-permute-done.3.refs_7_), channel_id=1, source_target_pairs={{0,2},{2,0},{1,3},{3,1},{4,6},{6,4},{5,7},{7,5},{8,10},{10,8},{9,1... | collective-permute-start | bytes 786440 | tf_op jit(solution)/shard_map/ppermute | solution.py:23
  25.4 1.6 %collective-permute-start.2 = (bf16[32,2048]{1,0:T(8,128)(2,1)S(1)}, bf16[32,2048]{1,0:T(8,128)(2,1)S(1)}, u32[]{:S(2)}, u32[]{:S(2)}) collective-permute-start(bf16[32,2048]{1,0:T(8,128)(2,1)S(1)} %collective-permute-done.refs_1_), channel_id=1, source_target_pairs={{0,2},{2,0},{1,3},{3,1},{4,6},{6,4},{5,7},{7,5},{8,10},{10,8},{9,1... | collective-permute-start | bytes 393224 | tf_op jit(solution)/shard_map/ppermute | solution.py:23
  25.4 1.8 %collective-permute-start.6 = (bf16[32,2048]{1,0:T(8,128)(2,1)S(1)}, bf16[32,2048]{1,0:T(8,128)(2,1)S(1)}, u32[]{:S(2)}, u32[]{:S(2)}) collective-permute-start(bf16[32,2048]{1,0:T(8,128)(2,1)S(1)} %collective-permute-done.5.refs_3_), channel_id=1, source_target_pairs={{0,2},{2,0},{1,3},{3,1},{4,6},{6,4},{5,7},{7,5},{8,10},{10,8},{9,1... | collective-permute-start | bytes 393224 | tf_op jit(solution)/shard_map/ppermute | solution.py:23
  31.5 20.8 %collective-permute-start.11 = (f16[512,768]{1,0:T(8,128)(2,1)S(1)}, f16[512,768]{1,0:T(8,128)(2,1)S(1)}, u32[]{:S(2)}, u32[]{:S(2)}) collective-permute-start(f16[512,768]{1,0:T(8,128)(2,1)S(1)} %get-tuple-element.36), channel_id=1, source_target_pairs={{0,4},{12,8},{1,5},{13,9},{2,6},{14,10},{3,7},{15,11},{16,20},{28,... | collective-permute-start | bytes 2359304 | tf_op jit(solution)/shard_map/ppermute | solution.py:406
  34.5 34.8 %collective-permute-start.10 = (f16[512,768]{1,0:T(8,128)(2,1)}, f16[512,768]{1,0:T(8,128)(2,1)}, u32[]{:S(2)}, u32[]{:S(2)}) collective-permute-start(f16[512,768]{1,0:T(8,128)(2,1)} %get-tuple-element.37), channel_id=1, source_target_pairs={{0,8},{12,4},{1,9},{13,5},{2,10},{14,6},{3,11},{15,7},{16,24},{28,... | collective-permute-start | bytes 2359304 | tf_op jit(solution)/shard_map/ppermute | solution.py:409
  38.6 30.7 %collective-permute-start.9 = (f16[512,768]{1,0:T(8,128)(2,1)}, f16[512,768]{1,0:T(8,128)(2,1)}, u32[]{:S(2)}, u32[]{:S(2)}) collective-permute-start(f16[512,768]{1,0:T(8,128)(2,1)} %get-tuple-element.37), channel_id=1, source_target_pairs={{4,8},{8,4},{5,9},{9,5},{6,10},{10,6},{7,11},{11,7},{20,24},{24,20... | collective-permute-start | bytes 2359304 | tf_op jit(solution)/shard_map/ppermute | solution.py:408
  40.2 0.9 copy-start.7
  53.4 32.0 %collective-permute-start.12 = (f16[512,768]{1,0:T(8,128)(2,1)}, f16[512,768]{1,0:T(8,128)(2,1)}, u32[]{:S(2)}, u32[]{:S(2)}) collective-permute-start(f16[512,768]{1,0:T(8,128)(2,1)} %fusion.4), channel_id=1, source_target_pairs={{0,4},{4,0},{8,12},{12,8},{1,5},{5,1},{9,13},{13,9},{2,6},{6,2},{1... | collective-permute-start | bytes 2359304 | tf_op jit(solution)/shard_map/ppermute | solution.py:413
  55.9 34.9 %collective-permute-start.13 = (f16[512,768]{1,0:T(8,128)(2,1)}, f16[512,768]{1,0:T(8,128)(2,1)}, u32[]{:S(2)}, u32[]{:S(2)}) collective-permute-start(f16[512,768]{1,0:T(8,128)(2,1)} %add_convert_fusion), channel_id=1, source_target_pairs={{4,12},{8,0},{5,13},{9,1},{6,14},{10,2},{7,15},{11,3},{20,28},{24,... | collective-permute-start | bytes 2359304 | tf_op jit(solution)/shard_map/ppermute | solution.py:411
  86.7 5.5 %copy-start.9 = (bf16[1,2048]{1,0:T(2,128)(2,1)S(1)}, bf16[1,2048]{1,0:T(2,128)(2,1)}, u32[]{:S(2)}) copy-start(bf16[1,2048]{1,0:T(2,128)(2,1)} %refs_3_.3) | copy-start | bytes 12292
  86.7 5.5 %copy-start.10 = (s32[4]{0:T(128)S(1)}, s32[4]{0:T(128)}, u32[]{:S(2)}) copy-start(s32[4]{0:T(128)} %lengths.1) | copy-start | bytes 52
  86.7 20.2 %copy-start.11 = (s32[4]{0:T(128)S(1)}, s32[4]{0:T(128)}, u32[]{:S(2)}) copy-start(s32[4]{0:T(128)} %prompt_len.1) | copy-start | bytes 52
  86.7 20.1 %copy-start.12 = (f32[4]{0:T(128)S(1)}, f32[4]{0:T(128)}, u32[]{:S(2)}) copy-start(f32[4]{0:T(128)} %reward.1) | copy-start | bytes 52

commit v8 on v7

--- a/solution.py
+++ b/solution.py
@@ -409,7 +409,7 @@
         skip = lax.ppermute(inner, "ctx", [(0, 2), (3, 1)])
         folded = (first[0] + fold.astype(f32)).astype(f16)
         ends = lax.ppermute(folded, "ctx", [(1, 3), (2, 0)])
-        beside, _ = lax.optimization_barrier((second[0].astype(f16), folded))
+        beside = second[0].astype(f16)
         near = lax.ppermute(beside, "ctx", [(0, 1), (1, 0), (2, 3), (3, 2)])
         total = second[1] + middle.astype(f32) + skip.astype(f32)
         total, near = lax.optimization_barrier((total, near))

time: 109 us -> 109 us (level)
  starting transfers between devices: 23.1 us -> 20.6 us
  waiting for transfers between devices: 42.3 us -> 44.8 us
    ppermute x1, starting transfers between devices: 2.48 us -> 0.01 us  [reduced(): near = lax.ppermute(beside, 'ctx', [(0, 1), (1, 0), (2, 3), (3, 2)])]
    ppermute x1, waiting for transfers between devices: 12.1 us -> 14.6 us  [reduced(): skip = lax.ppermute(inner, 'ctx', [(0, 2), (3, 1)])]
where the time goes in v8:
time: 109 us; the launch traced here: 108 us
  waiting for transfers between devices  44.8 us (41%)
  starting transfers between devices  20.6 us (19%)
  Pallas kernels  14.3 us (13%)
  blocking collectives  11.1 us (10%)
  local copies, waits for them, and re-layouts  8.94 us (8%)
  other arithmetic  7.42 us (7%)
    ppermute x1, waiting for transfers between devices, reduced(): skip = lax.ppermute(inner, 'ctx', [(0, 2), (3, 1)])  14.6 us
    ppermute x1, waiting for transfers between devices, reduced(): near = lax.ppermute(beside, 'ctx', [(0, 1), (1, 0), (2, 3), (3, 2)])  14.5 us
    all_to_all x1, blocking collectives, split_shards(): spread = lax.all_to_all(sums, ('ctx', 'sec', 'tp'), 0, 0, tiled=True)  11.1 us
    pallas_call x3, Pallas kernels, partial_call(): pl.pallas_call(kernel, out_shape=[jax.ShapeDtypeStruct(shape, jnp.float32...  8.9 us
    unnamed x26, local copies, waits for them, and re-layouts  8.77 us
    ppermute x3, starting transfers between devices, split_shards(): sent[step] = lax.ppermute(piece, 'ctx', pairs)  7.49 us
    ppermute x1, waiting for transfers between devices, reduced(): fold = lax.ppermute(far, 'ctx', [(0, 1), (3, 2)])  6.99 us
    ppermute x1, starting transfers between devices, reduced(): skip = lax.ppermute(inner, 'ctx', [(0, 2), (3, 1)])  4.11 us
  transfers between devices with their start and end apart: 14, of which 8 were waited for; matrix products, arithmetic and copies ran while one was open for 5% of the time, Pallas kernels for 5%

profile of v8, /device:TPU:0, one launch (start us, length us, event | category | flops | bytes accessed | tf_op | source)
XLA Modules:
  0.0 108.0 jit_solution(1704779195184868687)
XLA Ops:
  0.7 0.1 stack.69.plan
  0.8 1.2 %copy-done.8 = bf16[64,8192]{1,0:T(8,128)(2,1)S(1)} copy-done((bf16[64,8192]{1,0:T(8,128)(2,1)S(1)}, bf16[64,8192]{1,0:T(8,128)(2,1)}, u32[]{:S(2)}) %copy-start.8) | copy-done | bytes 1048600
  2.0 0.7 shard_map.95
  2.7 0.5 collective-permute-start.1
  3.2 3.7 %collective-permute-start = (bf16[32,2048]{1,0:T(8,128)(2,1)S(1)}, bf16[32,2048]{1,0:T(8,128)(2,1)S(1)}, u32[]{:S(2)}, u32[]{:S(2)}) collective-permute-start(bf16[32,2048]{1,0:T(8,128)(2,1)S(1)} %get-tuple-element.18), channel_id=1, source_target_pairs={{0,8},{4,12},{8,0},{12,4},{1,9},{5,13},{9,1},{13,5},{2,10},{6,14},... | collective-permute-start | bytes 393224 | tf_op jit(solution)/shard_map/ppermute | solution.py:360
  6.9 1.6 %collective-permute-start.3 = (bf16[64,2048]{1,0:T(8,128)(2,1)S(1)}, bf16[64,2048]{1,0:T(8,128)(2,1)S(1)}, u32[]{:S(2)}, u32[]{:S(2)}) collective-permute-start(bf16[64,2048]{1,0:T(8,128)(2,1)S(1)} %get-tuple-element.21), channel_id=1, source_target_pairs={{0,4},{4,8},{8,12},{12,0},{1,5},{5,9},{9,13},{13,1},{2,6},{6,10},{... | collective-permute-start | bytes 786440 | tf_op jit(solution)/shard_map/ppermute | solution.py:360
  8.4 2.2 %collective-permute-start.4 = (bf16[64,2048]{1,0:T(8,128)(2,1)S(1)}, bf16[64,2048]{1,0:T(8,128)(2,1)S(1)}, u32[]{:S(2)}, u32[]{:S(2)}) collective-permute-start(bf16[64,2048]{1,0:T(8,128)(2,1)S(1)} %get-tuple-element.22), channel_id=1, source_target_pairs={{0,12},{4,0},{8,4},{12,8},{1,13},{5,1},{9,5},{13,9},{2,14},{6,2},{... | collective-permute-start | bytes 786440 | tf_op jit(solution)/shard_map/ppermute | solution.py:360
  10.7 0.1 stack.64.refs_0_
  10.8 0.0 copy-start
  10.8 3.4 %copy-done = bf16[1,2048,2048]{2,1,0:T(8,128)(2,1)S(1)} copy-done((bf16[1,2048,2048]{2,1,0:T(8,128)(2,1)S(1)}, bf16[1,2048,2048]{2,1,0:T(8,128)(2,1)}, u32[]{:S(2)}) %copy-start) | copy-done | bytes 8388632
  14.2 1.6 %copy-done.2 = bf16[1,2048,512]{2,1,0:T(8,128)(2,1)S(1)} copy-done((bf16[1,2048,512]{2,1,0:T(8,128)(2,1)S(1)}, bf16[1,2048,512]{2,1,0:T(8,128)(2,1)}, u32[]{:S(2)}) %copy-start.2) | copy-done | bytes 2097176
  15.8 1.6 %copy-done.4 = bf16[1,2048,512]{2,1,0:T(8,128)(2,1)S(1)} copy-done((bf16[1,2048,512]{2,1,0:T(8,128)(2,1)S(1)}, bf16[1,2048,512]{2,1,0:T(8,128)(2,1)}, u32[]{:S(2)}) %copy-start.4) | copy-done | bytes 2097176
  17.3 2.4 %shard_map.96.refs_9_ = f32[4,128,768]{2,1,0:T(8,128)S(1)} custom-call(s32[9]{0:T(128)S(1)} %stack.64.refs_0_, bf16[64,2048]{1,0:T(8,128)(2,1)S(1)} %get-tuple-element.19.refs_1_, bf16[64,2048]{1,0:T(8,128)(2,1)S(1)} %collective-permute-done.1.refs_2_, bf16[1,2048,2048]{2,1,0:T(8,128)(2,1)S(1)} %copy-done, bf16[1,2048,512]{2,1,0:T(8,128)(2,1)S(1)} %copy-done.2, ...), custom_call_target="tpu_custom_call" | custom-call | flops 1610612736 | bytes 14680064 | tf_op jit(solution)/shard_map/pallas_call | solution.py:313
  19.8 0.0 collective-permute-done.refs_1_
  19.8 1.7 %collective-permute-start.5 = (bf16[32,2048]{1,0:T(8,128)(2,1)S(1)}, bf16[32,2048]{1,0:T(8,128)(2,1)S(1)}, u32[]{:S(2)}, u32[]{:S(2)}) collective-permute-start(bf16[32,2048]{1,0:T(8,128)(2,1)S(1)} %collective-permute-done.refs_1_), channel_id=1, source_target_pairs={{0,1},{1,0},{2,3},{3,2},{4,5},{5,4},{6,7},{7,6},{8,9},{9,8},{10,11... | collective-permute-start | bytes 393224 | tf_op jit(solution)/shard_map/ppermute | solution.py:23
  21.4 0.0 collective-permute-done.3.refs_7_
  21.4 2.3 %collective-permute-done.4.refs_5_ = bf16[64,2048]{1,0:T(8,128)(2,1)S(1)} collective-permute-done((bf16[64,2048]{1,0:T(8,128)(2,1)S(1)}, bf16[64,2048]{1,0:T(8,128)(2,1)S(1)}, u32[]{:S(2)}, u32[]{:S(2)}) %collective-permute-start.4) | collective-permute-done | bytes 262176 | tf_op jit(solution)/shard_map/ppermute | solution.py:360
  23.8 1.1 collective-permute-done.5.refs_3_
  24.8 0.5 collective-permute-start.8
  25.4 0.0 collective-permute-start.2
  25.4 0.5 collective-permute-start.6
  25.9 1.1 collective-permute-done.2.refs_2_
  26.9 0.2 collective-permute-done.6.refs_4_
  27.2 3.2 %shard_map.98 = f32[2,512,768]{2,1,0:T(8,128)S(1)} custom-call(s32[9]{0:T(128)S(1)} %stack.64.refs_0_, bf16[32,2048]{1,0:T(8,128)(2,1)S(1)} %collective-permute-done.refs_1_, bf16[32,2048]{1,0:T(8,128)(2,1)S(1)} %collective-permute-done.2.refs_2_, bf16[32,2048]{1,0:T(8,128)(2,1)S(1)} %collective-permute-done.5.refs_3_, ...), custom_call_target="tpu_custom_call" | custom-call | flops 2415919104 | bytes 10223616 | tf_op jit(solution)/shard_map/pallas_call | solution.py:313
  30.4 1.1 %fusion.2 = (f16[512,768]{1,0:T(8,128)(2,1)S(1)}, f16[512,768]{1,0:T(8,128)(2,1)}) fusion(f32[2,512,768]{2,1,0:T(8,128)S(1)} %shard_map.98), kind=kLoop, calls=%fused_computation.9 | loop fusion | flops 786432 | bytes 4718592 | tf_op jit(solution)/shard_map/convert_element_type | solution.py:405
  31.5 3.0 %collective-permute-start.12 = (f16[512,768]{1,0:T(8,128)(2,1)S(1)}, f16[512,768]{1,0:T(8,128)(2,1)S(1)}, u32[]{:S(2)}, u32[]{:S(2)}) collective-permute-start(f16[512,768]{1,0:T(8,128)(2,1)S(1)} %get-tuple-element.34), channel_id=1, source_target_pairs={{0,4},{12,8},{1,5},{13,9},{2,6},{14,10},{3,7},{15,11},{16,20},{28,... | collective-permute-start | bytes 2359304 | tf_op jit(solution)/shard_map/ppermute | solution.py:406
  34.5 4.1 %collective-permute-start.10 = (f16[512,768]{1,0:T(8,128)(2,1)}, f16[512,768]{1,0:T(8,128)(2,1)}, u32[]{:S(2)}, u32[]{:S(2)}) collective-permute-start(f16[512,768]{1,0:T(8,128)(2,1)} %get-tuple-element.35), channel_id=1, source_target_pairs={{0,8},{12,4},{1,9},{13,5},{2,10},{14,6},{3,11},{15,7},{16,24},{28,... | collective-permute-start | bytes 2359304 | tf_op jit(solution)/shard_map/ppermute | solution.py:409
  38.6 1.6 %collective-permute-start.9 = (f16[512,768]{1,0:T(8,128)(2,1)}, f16[512,768]{1,0:T(8,128)(2,1)}, u32[]{:S(2)}, u32[]{:S(2)}) collective-permute-start(f16[512,768]{1,0:T(8,128)(2,1)} %get-tuple-element.35), channel_id=1, source_target_pairs={{4,8},{8,4},{5,9},{9,5},{6,10},{10,6},{7,11},{11,7},{20,24},{24,20... | collective-permute-start | bytes 2359304 | tf_op jit(solution)/shard_map/ppermute | solution.py:408
  40.2 0.9 copy-done.7
  41.1 3.2 %shard_map.97 = f32[2,512,768]{2,1,0:T(8,128)S(1)} custom-call(s32[9]{0:T(128)S(1)} %stack.64.refs_0_, bf16[32,2048]{1,0:T(8,128)(2,1)S(1)} %collective-permute-done.refs_1_, bf16[32,2048]{1,0:T(8,128)(2,1)S(1)} %collective-permute-done.2.refs_2_, bf16[32,2048]{1,0:T(8,128)(2,1)S(1)} %collective-permute-done.5.refs_3_, ...), custom_call_target="tpu_custom_call" | custom-call | flops 2415919104 | bytes 10223616 | tf_op jit(solution)/shard_map/pallas_call | solution.py:313
  44.4 1.0 fusion.4
  45.3 7.0 %collective-permute-done.12 = f16[512,768]{1,0:T(8,128)(2,1)S(1)} collective-permute-done((f16[512,768]{1,0:T(8,128)(2,1)S(1)}, f16[512,768]{1,0:T(8,128)(2,1)S(1)}, u32[]{:S(2)}, u32[]{:S(2)}) %collective-permute-start.12) | collective-permute-done | bytes 786464 | tf_op jit(solution)/shard_map/ppermute | solution.py:406
  52.3 1.1 add_convert_fusion
  53.4 1.3 %collective-permute-start.13 = (f16[512,768]{1,0:T(8,128)(2,1)}, f16[512,768]{1,0:T(8,128)(2,1)}, u32[]{:S(2)}, u32[]{:S(2)}) collective-permute-start(f16[512,768]{1,0:T(8,128)(2,1)} %add_convert_fusion), channel_id=1, source_target_pairs={{4,12},{8,0},{5,13},{9,1},{6,14},{10,2},{7,15},{11,3},{20,28},{24,... | collective-permute-start | bytes 2359304 | tf_op jit(solution)/shard_map/ppermute | solution.py:411
  54.7 0.1 pad_add_fusion.plan.refs_1_.where
  54.8 14.6 %collective-permute-done.10 = f16[512,768]{1,0:T(8,128)(2,1)} collective-permute-done((f16[512,768]{1,0:T(8,128)(2,1)}, f16[512,768]{1,0:T(8,128)(2,1)}, u32[]{:S(2)}, u32[]{:S(2)}) %collective-permute-start.10) | collective-permute-done | bytes 786464 | tf_op jit(solution)/shard_map/ppermute | solution.py:409
  69.3 1.6 %fusion.1 = f32[512,768]{1,0:T(8,128)S(1)} fusion(f32[2,512,768]{2,1,0:T(8,128)S(1)} %shard_map.97, f16[512,768]{1,0:T(8,128)(2,1)} %collective-permute-done.10, f16[512,768]{1,0:T(8,128)(2,1)} %collective-permute-done.9), kind=kLoop, calls=%fused_computation.5 | loop fusion | flops 1572864 | bytes 4718592 | tf_op jit(solution)/shard_map/add | solution.py:414
  70.9 14.5 %collective-permute-done.11 = f16[512,768]{1,0:T(8,128)(2,1)} collective-permute-done((f16[512,768]{1,0:T(8,128)(2,1)}, f16[512,768]{1,0:T(8,128)(2,1)}, u32[]{:S(2)}, u32[]{:S(2)}) %collective-permute-start.11) | collective-permute-done | bytes 786464 | tf_op jit(solution)/shard_map/ppermute | solution.py:413
  85.4 1.3 %convert_add_fusion = f32[512,768]{1,0:T(8,128)S(1)} fusion(f32[512,768]{1,0:T(8,128)S(1)} %fusion.1, f16[512,768]{1,0:T(8,128)(2,1)} %collective-permute-done.11), kind=kLoop, calls=%fused_computation.8 | loop fusion | flops 786432 | bytes 3932160 | tf_op jit(solution)/shard_map/add | solution.py:416
  86.7 0.0 copy-start.9
  86.7 0.0 copy-start.10
  86.7 0.0 copy-start.11
  86.7 0.0 copy-start.12
  86.7 4.1 %collective-permute-done.13 = f16[512,768]{1,0:T(8,128)(2,1)} collective-permute-done((f16[512,768]{1,0:T(8,128)(2,1)}, f16[512,768]{1,0:T(8,128)(2,1)}, u32[]{:S(2)}, u32[]{:S(2)}) %collective-permute-start.13) | collective-permute-done | bytes 786464 | tf_op jit(solution)/shard_map/ppermute | solution.py:411
  90.8 1.3 %multiply_convert_fusion.refs_2_ = bf16[512,768]{1,0:T(8,128)(2,1)S(1)} fusion(f32[512,768]{1,0:T(8,128)S(1)} %convert_add_fusion, f16[512,768]{1,0:T(8,128)(2,1)} %collective-permute-done.13), kind=kLoop, calls=%fused_computation.6 | loop fusion | flops 1572864 | bytes 3145728 | tf_op jit(solution)/shard_map/convert_element_type | solution.py:418
  92.2 3.6 %shard_map.99 = f32[16,1,128]{2,1,0:T(1,128)S(1)} custom-call(s32[2]{0:T(128)S(1)} %pad_add_fusion.plan.refs_1_.where, s32[4]{0:T(128)S(1)} %copy-done.10, s32[2]{0:T(128)S(1)} %pad_add_fusion.plan.refs_1_.where, bf16[512,768]{1,0:T(8,128)(2,1)S(1)} %multiply_convert_fusion.refs_2_, bf16[1,2048]{1,0:T(2,128)(2,1)S(1)} %copy-done.9), custom_call_target="tpu_custom_call" | custom-call | tf_op jit(solution)/shard_map/pallas_call | solution.py:424
  95.7 11.1 %all_to_all.5.parts = f32[16,1,128]{2,1,0:T(1,128)S(1)} all-to-all(f32[16,1,128]{2,1,0:T(1,128)S(1)} %shard_map.99), channel_id=1, replica_groups=mesh['grp'=2,'ctx'=4,'sec'=2,'tp'=2] {'ctx','sec','tp'}, dimensions={0} | all-to-all | bytes 16384 | tf_op jit(solution)/shard_map/all_to_all | solution.py:441
  106.9 1.2 %shard_map.100 = (f32[1,64]{1,0:T(1,128)}, f32[1,64]{1,0:T(1,128)}) custom-call(s32[4]{0:T(128)S(1)} %copy-done.10, s32[4]{0:T(128)S(1)} %copy-done.11, f32[4]{0:T(128)S(1)} %copy-done.12, s32[2]{0:T(128)S(1)} %pad_add_fusion.plan.refs_1_.where, f32[16,1,128]{2,1,0:T(1,128)S(1)} %all_to_all.5.parts), custom_call_target="tpu_custom_call" | custom-call | tf_op jit(solution)/shard_map/pallas_call | solution.py:443
  (22 shorter events, 0.0 us)
Async XLA Ops:
  0.8 1.2 %copy-start.8 = (bf16[64,8192]{1,0:T(8,128)(2,1)S(1)}, bf16[64,8192]{1,0:T(8,128)(2,1)}, u32[]{:S(2)}) copy-start(bf16[64,8192]{1,0:T(8,128)(2,1)} %hidden.1) | copy-start | bytes 3145732
  2.7 8.1 %collective-permute-start.1 = (bf16[64,2048]{1,0:T(8,128)(2,1)S(1)}, bf16[64,2048]{1,0:T(8,128)(2,1)S(1)}, u32[]{:S(2)}, u32[]{:S(2)}) collective-permute-start(bf16[64,2048]{1,0:T(8,128)(2,1)S(1)} %get-tuple-element.19.refs_1_), channel_id=1, source_target_pairs={{0,2},{2,0},{1,3},{3,1},{4,6},{6,4},{5,7},{7,5},{8,10},{10,8},{9,1... | collective-permute-start | bytes 786440 | tf_op jit(solution)/shard_map/ppermute | solution.py:23
  3.2 16.6 %collective-permute-start = (bf16[32,2048]{1,0:T(8,128)(2,1)S(1)}, bf16[32,2048]{1,0:T(8,128)(2,1)S(1)}, u32[]{:S(2)}, u32[]{:S(2)}) collective-permute-start(bf16[32,2048]{1,0:T(8,128)(2,1)S(1)} %get-tuple-element.18), channel_id=1, source_target_pairs={{0,8},{4,12},{8,0},{12,4},{1,9},{5,13},{9,1},{13,5},{2,10},{6,14},... | collective-permute-start | bytes 393224 | tf_op jit(solution)/shard_map/ppermute | solution.py:360
  6.9 14.6 %collective-permute-start.3 = (bf16[64,2048]{1,0:T(8,128)(2,1)S(1)}, bf16[64,2048]{1,0:T(8,128)(2,1)S(1)}, u32[]{:S(2)}, u32[]{:S(2)}) collective-permute-start(bf16[64,2048]{1,0:T(8,128)(2,1)S(1)} %get-tuple-element.21), channel_id=1, source_target_pairs={{0,4},{4,8},{8,12},{12,0},{1,5},{5,9},{9,13},{13,1},{2,6},{6,10},{... | collective-permute-start | bytes 786440 | tf_op jit(solution)/shard_map/ppermute | solution.py:360
  8.4 15.3 %collective-permute-start.4 = (bf16[64,2048]{1,0:T(8,128)(2,1)S(1)}, bf16[64,2048]{1,0:T(8,128)(2,1)S(1)}, u32[]{:S(2)}, u32[]{:S(2)}) collective-permute-start(bf16[64,2048]{1,0:T(8,128)(2,1)S(1)} %get-tuple-element.22), channel_id=1, source_target_pairs={{0,12},{4,0},{8,4},{12,8},{1,13},{5,1},{9,5},{13,9},{2,14},{6,2},{... | collective-permute-start | bytes 786440 | tf_op jit(solution)/shard_map/ppermute | solution.py:360
  10.8 3.4 %copy-start = (bf16[1,2048,2048]{2,1,0:T(8,128)(2,1)S(1)}, bf16[1,2048,2048]{2,1,0:T(8,128)(2,1)}, u32[]{:S(2)}) copy-start(bf16[1,2048,2048]{2,1,0:T(8,128)(2,1)} %refs_10_.3) | copy-start | bytes 25165828
  14.2 1.6 %copy-start.2 = (bf16[1,2048,512]{2,1,0:T(8,128)(2,1)S(1)}, bf16[1,2048,512]{2,1,0:T(8,128)(2,1)}, u32[]{:S(2)}) copy-start(bf16[1,2048,512]{2,1,0:T(8,128)(2,1)} %refs_11_.3) | copy-start | bytes 6291460
  15.7 1.6 %copy-start.4 = (bf16[1,2048,512]{2,1,0:T(8,128)(2,1)S(1)}, bf16[1,2048,512]{2,1,0:T(8,128)(2,1)}, u32[]{:S(2)}) copy-start(bf16[1,2048,512]{2,1,0:T(8,128)(2,1)} %refs_12_.3) | copy-start | bytes 6291460
  17.3 9.8 %copy-start.1 = (bf16[1,2048,2048]{2,1,0:T(8,128)(2,1)S(1)}, bf16[1,2048,2048]{2,1,0:T(8,128)(2,1)}, u32[]{:S(2)}) copy-start(bf16[1,2048,2048]{2,1,0:T(8,128)(2,1)} %refs_10_.3) | copy-start | bytes 25165828
  17.3 9.8 %copy-start.3 = (bf16[1,2048,512]{2,1,0:T(8,128)(2,1)S(1)}, bf16[1,2048,512]{2,1,0:T(8,128)(2,1)}, u32[]{:S(2)}) copy-start(bf16[1,2048,512]{2,1,0:T(8,128)(2,1)} %refs_11_.3) | copy-start | bytes 6291460
  17.3 9.8 %copy-start.5 = (bf16[1,2048,512]{2,1,0:T(8,128)(2,1)S(1)}, bf16[1,2048,512]{2,1,0:T(8,128)(2,1)}, u32[]{:S(2)}) copy-start(bf16[1,2048,512]{2,1,0:T(8,128)(2,1)} %refs_12_.3) | copy-start | bytes 6291460
  19.8 5.1 %collective-permute-start.5 = (bf16[32,2048]{1,0:T(8,128)(2,1)S(1)}, bf16[32,2048]{1,0:T(8,128)(2,1)S(1)}, u32[]{:S(2)}, u32[]{:S(2)}) collective-permute-start(bf16[32,2048]{1,0:T(8,128)(2,1)S(1)} %collective-permute-done.refs_1_), channel_id=1, source_target_pairs={{0,1},{1,0},{2,3},{3,2},{4,5},{5,4},{6,7},{7,6},{8,9},{9,8},{10,11... | collective-permute-start | bytes 393224 | tf_op jit(solution)/shard_map/ppermute | solution.py:23
  23.8 6.6 %copy-start.6 = (bf16[64,2048]{1,0:T(8,128)(2,1)}, bf16[64,2048]{1,0:T(8,128)(2,1)S(1)}, u32[]{:S(2)}) copy-start(bf16[64,2048]{1,0:T(8,128)(2,1)S(1)} %collective-permute-done.4.refs_5_) | copy-start | bytes 786436
  24.8 2.3 %collective-permute-start.7 = (bf16[64,2048]{1,0:T(8,128)(2,1)S(1)}, bf16[64,2048]{1,0:T(8,128)(2,1)S(1)}, u32[]{:S(2)}, u32[]{:S(2)}) collective-permute-start(bf16[64,2048]{1,0:T(8,128)(2,1)S(1)} %collective-permute-done.4.refs_5_), channel_id=1, source_target_pairs={{0,2},{2,0},{1,3},{3,1},{4,6},{6,4},{5,7},{7,5},{8,10},{10,8},{9,1... | collective-permute-start | bytes 786440 | tf_op jit(solution)/shard_map/ppermute | solution.py:23
  24.8 2.3 %collective-permute-start.8 = (bf16[64,2048]{1,0:T(8,128)(2,1)S(1)}, bf16[64,2048]{1,0:T(8,128)(2,1)S(1)}, u32[]{:S(2)}, u32[]{:S(2)}) collective-permute-start(bf16[64,2048]{1,0:T(8,128)(2,1)S(1)} %collective-permute-done.3.refs_7_), channel_id=1, source_target_pairs={{0,2},{2,0},{1,3},{3,1},{4,6},{6,4},{5,7},{7,5},{8,10},{10,8},{9,1... | collective-permute-start | bytes 786440 | tf_op jit(solution)/shard_map/ppermute | solution.py:23
  25.4 1.6 %collective-permute-start.2 = (bf16[32,2048]{1,0:T(8,128)(2,1)S(1)}, bf16[32,2048]{1,0:T(8,128)(2,1)S(1)}, u32[]{:S(2)}, u32[]{:S(2)}) collective-permute-start(bf16[32,2048]{1,0:T(8,128)(2,1)S(1)} %collective-permute-done.refs_1_), channel_id=1, source_target_pairs={{0,2},{2,0},{1,3},{3,1},{4,6},{6,4},{5,7},{7,5},{8,10},{10,8},{9,1... | collective-permute-start | bytes 393224 | tf_op jit(solution)/shard_map/ppermute | solution.py:23
  25.4 1.8 %collective-permute-start.6 = (bf16[32,2048]{1,0:T(8,128)(2,1)S(1)}, bf16[32,2048]{1,0:T(8,128)(2,1)S(1)}, u32[]{:S(2)}, u32[]{:S(2)}) collective-permute-start(bf16[32,2048]{1,0:T(8,128)(2,1)S(1)} %collective-permute-done.5.refs_3_), channel_id=1, source_target_pairs={{0,2},{2,0},{1,3},{3,1},{4,6},{6,4},{5,7},{7,5},{8,10},{10,8},{9,1... | collective-permute-start | bytes 393224 | tf_op jit(solution)/shard_map/ppermute | solution.py:23
  31.5 20.8 %collective-permute-start.12 = (f16[512,768]{1,0:T(8,128)(2,1)S(1)}, f16[512,768]{1,0:T(8,128)(2,1)S(1)}, u32[]{:S(2)}, u32[]{:S(2)}) collective-permute-start(f16[512,768]{1,0:T(8,128)(2,1)S(1)} %get-tuple-element.34), channel_id=1, source_target_pairs={{0,4},{12,8},{1,5},{13,9},{2,6},{14,10},{3,7},{15,11},{16,20},{28,... | collective-permute-start | bytes 2359304 | tf_op jit(solution)/shard_map/ppermute | solution.py:406
  34.5 34.8 %collective-permute-start.10 = (f16[512,768]{1,0:T(8,128)(2,1)}, f16[512,768]{1,0:T(8,128)(2,1)}, u32[]{:S(2)}, u32[]{:S(2)}) collective-permute-start(f16[512,768]{1,0:T(8,128)(2,1)} %get-tuple-element.35), channel_id=1, source_target_pairs={{0,8},{12,4},{1,9},{13,5},{2,10},{14,6},{3,11},{15,7},{16,24},{28,... | collective-permute-start | bytes 2359304 | tf_op jit(solution)/shard_map/ppermute | solution.py:409
  38.6 30.7 %collective-permute-start.9 = (f16[512,768]{1,0:T(8,128)(2,1)}, f16[512,768]{1,0:T(8,128)(2,1)}, u32[]{:S(2)}, u32[]{:S(2)}) collective-permute-start(f16[512,768]{1,0:T(8,128)(2,1)} %get-tuple-element.35), channel_id=1, source_target_pairs={{4,8},{8,4},{5,9},{9,5},{6,10},{10,6},{7,11},{11,7},{20,24},{24,20... | collective-permute-start | bytes 2359304 | tf_op jit(solution)/shard_map/ppermute | solution.py:408
  40.2 0.9 copy-start.7
  45.3 40.0 %collective-permute-start.11 = (f16[512,768]{1,0:T(8,128)(2,1)}, f16[512,768]{1,0:T(8,128)(2,1)}, u32[]{:S(2)}, u32[]{:S(2)}) collective-permute-start(f16[512,768]{1,0:T(8,128)(2,1)} %fusion.4), channel_id=1, source_target_pairs={{0,4},{4,0},{8,12},{12,8},{1,5},{5,1},{9,13},{13,9},{2,6},{6,2},{1... | collective-permute-start | bytes 2359304 | tf_op jit(solution)/shard_map/ppermute | solution.py:413
  53.4 37.4 %collective-permute-start.13 = (f16[512,768]{1,0:T(8,128)(2,1)}, f16[512,768]{1,0:T(8,128)(2,1)}, u32[]{:S(2)}, u32[]{:S(2)}) collective-permute-start(f16[512,768]{1,0:T(8,128)(2,1)} %add_convert_fusion), channel_id=1, source_target_pairs={{4,12},{8,0},{5,13},{9,1},{6,14},{10,2},{7,15},{11,3},{20,28},{24,... | collective-permute-start | bytes 2359304 | tf_op jit(solution)/shard_map/ppermute | solution.py:411
  86.7 5.5 %copy-start.9 = (bf16[1,2048]{1,0:T(2,128)(2,1)S(1)}, bf16[1,2048]{1,0:T(2,128)(2,1)}, u32[]{:S(2)}) copy-start(bf16[1,2048]{1,0:T(2,128)(2,1)} %refs_3_.3) | copy-start | bytes 12292
  86.7 5.5 %copy-start.10 = (s32[4]{0:T(128)S(1)}, s32[4]{0:T(128)}, u32[]{:S(2)}) copy-start(s32[4]{0:T(128)} %lengths.1) | copy-start | bytes 52
  86.7 20.2 %copy-start.11 = (s32[4]{0:T(128)S(1)}, s32[4]{0:T(128)}, u32[]{:S(2)}) copy-start(s32[4]{0:T(128)} %prompt_len.1) | copy-start | bytes 52
  86.7 20.1 %copy-start.12 = (f32[4]{0:T(128)S(1)}, f32[4]{0:T(128)}, u32[]{:S(2)}) copy-start(f32[4]{0:T(128)} %reward.1) | copy-start | bytes 52
